TPU v7x, 32 devices: a whole 2x2x4 slice. The times are simulated.
32 devices in a mesh: grp: 4 (over y, x), row: 8 (over z, core).
Axes of the slice: x: 2, y: 2, z: 4, core: 2. Of those that a mesh axis runs over, the one named last changes fastest.
Arguments:
- cov_prior: float32 [16384, 16384], P(('grp', 'row')), may hold values from -7 to 23, as said below
- courant_x_field: float32 [128, 128], replicated, may hold values from -0.35 to 0.35
- courant_y_field: float32 [128, 128], replicated, may hold values from -0.35 to 0.35
- obs_cells: int32 [2, 128], replicated, may hold values from 0 to 16383
- obs_var: float32 [2, 128], replicated, may hold values from 0.5 to 2
Outputs:
- analysis: float32 [16384, 16384], P('grp', 'row')
Inputs may be any that keep to these rules, and one draw needn't show every extreme that they name: `cov_prior`: symmetric and positive definite. `obs_cells`: a cell may be observed more than once in an update.
All inputs are finite; a program needn't handle non-finite values.
Results may differ from a plain program's by a relative error of at most 0.0002.
Values sent between devices are 32-bit elements; how exact they have to be, the bound alone decides.
No kernel may reach another device: no remote copies, remote signals or barrier semaphores. Data moves between devices by JAX's collectives and lax.ppermute only.
A program may use at most 448 MiB of HBM per device.

v0:
```python
import jax
import jax.numpy as jnp
from jax import lax
from jax.sharding import PartitionSpec as P

ZONAL_POINTS = 128
NY = 128
NCELL = 16384
UPDATES = 2


diffusion = 0.1


def extended_2(block, sides, width):
    for axis, dim in sides:
        count = lax.axis_size(axis)
        forward = [(i, i + 1) for i in range(count - 1)]
        backward = [(target, source) for source, target in forward]
        low = lax.ppermute(
            lax.slice_in_dim(block, block.shape[dim] - width, None, axis=dim), axis, forward
        )
        high = lax.ppermute(lax.slice_in_dim(block, 0, width, axis=dim), axis, backward)
        block = jnp.concatenate([low, block, high], axis=dim)
    return block


def tendency_first(padded, u_part, v_part):
    middle = padded[:, 2:-2]
    center = middle[:, :, 2:-2]
    along_x = (
        8.0 * (middle[:, :, 3:-1] - middle[:, :, 1:-3]) - (middle[:, :, 4:] - middle[:, :, :-4])
    ) / 12.0
    column = padded[:, :, 2:-2]
    along_y = (8.0 * (column[:, 3:-1] - column[:, 1:-3]) - (column[:, 4:] - column[:, :-4])) / 12.0
    laplace = (
        middle[:, :, 3:-1] + middle[:, :, 1:-3] + column[:, 3:-1] + column[:, 1:-3] - 4.0 * center
    )
    return diffusion * laplace - u_part * along_x - v_part * along_y


def heun_whole(fields, courant_x_field, courant_y_field):
    slope_first = tendency_first(
        jnp.pad(fields, ((0, 0), (2, 2), (2, 2))), courant_x_field, courant_y_field
    )
    latter_increment = tendency_first(
        jnp.pad(fields + slope_first, ((0, 0), (2, 2), (2, 2))), courant_x_field, courant_y_field
    )
    return fields + 0.5 * (slope_first + latter_increment)


def tendency_last(extended, u_part, v_part):
    padded = jnp.pad(extended, ((0, 0), (2, 2), (0, 0)))
    middle = padded[2:-2]
    center = middle[:, 2:-2]
    along_x = (8.0 * (middle[:, 3:-1] - middle[:, 1:-3]) - (middle[:, 4:] - middle[:, :-4])) / 12.0
    column = padded[:, 2:-2]
    along_y = (8.0 * (column[3:-1] - column[1:-3]) - (column[4:] - column[:-4])) / 12.0
    laplace = middle[:, 3:-1] + middle[:, 1:-3] + column[3:-1] + column[1:-3] - 4.0 * center
    return diffusion * laplace - u_part * along_x - v_part * along_y


def linear_source_term(local_block, courant_x_field, courant_y_field):
    meridional_count = local_block.shape[0]
    first_row = lax.axis_index("grp") * meridional_count
    u_padded = jnp.pad(courant_x_field, ((4, 4), (0, 0)))
    v_padded = jnp.pad(courant_y_field, ((4, 4), (0, 0)))
    u_inner = lax.dynamic_slice_in_dim(u_padded, first_row + 4, meridional_count, 0)[:, :, None]
    v_inner = lax.dynamic_slice_in_dim(v_padded, first_row + 4, meridional_count, 0)[:, :, None]

    def section_slope(current):
        extended = extended_2(current, (("grp", 0),), 2)
        return tendency_last(extended, u_inner, v_inner)

    slope_first = section_slope(local_block)
    latter_increment = section_slope(local_block + slope_first)
    local_block = local_block + 0.5 * (slope_first + latter_increment)
    return local_block


def local(cov_prior, courant_x_field, courant_y_field, obs_cells, obs_var):
    row_count = cov_prior.shape[0]
    fields = cov_prior.reshape(row_count, NY, ZONAL_POINTS)
    fields = heun_whole(fields, courant_x_field, courant_y_field)
    advanced = fields.reshape(row_count, NCELL)
    members = lax.axis_size("row")
    zonal_extent = NCELL // members
    meridional_count = row_count * members // ZONAL_POINTS
    pieces = max(1, zonal_extent // 128)
    piece_width = zonal_extent // pieces
    received = lax.all_to_all(
        advanced.reshape(row_count, members, pieces, piece_width),
        "row",
        split_axis=1,
        concat_axis=0,
        tiled=True,
    )
    predicted_tracer = linear_source_term(
        received.reshape(meridional_count, ZONAL_POINTS, received.shape[2] * piece_width),
        courant_x_field,
        courant_y_field,
    )
    posterior_mean = predicted_tracer.reshape(meridional_count * ZONAL_POINTS, zonal_extent)
    local_rows = posterior_mean.shape[0]
    first_cell = lax.axis_index("grp") * local_rows
    first_column = lax.axis_index("row") * zonal_extent
    for update_number in range(UPDATES):
        picked = obs_cells[update_number]
        row_offset = picked - first_cell
        row_owned = (row_offset >= 0) & (row_offset < local_rows)
        rows_part = jnp.where(
            row_owned[:, None], posterior_mean[jnp.clip(row_offset, 0, local_rows - 1)], 0.0
        )
        observed_rows = lax.psum(rows_part, "grp")
        column_offset = picked - first_column
        column_owned = (column_offset >= 0) & (column_offset < zonal_extent)
        safe_column = jnp.clip(column_offset, 0, zonal_extent - 1)
        cols_part = jnp.where(column_owned[None, :], posterior_mean[:, safe_column], 0.0)
        inner_part = jnp.where(column_owned[None, :], observed_rows[:, safe_column], 0.0)
        observed_cols, inner_block = lax.psum((cols_part, inner_part), "row")
        system = 0.5 * (inner_block + inner_block.T) + jnp.diag(obs_var[update_number])
        factor = jnp.linalg.cholesky(system)
        halfway = lax.linalg.triangular_solve(factor, observed_rows, left_side=True, lower=True)
        weights = lax.linalg.triangular_solve(
            factor, halfway, left_side=True, lower=True, transpose_a=True
        )
        posterior_mean = posterior_mean - jnp.dot(
            observed_cols, weights, precision=lax.Precision.HIGHEST
        )
    return posterior_mean


def solution(mesh):
    placed = (P(("grp", "row"), None), P(), P(), P(), P())
    return jax.shard_map(
        local, mesh=mesh, in_specs=placed, out_specs=P("grp", "row"), check_vma=False
    )
```

profile of v0, /device:TPU:0, one launch (start us, length us, event | category | flops | bytes accessed | tf_op | source)
XLA Modules:
  0.0 1995.2 jit_solution(3183743674395259142)
XLA Ops:
  6.5 27.6 %copy.29 = f32[64,8,128,128]{3,2,1,0:T(8,128)} copy(f32[64,8,128,128]{3,1,2,0:T(8,128)} %bitcast.99) | data formatting | bytes 67108864
  34.2 143.1 %bitcast_add_fusion.4 = (f32[512,128,128]{2,1,0:T(8,128)}, f32[512,128,128]{2,1,0:T(8,128)}) fusion(f32[64,8,128,128]{3,2,1,0:T(8,128)} %copy.29, f32[128,128]{1,0:T(8,128)S(1)} %get-tuple-element.32, f32[128,128]{1,0:T(8,128)S(1)} %get-tuple-element.33, f32[512,128,128]{2,1,0:T(8,128)} %bitcast.93), kind=kLoop, calls=%fused_computation.139 | loop fusion | flops 159383552 | bytes 134348800 | tf_op jit(solution)/shard_map/add | solution.py:47
  177.2 147.2 %fusion.18 = f32[512,128,128]{2,1,0:T(8,128)} fusion(f32[512,128,128]{2,1,0:T(8,128)} %get-tuple-element.15, f32[512,128,128]{2,1,0:T(8,128)} %get-tuple-element.14, f32[128,128]{1,0:T(8,128)S(1)} %get-tuple-element.32, f32[128,128]{1,0:T(8,128)S(1)} %get-tuple-element.33, f32[64,8,128,128]{3,2,1,0:T(8,128)} %copy.29), kind=kLoop, calls=%fused_computation.50 | loop fusion | flops 176160768 | bytes 134348800 | tf_op jit(solution)/shard_map/add | solution.py:49
  324.5 12.1 copy.6
  336.6 729.4 %all_to_all.15 = f32[512,8,16,128]{3,2,0,1:T(8,128)} all-to-all(f32[512,8,16,128]{3,2,0,1:T(8,128)S(1)} %copy.6), channel_id=1, replica_groups=mesh['grp'=4,'row'=8] {'row'}, dimensions={1} | all-to-all | bytes 67108864 | tf_op jit(solution)/shard_map/all_to_all | solution.py:91
  1066.0 35.4 %reshape.170 = f32[32,128,2048]{2,1,0:T(8,128)} reshape(f32[8,512,1,16,128]{4,3,1,0,2:T(8,128)} %bitcast.98) | data formatting | bytes 67108864 | tf_op jit(solution)/shard_map/reshape | solution.py:99
  1101.5 4.7 fusion.63
  1106.1 3.5 collective-permute-start
  1109.7 1.5 collective-permute-start.1
  1111.2 43.2 %collective-permute-done = f32[2,128,2048]{2,1,0:T(8,128)S(1)} collective-permute-done((f32[2,128,2048]{2,1,0:T(8,128)}, f32[2,128,2048]{2,1,0:T(8,128)S(1)}, u32[]{:S(2)}, u32[]{:S(2)}) %collective-permute-start) | collective-permute-done | bytes 2097184 | tf_op jit(solution)/shard_map/ppermute | solution.py:20
  1154.4 1.4 constant_dynamic-update-slice_fusion.3
  1155.8 33.3 %constant_dynamic-update-slice_fusion.1 = (f32[34,128,2048]{2,1,0:T(8,128)}, f32[34,128,2048]{2,1,0:T(8,128)}) fusion(f32[32,128,2048]{2,1,0:T(8,128)} %reshape.170, f32[34,128,2048]{2,1,0:T(8,128)} %constant_dynamic-update-slice_fusion.3), kind=kLoop, calls=%fused_computation.116 | loop fusion | bytes 100663296
  1189.1 12.2 collective-permute-done.1
  1201.2 25.3 %select_maximum_fusion.2 = f32[36,132,2048]{2,1,0:T(8,128)} fusion(f32[2,128,2048]{2,1,0:T(8,128)} %collective-permute-done.1, f32[32,128,2048]{2,1,0:T(8,128)} %reshape.170, f32[2,128,2048]{2,1,0:T(8,128)S(1)} %collective-permute-done), kind=kLoop, calls=%fused_computation.26 | loop fusion | flops 77856768 | bytes 76677120 | tf_op jit(solution)/shard_map/concatenate | solution.py:24
  1226.6 3.2 constant_dynamic-update-slice_fusion
  1229.8 119.7 %fusion.59 = (f32[32,128,2048]{2,1,0:T(8,128)}, f32[32,128,2048]{2,1,0:T(8,128)}) fusion(f32[32,128,2048]{2,1,0:T(8,128)} %reshape.170, f32[32,128]{1,0:T(8,128)S(1)} %get-tuple-element.35, f32[34,128,2048]{2,1,0:T(8,128)} %get-tuple-element.21, f32[34,128,2048]{2,1,0:T(8,128)} %constant_dynamic-update-slice_fusion, f32[32,128]{1,0:T(8,128)S(1)} %get-tuple-element.34, ...), kind=kLoop, calls=%fused_computation.140 | loop fusion | flops 159383552 | bytes 369131520 | tf_op jit(solution)/shard_map/add | solution.py:76
  1349.5 4.7 fusion.62
  1354.1 3.5 collective-permute-start.2
  1357.7 1.3 collective-permute-start.3
  1359.0 0.5 fusion.58
  1359.5 0.6 and_bitcast_fusion
  1360.1 41.4 %collective-permute-done.2 = f32[2,128,2048]{2,1,0:T(8,128)S(1)} collective-permute-done((f32[2,128,2048]{2,1,0:T(8,128)}, f32[2,128,2048]{2,1,0:T(8,128)S(1)}, u32[]{:S(2)}, u32[]{:S(2)}) %collective-permute-start.2) | collective-permute-done | bytes 2097184 | tf_op jit(solution)/shard_map/ppermute | solution.py:20
  1401.5 45.7 %collective-permute-done.3 = f32[2,128,2048]{2,1,0:T(8,128)} collective-permute-done((f32[2,128,2048]{2,1,0:T(8,128)}, f32[2,128,2048]{2,1,0:T(8,128)}, u32[]{:S(2)}, u32[]{:S(2)}) %collective-permute-start.3) | collective-permute-done | bytes 2097184 | tf_op jit(solution)/shard_map/ppermute | solution.py:23
  1447.2 25.3 %select_maximum_fusion = f32[36,132,2048]{2,1,0:T(8,128)} fusion(f32[2,128,2048]{2,1,0:T(8,128)} %collective-permute-done.3, f32[32,128,2048]{2,1,0:T(8,128)} %get-tuple-element.12, f32[2,128,2048]{2,1,0:T(8,128)S(1)} %collective-permute-done.2), kind=kLoop, calls=%fused_computation.24 | loop fusion | flops 77856768 | bytes 76677120 | tf_op jit(solution)/shard_map/concatenate | solution.py:24
  1472.5 123.9 %fusion.28 = f32[32,128,2048]{2,1,0:T(8,128)} fusion(f32[32,128,2048]{2,1,0:T(8,128)} %reshape.170, f32[32,128,2048]{2,1,0:T(8,128)} %get-tuple-element.13, f32[32,128,2048]{2,1,0:T(8,128)} %get-tuple-element.12, f32[2,128,2048]{2,1,0:T(8,128)S(1)} %collective-permute-done.2, f32[2,128,2048]{2,1,0:T(8,128)} %collective-permute-done.3, ...), kind=kLoop, calls=%fused_computation.61 | loop fusion | flops 209715200 | bytes 272662528 | tf_op jit(solution)/shard_map/add | solution.py:77
  1596.4 12.0 gather_fusion.1
  1608.4 1.1 broadcast_select_fusion.1
  1609.6 0.3 all-reduce.19.cloned.1.call-start
  1609.9 31.2 %copy.7 = f32[4096,2048]{0,1:T(8,128)} copy(f32[4096,2048]{1,0:T(8,128)} %bitcast.95) | data formatting | bytes 67108864 | tf_op jit(solution)/shard_map/reshape | solution.py:103
  1641.1 12.9 gather_fusion
  1654.0 1.6 select_bitcast_fusion.1
  1655.5 4.9 all-reduce.13.cloned.1.call-done
  1660.4 1.5 copy.8
  1662.0 0.6 gather_fusion.2
  1662.6 0.7 select_bitcast_fusion.3
  1663.5 65.6 %all-reduce.19.cloned.1.call-done = (f32[4096,128]{0,1:T(8,128)}, f32[128,128]{0,1:T(8,128)}) async-done(((f32[4096,128]{0,1:T(8,128)}, f32[128,128]{0,1:T(8,128)}), (f32[4096,128]{0,1:T(8,128)}, f32[128,128]{0,1:T(8,128)})) %all-reduce.19.cloned.1.call-update) | async-done | bytes 2162704 | tf_op jit(solution)/shard_map/psum | solution.py:120
  1729.1 0.9 copy.10
  1730.0 0.9 fusion.52
  1731.2 11.7 cholesky.44
  1742.9 0.7 compare_reduce_fusion.1
  1743.6 0.6 fusion.38
  1744.2 9.8 custom-call.11
  1754.1 2.3 fusion.46
  1756.3 1.0 fusion.48
  1757.4 34.4 %convolution_subtract_fusion.1 = f32[4096,2048]{1,0:T(8,128)} fusion(f32[4096,2048]{1,0:T(8,128)} %bitcast.96, f32[4096,128]{0,1:T(8,128)} %get-tuple-element.10, f32[128,2048]{1,0:T(8,128)S(1)} %fusion.48), kind=kOutput, calls=%fused_computation.76 | convolution fusion | flops 12893290496 | bytes 70254592 | tf_op jit(solution)/shard_map/dot_general | solution.py:127
  1791.8 12.0 gather_fusion.4
  1803.8 1.1 broadcast_select_fusion
  1805.1 31.5 %copy.14 = f32[4096,2048]{0,1:T(8,128)} copy(f32[4096,2048]{1,0:T(8,128)} %convolution_subtract_fusion.1) | data formatting | bytes 67108864 | tf_op jit(solution)/shard_map/sub | solution.py:127
  1836.6 13.0 gather_fusion.3
  1849.5 1.6 select_bitcast_fusion
  1851.1 6.2 all-reduce.15.cloned.1.call-done
  1857.3 1.5 copy.15
  1858.9 0.6 gather_fusion.5
  1859.6 0.6 select_bitcast_fusion.2
  1860.4 65.6 %all-reduce.17.cloned.1.call-done = (f32[4096,128]{0,1:T(8,128)}, f32[128,128]{1,0:T(8,128)}) async-done(((f32[4096,128]{0,1:T(8,128)}, f32[128,128]{1,0:T(8,128)}), (f32[4096,128]{0,1:T(8,128)}, f32[128,128]{1,0:T(8,128)})) %all-reduce.17.cloned.1.call-update) | async-done | bytes 2162704 | tf_op jit(solution)/shard_map/psum | solution.py:120
  1926.0 0.9 copy.17
  1926.9 0.9 fusion.45
  1928.0 11.7 cholesky.55
  1939.8 0.7 compare_reduce_fusion
  1940.4 0.6 fusion.39
  1941.1 9.8 custom-call.13
  1950.9 2.3 fusion.40
  1953.2 1.0 fusion.42
  1954.2 34.2 %convolution_subtract_fusion = f32[4096,2048]{1,0:T(8,128)} fusion(f32[4096,2048]{1,0:T(8,128)} %convolution_subtract_fusion.1, f32[4096,128]{0,1:T(8,128)} %get-tuple-element.6, f32[128,2048]{1,0:T(8,128)S(1)} %fusion.42), kind=kOutput, calls=%fused_computation.75 | convolution fusion | flops 12893290496 | bytes 70254592 | tf_op jit(solution)/shard_map/dot_general | solution.py:127
  (40 shorter events, 0.9 us)
Async XLA Ops:
  6.5 1653.9 %all-reduce.13.cloned.1.call-start = ((), (), s32[]{:S(2)}) async-start(), calls=%async_computation.1 | async-start | bytes 2097152 | tf_op jit(solution)/shard_map/psum | solution.py:114
  6.5 27.6 %copy-start = (f32[128,128]{1,0:T(8,128)S(1)}, f32[128,128]{1,0:T(8,128)}, u32[]{:S(2)}) copy-start(f32[128,128]{1,0:T(8,128)} %param.12) | copy-start | bytes 196612
  6.5 27.6 %copy-start.1 = (f32[128,128]{1,0:T(8,128)S(1)}, f32[128,128]{1,0:T(8,128)}, u32[]{:S(2)}) copy-start(f32[128,128]{1,0:T(8,128)} %param.11) | copy-start | bytes 196612
  1106.1 48.2 %collective-permute-start = (f32[2,128,2048]{2,1,0:T(8,128)}, f32[2,128,2048]{2,1,0:T(8,128)S(1)}, u32[]{:S(2)}, u32[]{:S(2)}) collective-permute-start(f32[2,128,2048]{2,1,0:T(8,128)} %get-tuple-element.19), channel_id=1, source_target_pairs={{0,8},{8,16},{16,24},{1,9},{9,17},{17,25},{2,10},{10,18},{18,26},{... | collective-permute-start | bytes 6291464 | tf_op jit(solution)/shard_map/ppermute | solution.py:20
  1109.7 91.5 %collective-permute-start.1 = (f32[2,128,2048]{2,1,0:T(8,128)}, f32[2,128,2048]{2,1,0:T(8,128)}, u32[]{:S(2)}, u32[]{:S(2)}) collective-permute-start(f32[2,128,2048]{2,1,0:T(8,128)} %get-tuple-element.18), channel_id=1, source_target_pairs={{8,0},{16,8},{24,16},{9,1},{17,9},{25,17},{10,2},{18,10},{26,18},{... | collective-permute-start | bytes 6291464 | tf_op jit(solution)/shard_map/ppermute | solution.py:23
  1229.8 129.2 %copy-start.3 = (s32[2,128]{1,0:T(2,128)S(1)}, s32[2,128]{1,0:T(2,128)}, u32[]{:S(2)}) copy-start(s32[2,128]{1,0:T(2,128)} %param.13) | copy-start | bytes 3076
  1354.1 47.4 %collective-permute-start.2 = (f32[2,128,2048]{2,1,0:T(8,128)}, f32[2,128,2048]{2,1,0:T(8,128)S(1)}, u32[]{:S(2)}, u32[]{:S(2)}) collective-permute-start(f32[2,128,2048]{2,1,0:T(8,128)} %get-tuple-element.17), channel_id=1, source_target_pairs={{0,8},{8,16},{16,24},{1,9},{9,17},{17,25},{2,10},{10,18},{18,26},{... | collective-permute-start | bytes 6291464 | tf_op jit(solution)/shard_map/ppermute | solution.py:20
  1357.7 89.5 %collective-permute-start.3 = (f32[2,128,2048]{2,1,0:T(8,128)}, f32[2,128,2048]{2,1,0:T(8,128)}, u32[]{:S(2)}, u32[]{:S(2)}) collective-permute-start(f32[2,128,2048]{2,1,0:T(8,128)} %get-tuple-element.16), channel_id=1, source_target_pairs={{8,0},{16,8},{24,16},{9,1},{17,9},{25,17},{10,2},{18,10},{26,18},{... | collective-permute-start | bytes 6291464 | tf_op jit(solution)/shard_map/ppermute | solution.py:23
  1609.6 119.5 %all-reduce.19.cloned.1.call-start = ((), (), s32[]{:S(2)}) async-start(), calls=%async_computation.4 | async-start | bytes 4325376 | tf_op jit(solution)/shard_map/psum | solution.py:120
  1609.9 53.6 %copy-start.6 = (f32[2,128]{1,0:T(2,128)S(1)}, f32[2,128]{1,0:T(2,128)}, u32[]{:S(2)}) copy-start(f32[2,128]{1,0:T(2,128)} %param.14) | copy-start | bytes 3076
  1663.4 194.0 %all-reduce.15.cloned.1.call-start = ((), (), s32[]{:S(2)}) async-start(), calls=%async_computation.2 | async-start | bytes 2097152 | tf_op jit(solution)/shard_map/psum | solution.py:114
  1757.3 46.5 %copy-start.4 = (pred[128]{0:T(512)(128)(4,1)S(1)}, pred[128]{0:T(512)(128)(4,1)}, u32[]{:S(2)}) copy-start(pred[128]{0:T(512)(128)(4,1)} %get-tuple-element.24) | copy-start | bytes 388
  1757.4 47.7 %copy-start.5 = (s32[128]{0:T(128)S(1)}, s32[128]{0:T(128)}, u32[]{:S(2)}) copy-start(s32[128]{0:T(128)} %get-tuple-element.29) | copy-start | bytes 1540
  1805.0 121.0 %all-reduce.17.cloned.1.call-start = ((), (), s32[]{:S(2)}) async-start(), calls=%async_computation.3 | async-start | bytes 4325376 | tf_op jit(solution)/shard_map/psum | solution.py:120
  1805.1 44.5 %copy-start.2 = (pred[128]{0:T(512)(128)(4,1)S(1)}, pred[128]{0:T(512)(128)(4,1)}, u32[]{:S(2)}) copy-start(pred[128]{0:T(512)(128)(4,1)} %get-tuple-element.26) | copy-start | bytes 388
Sparse Core Ops, SparseCore 0:
  1609.7 50.6 all-reduce.12
  1663.5 65.5 all-reduce.18
  1805.1 52.1 all-reduce.14
  1860.4 65.5 all-reduce.16
where the time goes:
time: 2000 us
  blocking collectives  729 us (36%)
  other arithmetic  640 us (32%)
  waiting for transfers between devices  285 us (14%)
  local copies, waits for them, and re-layouts  242 us (12%)
  matrix products  75.2 us (4%)
    all_to_all x1, blocking collectives, local(): lax.all_to_all(advanced.reshape(row_count, members, pieces, piece_width),...  729 us
    add x1, other arithmetic, heun_whole(): return fields + 0.5 * (slope_first + latter_increment)  147 us
    add x1, other arithmetic, heun_whole(): fields + slope_first  143 us
    psum x2, waiting for transfers between devices, local(): observed_cols, inner_block = lax.psum((cols_part, inner_part), 'row')  131 us
    add x1, other arithmetic, linear_source_term(): local_block = local_block + 0.5 * (slope_first + latter_increment)  124 us
    add x1, other arithmetic, linear_source_term(): latter_increment = section_slope(local_block + slope_first)  120 us
    ppermute x2, waiting for transfers between devices, extended_2(): lax.ppermute(lax.slice_in_dim(block, block.shape[dim] - width, None, axis...  84.5 us
    dot_general x2, matrix products, local(): jnp.dot(observed_cols, weights, precision=lax.Precision.HIGHEST)  68.7 us
  transfers between devices with their start and end apart: 8, of which 8 were waited for; matrix products, arithmetic and copies ran while one was open for 6% of the time, Pallas kernels for 0%

commit v1 on v0

v1 whole, which is shorter than its diff:
```python
import functools

import jax
import jax.numpy as jnp
from jax import lax
from jax.experimental import pallas as pl
from jax.experimental.pallas import tpu as pltpu
from jax.sharding import PartitionSpec as P


diffusion = 0.1
LANES = 128
SUB = 8
REACH = 2
EXACT = lax.Precision.HIGHEST


def stencil_coefficients(u, v):
    nx = u.shape[1]
    x = lax.broadcasted_iota(jnp.int32, u.shape, 1)
    u12, v12 = u / 12.0, v / 12.0
    return [
        diffusion - 8.0 * v12,
        diffusion + 8.0 * v12,
        v12,
        jnp.where(x < nx - 1, diffusion - 8.0 * u12, 0.0),
        jnp.where(x >= 1, diffusion + 8.0 * u12, 0.0),
        jnp.where(x < nx - 2, u12, 0.0),
        jnp.where(x >= 2, -u12, 0.0),
    ]


KEEP = 1.0 - 4.0 * diffusion


def neighbours(c, ym2, ym1, yp1, yp2, xp1, xm1, xp2, xm2):
    along_y = c[0] * yp1 + c[1] * ym1 + c[2] * (yp2 - ym2)
    return along_y + ((c[3] * xp1 + c[4] * xm1) + (c[5] * xp2 + c[6] * xm2))


def row_coefficients(coefs):
    moved = [jnp.roll(c, 2, axis=1) if i in (3, 5) else c for i, c in enumerate(coefs)]
    return jnp.stack([jnp.repeat(c, SUB, axis=0) for c in moved])


def row_step_kernel(me_ref, coef_ref, p_ref, o_ref, *, nx, per_dest, lead, groups):
    me = me_ref[0]
    rows = p_ref.shape[0]
    members = o_ref.shape[0]
    depth = o_ref.shape[2] // nx
    deep = min(4, depth)
    zero = jnp.zeros((SUB, nx), jnp.float32)

    def block(step, _):
        r0 = pl.multiple_of(step * (SUB * groups), SUB * groups)

        def cols(y):
            start = y * nx
            return pl.ds(start if isinstance(start, int) else pl.multiple_of(start, nx), nx)

        def coefs(y):
            start = y * SUB
            start = start if isinstance(start, int) else pl.multiple_of(start, SUB)
            return [coef_ref[i, pl.ds(start, SUB), :] for i in range(7)]

        def around(c, m2, m1, mid, p1, p2):
            before = pltpu.roll(mid, 1, 1)
            along_y = c[0] * p1 + c[1] * m1 + c[2] * (p2 - m2)
            ahead = pltpu.roll(c[5] * mid + c[3] * before, nx - 2, 1)
            return along_y + (ahead + (c[4] * before + c[6] * pltpu.roll(before, 1, 1)))

        def part(dest, inner, low, high):
            y0 = dest * per_dest + lead + inner
            q = {}
            for k in range(-4, deep + 4):
                outside = (low and k < 0) or (high and k >= deep)
                for g in range(groups):
                    spot = pl.ds(pl.multiple_of(r0 + SUB * g, SUB), SUB)
                    q[k, g] = zero if outside else p_ref[spot, cols(y0 + k)]
            s = {}
            for k in range(-2, deep + 2):
                outside = (low and k < 0) or (high and k >= deep)
                c = None if outside else coefs(y0 + k)
                for g in range(groups):
                    s[k, g] = zero if outside else KEEP * q[k, g] + around(
                        c, *[q[k + j, g] for j in range(-2, 3)]
                    )
            slot = jnp.bitwise_xor(jnp.int32(dest), me)
            for k in range(deep):
                c = coefs(y0 + k)
                for g in range(groups):
                    value = KEEP * s[k, g] + around(c, *[s[k + j, g] for j in range(-2, 3)])
                    spot = pl.ds(pl.multiple_of(r0 + SUB * g, SUB), SUB)
                    o_ref[slot, spot, cols(inner + k)] = 0.5 * (q[k, g] + value)

        for inner in range(0, depth, deep):
            low = lead + inner == 0
            high = lead + inner + deep == per_dest
            if low:
                part(0, inner, True, high and members == 1)

            def one(dest, _):
                part(dest, inner, False, False)
                return 0

            lax.fori_loop(int(low), members - int(high), one, 0)
            if high and not (low and members == 1):
                part(members - 1, inner, False, True)
        return 0

    lax.fori_loop(0, rows // (SUB * groups), block, 0)


def row_step(cov, table, me, nx, members, lead, depth):
    rows, cells = cov.shape
    per_dest = cells // members // nx
    tall = min(64, rows)
    groups = 2 if tall % (2 * SUB) == 0 else 1
    return pl.pallas_call(
        functools.partial(row_step_kernel, nx=nx, per_dest=per_dest, lead=lead, groups=groups),
        out_shape=jax.ShapeDtypeStruct((members, rows, depth * nx), jnp.float32),
        grid_spec=pltpu.PrefetchScalarGridSpec(
            num_scalar_prefetch=1,
            grid=(rows // tall,),
            in_specs=[
                pl.BlockSpec(table.shape, lambda i, m: (0, 0, 0), pipeline_mode=pl.Buffered(1)),
                pl.BlockSpec((tall, cells), lambda i, m: (i, 0)),
            ],
            out_specs=pl.BlockSpec((members, tall, depth * nx), lambda i, m: (0, i, 0)),
        ),
        compiler_params=pltpu.CompilerParams(vmem_limit_bytes=56 << 20),
        cost_estimate=work(members * rows * depth * nx, 60),
        name="row_step",
    )(me, table, cov)


def work(elements, flops):
    return pl.CostEstimate(
        flops=flops * elements, transcendentals=0, bytes_accessed=32 * elements
    )


def pick_columns(blocks, leads, cells, me, zonal):
    total = 0.0
    for array, lead in zip(blocks, leads):
        members, _, width = array.shape
        for s in range(members):
            first = jnp.bitwise_xor(me, s) * zonal + lead
            ids = first + lax.broadcasted_iota(jnp.int32, (width, cells.shape[0]), 0)
            chosen = (ids == cells[None, :]).astype(jnp.float32)
            total = total + jnp.dot(array[s], chosen, precision=lax.Precision.HIGH)
    return total


FRONT = SUB


def column_step_kernel(me_ref, *refs, sources, halo, nx, grid_rows, update):
    coef_ref, refs = refs[0], refs[1:]
    own = refs[: len(sources)]
    refs = refs[len(sources) :]
    if update:
        c_ref, w_ref = refs[:2]
        refs = refs[2:]
        if len(refs) == 4:
            refs = refs[1:]
    o_ref, q_ref, s_ref = refs
    me = me_ref[0]
    tiles = o_ref.shape[1] // LANES
    border = jnp.zeros((FRONT, LANES), jnp.float32)
    span = (grid_rows + 4 * REACH) * nx
    for t in range(tiles):
        for ref in (q_ref, s_ref):
            ref[t, 0:FRONT, :] = border
            ref[t, FRONT + span : FRONT + span + SUB, :] = border

    for ref, (kind, at) in zip(own, sources):
        tall = ref.shape[0]
        if kind == "partner":
            start = FRONT + halo + jnp.bitwise_xor(me, at) * tall
        else:
            start = FRONT + at
        start = pl.multiple_of(start, SUB)
        piece = min(64, tall)

        def copy(i, _):
            r = pl.multiple_of(i * piece, piece)
            for t in range(tiles):
                q_ref[t, pl.ds(start + r, piece), :] = ref[
                    pl.ds(r, piece), t * LANES : (t + 1) * LANES
                ]
            return 0

        lax.fori_loop(0, tall // piece, copy, 0)

    def sweep(src, low, count, emit):
        def strip(xg, _):
            base = FRONT + xg * SUB

            def at(y, shift=0):
                rows = y * nx + base
                if shift == 0:
                    rows = pl.multiple_of(rows, SUB)
                else:
                    rows = rows + shift
                return [src[t, pl.ds(rows, SUB), :] for t in range(tiles)]

            def step(y, win):
                far = at(y + 2)
                xp1, xm1, xp2, xm2 = at(y, 1), at(y, -1), at(y, 2), at(y, -2)
                spot = pl.multiple_of(y * nx + xg * SUB, SUB)
                c = [coef_ref[i, pl.ds(spot, SUB), :] for i in range(7)]
                for t in range(tiles):
                    value = neighbours(
                        c, win[0][t], win[1][t], win[3][t], far[t],
                        xp1[t], xm1[t], xp2[t], xm2[t],
                    )
                    emit(t, spot, KEEP * win[2][t] + value)
                return win[1:] + [far]

            def several(i, win):
                for k in range(4):
                    win = step(low + 4 * i + k, win)
                return win

            win = [at(low - 2), at(low - 1), at(low), at(low + 1)]
            lax.fori_loop(0, count // 4, several, win)
            return 0

        lax.fori_loop(0, nx // SUB, strip, 0)

    def emit_first(t, spot, value):
        s_ref[t, pl.ds(spot + FRONT, SUB), :] = value

    def emit_last(t, spot, value):
        row = pl.multiple_of(spot - 2 * REACH * nx, SUB)
        mid = q_ref[t, pl.ds(pl.multiple_of(spot + FRONT, SUB), SUB), :]
        o_ref[pl.ds(row, SUB), t * LANES : (t + 1) * LANES] = 0.5 * (mid + value)

    sweep(q_ref, REACH, grid_rows + 2 * REACH, emit_first)
    sweep(s_ref, 2 * REACH, grid_rows, emit_last)

    if update:

        def subtract(y, _):
            rows = pl.ds(pl.multiple_of(y * nx, nx), nx)
            o_ref[rows, :] = o_ref[rows, :] - jnp.dot(
                c_ref[rows, :], w_ref[...], preferred_element_type=jnp.float32
            )
            return 0

        lax.fori_loop(0, grid_rows, subtract, 0)


def column_step(me, coefs, parts, sources, halo, nx, grid_rows, tile, out_shape, offset,
                own=0, gains=None, into=None):
    width = parts[0].shape[-1]
    steps = width // tile
    lead = offset // tile
    once = pl.Buffered(1)
    specs = [pl.BlockSpec(coefs.shape, lambda j, m: (0, 0, 0), pipeline_mode=once)]
    for part in parts:
        if part.ndim == 3:
            specs.append(
                pl.BlockSpec((None, part.shape[1], tile), lambda j, m: (0, 0, own // tile + j))
            )
        else:
            specs.append(pl.BlockSpec((part.shape[0], tile), lambda j, m: (0, j)))
    args = [coefs, *parts]
    aliases = {}
    if gains is not None:
        c, w = gains
        specs.append(pl.BlockSpec(c.shape, lambda j, m: (0, 0), pipeline_mode=once))
        specs.append(pl.BlockSpec((w.shape[0], tile), lambda j, m: (0, lead + j)))
        args += [c, w]
    if into is not None:
        specs.append(pl.BlockSpec(memory_space=pl.ANY))
        args.append(into)
        aliases = {len(args): 0}
    span = (grid_rows + 4 * REACH) * nx + FRONT + SUB
    scratch = pltpu.VMEM((tile // LANES, span, LANES), jnp.float32)
    return pl.pallas_call(
        functools.partial(
            column_step_kernel, sources=sources, halo=halo, nx=nx, grid_rows=grid_rows,
            update=gains is not None,
        ),
        out_shape=jax.ShapeDtypeStruct(out_shape, jnp.float32),
        grid_spec=pltpu.PrefetchScalarGridSpec(
            num_scalar_prefetch=1,
            grid=(steps,),
            in_specs=specs,
            out_specs=pl.BlockSpec((out_shape[0], tile), lambda j, m: (0, lead + j)),
            scratch_shapes=[scratch, scratch],
        ),
        input_output_aliases=aliases,
        compiler_params=pltpu.CompilerParams(vmem_limit_bytes=60 << 20),
        cost_estimate=work(out_shape[0] * width, 100),
        name="column_step",
    )(me, *args)


def split(value):
    high = lax.reduce_precision(value, 8, 7)
    return high.astype(jnp.bfloat16), (value - high).astype(jnp.bfloat16)


def solve(inner, variance, right):
    system = 0.5 * (inner + inner.T) + jnp.diag(variance)
    factor = jnp.linalg.cholesky(system)
    halfway = lax.linalg.triangular_solve(factor, right, left_side=True, lower=True)
    return lax.linalg.triangular_solve(factor, halfway, left_side=True, lower=True, transpose_a=True)


def gains_of(columns, rows, inner, obs_var):
    updates, count = obs_var.shape
    weights = []
    for u in range(updates):
        here = slice(u * count, (u + 1) * count)
        after = slice((u + 1) * count, updates * count)
        later = inner[here, after]
        both = jnp.concatenate([rows[here], later], axis=1)
        both = solve(inner[here, here], obs_var[u], both)
        w, w_later = both[:, : rows.shape[1]], both[:, rows.shape[1] :]
        weights.append(w)
        if u + 1 < updates:
            left = inner[after, here]
            rows = rows.at[after].add(-jnp.dot(left, w, precision=EXACT))
            columns = columns.at[:, after].add(-jnp.dot(columns[:, here], w_later, precision=EXACT))
            inner = inner.at[after, after].add(-jnp.dot(left, w_later, precision=EXACT))
    c_high, c_low = split(columns)
    w_high, w_low = split(jnp.concatenate(weights, axis=0))
    return (
        jnp.concatenate([c_high, c_high, c_low], axis=1),
        jnp.concatenate([w_high, w_low, w_high], axis=0),
    )


def local(cov_prior, courant_x_field, courant_y_field, obs_cells, obs_var):
    rows, cells = cov_prior.shape
    _, nx = courant_x_field.shape
    members, clusters = lax.axis_size("row"), lax.axis_size("grp")
    zonal, local_rows = cells // members, rows * members
    grid_rows = local_rows // nx
    halo = 2 * REACH * nx
    me, group = lax.axis_index("row"), lax.axis_index("grp")
    me_arg = me.reshape(1).astype(jnp.int32)
    coefs = stencil_coefficients(courant_x_field, courant_y_field)

    per_dest = zonal // nx
    table = row_coefficients(coefs)
    shares, slots = plan(per_dest)
    leads = [sum(shares[:i]) for i in range(len(shares))]
    blocks = []
    for lead, depth in zip(leads, shares):
        blocks.append(row_step(cov_prior, table, me_arg, nx, members, lead, depth))

    column_coefs = jnp.stack(
        [
            jnp.broadcast_to(
                lax.dynamic_slice_in_dim(
                    jnp.pad(c, ((2 * REACH, 2 * REACH), (0, 0))),
                    group * grid_rows, grid_rows + 4 * REACH, 0,
                ).reshape(-1)[:, None],
                (local_rows + 2 * halo, LANES),
            )
            for c in coefs
        ]
    )

    forward = [(i, i + 1) for i in range(clusters - 1)]
    backward = [(i + 1, i) for i in range(clusters - 1)]
    received = []
    for index, start, take in slots:
        cut = slice(start * nx, (start + take) * nx)
        got = [blocks[index][0, :, cut]]
        for s in range(1, members):
            pairs = [(i, i ^ s) for i in range(members)]
            got.append(lax.ppermute(blocks[index][s, :, cut], "row", pairs))
        received.append(got)

    all_cells = obs_cells.reshape(-1)
    picked = pick_columns(blocks, tuple(n * nx for n in leads), all_cells, me, zonal)
    picked = lax.all_gather(picked, "row", axis=0, tiled=True)
    below = lax.ppermute(picked[local_rows - halo :], "grp", forward)
    above = lax.ppermute(picked[:halo], "grp", backward)
    picked = jnp.concatenate([below, picked, above], axis=0)
    count = all_cells.shape[0]
    columns = column_step(
        me_arg, column_coefs, [picked], [("fixed", 0)], halo, nx, grid_rows,
        min(256, count), (local_rows, count), 0,
    )
    first_mine = me * zonal
    mine = lax.dynamic_slice_in_dim(columns, first_mine % local_rows, zonal, 0)
    mine = jnp.where(group == first_mine // local_rows, mine, 0.0)
    place = all_cells - group * local_rows
    held = (place >= 0) & (place < local_rows)
    inner = jnp.where(held[:, None], columns[jnp.clip(place, 0, local_rows - 1)], 0.0)
    mine, inner = lax.psum((mine, inner), "grp")
    gains = gains_of(columns, mine.T, inner, obs_var)

    edge = halo // rows
    result = None
    for k, (index, start, take) in enumerate(slots):
        got = received[k]
        if result is not None:
            got, result = lax.optimization_barrier((got, result))
        last = [lax.select_n(jnp.bitwise_xor(me, members - edge + i), *got) for i in range(edge)]
        head = [lax.select_n(jnp.bitwise_xor(me, i), *got) for i in range(edge)]
        below = lax.ppermute(jnp.concatenate(last, axis=0), "grp", forward)
        above = lax.ppermute(jnp.concatenate(head, axis=0), "grp", backward)
        parts = [below, above, blocks[index]] + got[1:]
        sources = [("fixed", 0), ("fixed", halo + local_rows), ("partner", 0)]
        sources += [("partner", s) for s in range(1, members)]
        result = column_step(
            me_arg, column_coefs, parts, tuple(sources), halo, nx, grid_rows,
            min(256, take * nx), (local_rows, zonal), (leads[index] + start) * nx,
            start * nx, gains, result,
        )
    return result


def plan(per_dest):
    shares = [per_dest] if per_dest <= 4 else [4, per_dest - 4]
    slots = []
    for index, depth in enumerate(shares):
        done = 0
        while done < depth:
            take = min(4, depth - done)
            if index > 0 and depth - done <= 4:
                take = min(2, depth - done)
            slots.append((index, done, take))
            done += take
    return shares, slots


def solution(mesh):
    placed = (P(("grp", "row"), None), P(), P(), P(), P())

    return jax.shard_map(
        local, mesh=mesh, in_specs=placed, out_specs=P("grp", "row"), check_vma=False
    )
```

time: 2000 us -> 1440 us (0.72)
  the two profiles are of different devices: /device:TPU:0 before, /device:TPU:22 now
where the time goes in v1:
time: 1440 us; the launch traced here: 1430 us
  waiting for transfers between devices  552 us (38%)
  Pallas kernels  526 us (37%)
  starting transfers between devices  149 us (10%)
  other arithmetic  86.6 us (6%)
  local copies, waits for them, and re-layouts  64.1 us (4%)
  matrix products  39.8 us (3%)
  between operations  15 us (1%)
    ppermute x35, waiting for transfers between devices, local(): got.append(lax.ppermute(blocks[index][s, :, cut], 'row', pairs))  423 us
    pallas_call x2, Pallas kernels, row_step(): pl.pallas_call(functools.partial(row_step_kernel, nx=nx, per_dest=per_des...  320 us
    pallas_call x6, Pallas kernels, column_step(): pl.pallas_call(functools.partial(column_step_kernel, sources=sources, hal...  206 us
    ppermute x35, starting transfers between devices, local(): got.append(lax.ppermute(blocks[index][s, :, cut], 'row', pairs))  103 us
    ppermute x5, waiting for transfers between devices, local(): below = lax.ppermute(jnp.concatenate(last, axis=0), 'grp', forward)  52.7 us
    all_gather x1, waiting for transfers between devices, local(): picked = lax.all_gather(picked, 'row', axis=0, tiled=True)  36.8 us
    ppermute x5, starting transfers between devices, local(): above = lax.ppermute(jnp.concatenate(head, axis=0), 'grp', backward)  33.6 us
    dot_general x16, matrix products, pick_columns(): total = total + jnp.dot(array[s], chosen, precision=lax.Precision.HIGH)  29.1 us
  transfers between devices with their start and end apart: 49, of which 28 were waited for; matrix products, arithmetic and copies ran while one was open for 10% of the time, Pallas kernels for 12%

profile of v1, /device:TPU:22, one launch (start us, length us, event | category | flops | bytes accessed | tf_op | source)
XLA Modules:
  0.0 1433.0 jit_solution(15543772627211000301)
XLA Ops:
  14.5 82.2 %row_step.3.refs_3_ = f32[8,512,512]{2,1,0:T(8,128)} custom-call(s32[1]{0:T(128)} %bitcast.me_ref, f32[7,1024,128]{2,1,0:T(8,128)} %bitcast_dynamic-update-slice_fusion.coef_ref, f32[512,16384]{1,0:T(8,128)} %p_ref.3), custom_call_target="tpu_custom_call" | custom-call | flops 125829120 | bytes 67108864 | tf_op jit(solution)/shard_map/row_step/pallas_call | solution.py:119
  96.7 237.6 %row_step.2.refs_3_ = f32[8,512,1536]{2,1,0:T(8,128)} custom-call(s32[1]{0:T(128)} %bitcast.me_ref, f32[7,1024,128]{2,1,0:T(8,128)} %bitcast_dynamic-update-slice_fusion.coef_ref, f32[512,16384]{1,0:T(8,128)} %p_ref.3), custom_call_target="tpu_custom_call" | custom-call | flops 377487360 | bytes 201326592 | tf_op jit(solution)/shard_map/row_step/pallas_call | solution.py:119
  343.3 3.1 fusion.3
  349.4 3.1 fusion.5
  364.2 6.1 slice_bitcast_fusion.23
  372.0 3.2 broadcast_dynamic-update-slice_fusion.6
  375.2 3.2 broadcast_dynamic-update-slice_fusion.5
  378.4 3.2 broadcast_dynamic-update-slice_fusion.4
  381.6 3.2 broadcast_dynamic-update-slice_fusion.3
  384.8 3.2 broadcast_dynamic-update-slice_fusion.2
  388.0 3.3 broadcast_dynamic-update-slice_fusion.1
  391.3 3.2 broadcast_dynamic-update-slice_fusion.refs_0_
  394.5 36.8 %all-gather.2.cloned.1.call-done = f32[4096,256]{1,0:T(8,128)} async-done(((f32[512,256]{1,0:T(8,128)}), f32[4096,256]{1,0:T(8,128)}) %all-gather.2.cloned.1.call-update) | async-done | bytes 4194320 | tf_op jit(solution)/shard_map/all_gather | solution.py:383
  433.9 4.6 collective-permute-start.38
  438.5 10.8 collective-permute-done.37
  449.7 4.9 pad_maximum_fusion.1.refs_1_
  454.6 18.5 %column_step.6 = f32[4096,256]{1,0:T(8,128)} custom-call(s32[1]{0:T(128)} %bitcast.me_ref, f32[7,5120,128]{2,1,0:T(8,128)} %broadcast_dynamic-update-slice_fusion.refs_0_, f32[5120,256]{1,0:T(8,128)} %pad_maximum_fusion.1.refs_1_), custom_call_target="tpu_custom_call" | custom-call | flops 104857600 | bytes 33554432 | tf_op jit(solution)/shard_map/column_step/pallas_call | solution.py:282
  473.1 3.2 gather_fusion
  484.8 12.2 slice_bitcast_fusion.25
  497.0 26.5 %collective-permute-done.30.refs_6_ = f32[512,512]{1,0:T(8,128)S(1)} collective-permute-done((f32[512,512]{1,0:T(8,128)}, f32[512,512]{1,0:T(8,128)S(1)}, u32[]{:S(2)}, u32[]{:S(2)}) %collective-permute-start.30) | collective-permute-done | bytes 1048608 | tf_op jit(solution)/shard_map/ppermute | solution.py:378
  523.5 3.5 collective-permute-done.31.refs_7_
  527.0 70.7 %collective-permute-start.22 = (f32[512,512]{1,0:T(8,128)}, f32[512,512]{1,0:T(8,128)}, u32[]{:S(2)}, u32[]{:S(2)}) collective-permute-start(f32[512,512]{1,0:T(8,128)} %get-tuple-element.121), channel_id=1, source_target_pairs={{0,2},{1,3},{2,0},{3,1},{4,6},{5,7},{6,4},{7,5},{8,10},{9,11},{10,... | collective-permute-start | bytes 3145736 | tf_op jit(solution)/shard_map/ppermute | solution.py:378
  597.7 19.0 %collective-permute-done.32.refs_8_ = f32[512,512]{1,0:T(8,128)} collective-permute-done((f32[512,512]{1,0:T(8,128)}, f32[512,512]{1,0:T(8,128)}, u32[]{:S(2)}, u32[]{:S(2)}) %collective-permute-start.32) | collective-permute-done | bytes 1048608 | tf_op jit(solution)/shard_map/ppermute | solution.py:378
  616.7 3.2 collective-permute-start.23
  620.0 21.3 %collective-permute-done.33.refs_9_ = f32[512,512]{1,0:T(8,128)} collective-permute-done((f32[512,512]{1,0:T(8,128)}, f32[512,512]{1,0:T(8,128)}, u32[]{:S(2)}, u32[]{:S(2)}) %collective-permute-start.33) | collective-permute-done | bytes 1048608 | tf_op jit(solution)/shard_map/ppermute | solution.py:378
  641.2 22.9 %collective-permute-done.34.refs_10_ = f32[512,512]{1,0:T(8,128)} collective-permute-done((f32[512,512]{1,0:T(8,128)}, f32[512,512]{1,0:T(8,128)}, u32[]{:S(2)}, u32[]{:S(2)}) %collective-permute-start.34) | collective-permute-done | bytes 1048608 | tf_op jit(solution)/shard_map/ppermute | solution.py:378
  664.2 3.9 select_select_fusion.4
  668.1 12.8 collective-permute-start.36
  680.8 3.9 select_select_fusion.5
  688.4 11.7 cholesky.44
  701.5 9.8 custom-call.12
  720.5 11.7 cholesky.55
  733.6 9.8 custom-call.13
  758.5 44.2 %column_step.7.refs_13_ = f32[4096,2048]{1,0:T(8,128)} custom-call(s32[1]{0:T(128)} %bitcast.me_ref, f32[7,5120,128]{2,1,0:T(8,128)} %broadcast_dynamic-update-slice_fusion.refs_0_, f32[512,512]{1,0:T(8,128)} %collective-permute-done.35.refs_1_, f32[512,512]{1,0:T(8,128)} %collective-permute-done.36.refs_2_, f32[8,512,512]{2,1,0:T(8,128)} %row_step.3.refs_3_, ...), custom_call_target="tpu_custom_call" | custom-call | flops 209715200 | bytes 67108864 | tf_op jit(solution)/shard_map/column_step/pallas_call | solution.py:282
  802.7 59.3 %collective-permute-done.24.refs_7_ = f32[512,512]{1,0:T(8,128)S(1)} collective-permute-done((f32[512,512]{1,0:T(8,128)S(1)}, f32[512,512]{1,0:T(8,128)S(1)}, u32[]{:S(2)}, u32[]{:S(2)}) %collective-permute-start.24) | collective-permute-done | bytes 1048608 | tf_op jit(solution)/shard_map/ppermute | solution.py:378
  864.4 20.3 %collective-permute-done.25.refs_8_ = f32[512,512]{1,0:T(8,128)} collective-permute-done((f32[512,512]{1,0:T(8,128)}, f32[512,512]{1,0:T(8,128)}, u32[]{:S(2)}, u32[]{:S(2)}) %collective-permute-start.25) | collective-permute-done | bytes 1048608 | tf_op jit(solution)/shard_map/ppermute | solution.py:378
  884.6 23.4 %collective-permute-done.26.refs_9_ = f32[512,512]{1,0:T(8,128)} collective-permute-done((f32[512,512]{1,0:T(8,128)}, f32[512,512]{1,0:T(8,128)}, u32[]{:S(2)}, u32[]{:S(2)}) %collective-permute-start.26) | collective-permute-done | bytes 1048608 | tf_op jit(solution)/shard_map/ppermute | solution.py:378
  908.0 20.5 %collective-permute-done.27.refs_10_ = f32[512,512]{1,0:T(8,128)} collective-permute-done((f32[512,512]{1,0:T(8,128)}, f32[512,512]{1,0:T(8,128)}, u32[]{:S(2)}, u32[]{:S(2)}) %collective-permute-start.27) | collective-permute-done | bytes 1048608 | tf_op jit(solution)/shard_map/ppermute | solution.py:378
  931.6 6.0 collective-permute-start.40
  944.9 15.1 %collective-permute-done.40.refs_2_ = f32[512,512]{1,0:T(8,128)} collective-permute-done((f32[512,512]{1,0:T(8,128)S(1)}, f32[512,512]{1,0:T(8,128)}, u32[]{:S(2)}, u32[]{:S(2)}) %collective-permute-start.40) | collective-permute-done | bytes 1048608 | tf_op jit(solution)/shard_map/ppermute | solution.py:410
  961.4 24.3 %collective-permute-done.39.refs_1_ = f32[512,512]{1,0:T(8,128)} collective-permute-done((f32[512,512]{1,0:T(8,128)S(1)}, f32[512,512]{1,0:T(8,128)}, u32[]{:S(2)}, u32[]{:S(2)}) %collective-permute-start.39) | collective-permute-done | bytes 1048608 | tf_op jit(solution)/shard_map/ppermute | solution.py:409
  986.8 44.2 %column_step.8.refs_13_ = f32[4096,2048]{1,0:T(8,128)} custom-call(s32[1]{0:T(128)} %bitcast.me_ref, f32[7,5120,128]{2,1,0:T(8,128)} %broadcast_dynamic-update-slice_fusion.refs_0_, f32[512,512]{1,0:T(8,128)} %collective-permute-done.39.refs_1_, f32[512,512]{1,0:T(8,128)} %collective-permute-done.40.refs_2_, ...), custom_call_target="tpu_custom_call", output_to_operand_aliasing={{}: (14, {})} | custom-call | flops 209715200 | bytes 67108864 | tf_op jit(solution)/shard_map/column_step/pallas_call | solution.py:282
  1031.0 27.7 %collective-permute-done.17.refs_7_ = f32[512,512]{1,0:T(8,128)} collective-permute-done((f32[512,512]{1,0:T(8,128)}, f32[512,512]{1,0:T(8,128)}, u32[]{:S(2)}, u32[]{:S(2)}) %collective-permute-start.17) | collective-permute-done | bytes 1048608 | tf_op jit(solution)/shard_map/ppermute | solution.py:378
  1058.7 22.5 %collective-permute-done.18.refs_8_ = f32[512,512]{1,0:T(8,128)} collective-permute-done((f32[512,512]{1,0:T(8,128)}, f32[512,512]{1,0:T(8,128)}, u32[]{:S(2)}, u32[]{:S(2)}) %collective-permute-start.18) | collective-permute-done | bytes 1048608 | tf_op jit(solution)/shard_map/ppermute | solution.py:378
  1081.2 23.6 %collective-permute-done.19.refs_9_ = f32[512,512]{1,0:T(8,128)} collective-permute-done((f32[512,512]{1,0:T(8,128)}, f32[512,512]{1,0:T(8,128)}, u32[]{:S(2)}, u32[]{:S(2)}) %collective-permute-start.19) | collective-permute-done | bytes 1048608 | tf_op jit(solution)/shard_map/ppermute | solution.py:378
  1104.8 20.6 %collective-permute-done.20.refs_10_ = f32[512,512]{1,0:T(8,128)} collective-permute-done((f32[512,512]{1,0:T(8,128)}, f32[512,512]{1,0:T(8,128)}, u32[]{:S(2)}, u32[]{:S(2)}) %collective-permute-start.20) | collective-permute-done | bytes 1048608 | tf_op jit(solution)/shard_map/ppermute | solution.py:378
  1128.1 5.5 collective-permute-start.42
  1137.5 6.4 slice_bitcast_fusion.42
  1148.3 41.8 %collective-permute-done.10.refs_7_ = f32[512,256]{1,0:T(8,128)S(1)} collective-permute-done((f32[512,256]{1,0:T(8,128)S(1)}, f32[512,256]{1,0:T(8,128)S(1)}, u32[]{:S(2)}, u32[]{:S(2)}) %collective-permute-start.10) | collective-permute-done | bytes 524320 | tf_op jit(solution)/shard_map/ppermute | solution.py:378
  1190.4 22.1 %collective-permute-done.11.refs_8_ = f32[512,256]{1,0:T(8,128)S(1)} collective-permute-done((f32[512,256]{1,0:T(8,128)S(1)}, f32[512,256]{1,0:T(8,128)S(1)}, u32[]{:S(2)}, u32[]{:S(2)}) %collective-permute-start.11) | collective-permute-done | bytes 524320 | tf_op jit(solution)/shard_map/ppermute | solution.py:378
  1212.6 3.8 collective-permute-start.8
  1217.4 44.2 %column_step.9.refs_13_ = f32[4096,2048]{1,0:T(8,128)} custom-call(s32[1]{0:T(128)} %bitcast.me_ref, f32[7,5120,128]{2,1,0:T(8,128)} %broadcast_dynamic-update-slice_fusion.refs_0_, f32[512,512]{1,0:T(8,128)} %copy-done.27, f32[512,512]{1,0:T(8,128)} %collective-permute-done.42.refs_2_, ...), custom_call_target="tpu_custom_call", output_to_operand_aliasing={{}: (14, {})} | custom-call | flops 209715200 | bytes 67108864 | tf_op jit(solution)/shard_map/column_step/pallas_call | solution.py:282
  1264.3 4.6 collective-permute-start.44
  1272.3 4.4 collective-permute-done.1.refs_5_
  1276.8 3.2 collective-permute-done.44.refs_2_
  1280.0 14.0 collective-permute-done.43.refs_1_
  1294.8 27.6 %column_step.10.refs_13_ = f32[4096,2048]{1,0:T(8,128)} custom-call(s32[1]{0:T(128)} %bitcast.me_ref, f32[7,5120,128]{2,1,0:T(8,128)} %broadcast_dynamic-update-slice_fusion.refs_0_, f32[512,256]{1,0:T(8,128)} %copy-done.30, f32[512,256]{1,0:T(8,128)} %copy-done.29, f32[8,512,1536]{2,1,0:T(8,128)} %row_step.2.refs_3_, ...), custom_call_target="tpu_custom_call", output_to_operand_aliasing={{}: (14, {})} | custom-call | flops 104857600 | bytes 33554432 | tf_op jit(solution)/shard_map/column_step/pallas_call | solution.py:282
  1322.4 17.0 %collective-permute-done.4.refs_8_ = f32[512,256]{1,0:T(8,128)S(1)} collective-permute-done((f32[512,256]{1,0:T(8,128)}, f32[512,256]{1,0:T(8,128)S(1)}, u32[]{:S(2)}, u32[]{:S(2)}) %collective-permute-start.4) | collective-permute-done | bytes 524320 | tf_op jit(solution)/shard_map/ppermute | solution.py:378
  1339.4 15.3 %collective-permute-done.5.refs_9_ = f32[512,256]{1,0:T(8,128)S(1)} collective-permute-done((f32[512,256]{1,0:T(8,128)}, f32[512,256]{1,0:T(8,128)S(1)}, u32[]{:S(2)}, u32[]{:S(2)}) %collective-permute-start.5) | collective-permute-done | bytes 524320 | tf_op jit(solution)/shard_map/ppermute | solution.py:378
  1354.7 11.2 collective-permute-done.6.refs_10_
  1366.8 4.8 collective-permute-start.46
  1372.9 10.1 collective-permute-done.46.refs_2_
  1383.0 14.4 %collective-permute-done.45.refs_1_ = f32[512,256]{1,0:T(8,128)S(1)} collective-permute-done((f32[512,256]{1,0:T(8,128)S(1)}, f32[512,256]{1,0:T(8,128)S(1)}, u32[]{:S(2)}, u32[]{:S(2)}) %collective-permute-start.45) | collective-permute-done | bytes 524320 | tf_op jit(solution)/shard_map/ppermute | solution.py:409
  1398.3 27.5 %column_step.11 = f32[4096,2048]{1,0:T(8,128)} custom-call(s32[1]{0:T(128)} %bitcast.me_ref, f32[7,5120,128]{2,1,0:T(8,128)} %broadcast_dynamic-update-slice_fusion.refs_0_, f32[512,256]{1,0:T(8,128)} %copy-done.32, f32[512,256]{1,0:T(8,128)} %copy-done.31, f32[8,512,1536]{2,1,0:T(8,128)} %row_step.2.refs_3_, ...), custom_call_target="tpu_custom_call", output_to_operand_aliasing={{}: (14, {})} | custom-call | flops 104857600 | bytes 33554432 | tf_op jit(solution)/shard_map/column_step/pallas_call | solution.py:282
  (243 shorter events, 112.1 us)
Async XLA Ops:
  6.5 424.8 %all-gather.2.cloned.1.call-start = ((), (), s32[]{:S(2)}) async-start(), calls=%async_computation | async-start | bytes 4718592 | tf_op jit(solution)/shard_map/all_gather | solution.py:383
  96.7 237.7 %copy-start.34 = (s32[2,128]{1,0:T(2,128)S(1)}, s32[2,128]{1,0:T(2,128)}, u32[]{:S(2)}) copy-start(s32[2,128]{1,0:T(2,128)} %param.15) | copy-start | bytes 3076
  363.8 322.5 %all-reduce.10.cloned.1.call-start = ((), (), s32[]{:S(2)}) async-start(), calls=%async_computation.1 | async-start | bytes 4718592 | tf_op jit(solution)/shard_map/psum | solution.py:398
  370.3 111.7 %collective-permute-start.28 = (f32[512,512]{1,0:T(8,128)}, f32[512,512]{1,0:T(8,128)S(1)}, u32[]{:S(2)}, u32[]{:S(2)}) collective-permute-start(f32[512,512]{1,0:T(8,128)} %get-tuple-element.148), channel_id=1, source_target_pairs={{0,1},{1,0},{2,3},{3,2},{4,5},{5,4},{6,7},{7,6},{8,9},{9,8},{10,11... | collective-permute-start | bytes 3145736 | tf_op jit(solution)/shard_map/ppermute | solution.py:378
  370.3 113.2 %collective-permute-start.29 = (f32[512,512]{1,0:T(8,128)}, f32[512,512]{1,0:T(8,128)S(1)}, u32[]{:S(2)}, u32[]{:S(2)}) collective-permute-start(f32[512,512]{1,0:T(8,128)} %get-tuple-element.154), channel_id=1, source_target_pairs={{0,2},{1,3},{2,0},{3,1},{4,6},{5,7},{6,4},{7,5},{8,10},{9,11},{10,... | collective-permute-start | bytes 3145736 | tf_op jit(solution)/shard_map/ppermute | solution.py:378
  432.6 16.7 %collective-permute-start.37 = (f32[512,256]{1,0:T(8,128)S(1)}, f32[512,256]{1,0:T(8,128)S(1)}, u32[]{:S(2)}, u32[]{:S(2)}) collective-permute-start(f32[512,256]{1,0:T(8,128)S(1)} %get-tuple-element.157), channel_id=1, source_target_pairs={{0,8},{8,16},{16,24},{1,9},{9,17},{17,25},{2,10},{10,18},{18,26},{... | collective-permute-start | bytes 1572872 | tf_op jit(solution)/shard_map/ppermute | solution.py:384
  433.9 15.8 %collective-permute-start.38 = (f32[512,256]{1,0:T(8,128)S(1)}, f32[512,256]{1,0:T(8,128)S(1)}, u32[]{:S(2)}, u32[]{:S(2)}) collective-permute-start(f32[512,256]{1,0:T(8,128)S(1)} %get-tuple-element.158), channel_id=1, source_target_pairs={{8,0},{16,8},{24,16},{9,1},{17,9},{25,17},{10,2},{18,10},{26,18},{... | collective-permute-start | bytes 1572872 | tf_op jit(solution)/shard_map/ppermute | solution.py:385
  480.2 43.3 %collective-permute-start.30 = (f32[512,512]{1,0:T(8,128)}, f32[512,512]{1,0:T(8,128)S(1)}, u32[]{:S(2)}, u32[]{:S(2)}) collective-permute-start(f32[512,512]{1,0:T(8,128)} %get-tuple-element.153), channel_id=1, source_target_pairs={{0,3},{1,2},{2,1},{3,0},{4,7},{5,6},{6,5},{7,4},{8,11},{9,10},{10,... | collective-permute-start | bytes 3145736 | tf_op jit(solution)/shard_map/ppermute | solution.py:378
  480.3 46.8 %collective-permute-start.31 = (f32[512,512]{1,0:T(8,128)}, f32[512,512]{1,0:T(8,128)}, u32[]{:S(2)}, u32[]{:S(2)}) collective-permute-start(f32[512,512]{1,0:T(8,128)} %get-tuple-element.152), channel_id=1, source_target_pairs={{0,4},{1,5},{2,6},{3,7},{4,0},{5,1},{6,2},{7,3},{8,12},{9,13},{10,... | collective-permute-start | bytes 3145736 | tf_op jit(solution)/shard_map/ppermute | solution.py:378
  480.9 135.9 %collective-permute-start.32 = (f32[512,512]{1,0:T(8,128)}, f32[512,512]{1,0:T(8,128)}, u32[]{:S(2)}, u32[]{:S(2)}) collective-permute-start(f32[512,512]{1,0:T(8,128)} %get-tuple-element.151), channel_id=1, source_target_pairs={{0,5},{1,4},{2,7},{3,6},{4,1},{5,0},{6,3},{7,2},{8,13},{9,12},{10,... | collective-permute-start | bytes 3145736 | tf_op jit(solution)/shard_map/ppermute | solution.py:378
  481.9 198.9 %copy-start.3 = (f32[512,512]{1,0:T(8,128)}, f32[512,512]{1,0:T(8,128)S(1)}, u32[]{:S(2)}) copy-start(f32[512,512]{1,0:T(8,128)S(1)} %collective-permute-done.28.refs_4_) | copy-start | bytes 3145732
  481.9 159.3 %collective-permute-start.33 = (f32[512,512]{1,0:T(8,128)}, f32[512,512]{1,0:T(8,128)}, u32[]{:S(2)}, u32[]{:S(2)}) collective-permute-start(f32[512,512]{1,0:T(8,128)} %get-tuple-element.150), channel_id=1, source_target_pairs={{0,6},{1,7},{2,4},{3,5},{4,2},{5,3},{6,0},{7,1},{8,14},{9,15},{10,... | collective-permute-start | bytes 3145736 | tf_op jit(solution)/shard_map/ppermute | solution.py:378
  483.5 197.3 %copy-start.4 = (f32[512,512]{1,0:T(8,128)}, f32[512,512]{1,0:T(8,128)S(1)}, u32[]{:S(2)}) copy-start(f32[512,512]{1,0:T(8,128)S(1)} %collective-permute-done.29.refs_5_) | copy-start | bytes 3145732
  483.5 180.7 %collective-permute-start.34 = (f32[512,512]{1,0:T(8,128)}, f32[512,512]{1,0:T(8,128)}, u32[]{:S(2)}, u32[]{:S(2)}) collective-permute-start(f32[512,512]{1,0:T(8,128)} %get-tuple-element.149), channel_id=1, source_target_pairs={{0,7},{1,6},{2,5},{3,4},{4,3},{5,2},{6,1},{7,0},{8,15},{9,14},{10,... | collective-permute-start | bytes 3145736 | tf_op jit(solution)/shard_map/ppermute | solution.py:378
  523.5 157.3 %copy-start.5 = (f32[512,512]{1,0:T(8,128)}, f32[512,512]{1,0:T(8,128)S(1)}, u32[]{:S(2)}) copy-start(f32[512,512]{1,0:T(8,128)S(1)} %collective-permute-done.30.refs_6_) | copy-start | bytes 3145732
  523.5 224.6 %collective-permute-start.21 = (f32[512,512]{1,0:T(8,128)}, f32[512,512]{1,0:T(8,128)}, u32[]{:S(2)}, u32[]{:S(2)}) collective-permute-start(f32[512,512]{1,0:T(8,128)} %get-tuple-element.122), channel_id=1, source_target_pairs={{0,1},{1,0},{2,3},{3,2},{4,5},{5,4},{6,7},{7,6},{8,9},{9,8},{10,11... | collective-permute-start | bytes 3145736 | tf_op jit(solution)/shard_map/ppermute | solution.py:378
  527.0 221.6 %collective-permute-start.22 = (f32[512,512]{1,0:T(8,128)}, f32[512,512]{1,0:T(8,128)}, u32[]{:S(2)}, u32[]{:S(2)}) collective-permute-start(f32[512,512]{1,0:T(8,128)} %get-tuple-element.121), channel_id=1, source_target_pairs={{0,2},{1,3},{2,0},{3,1},{4,6},{5,7},{6,4},{7,5},{8,10},{9,11},{10,... | collective-permute-start | bytes 3145736 | tf_op jit(solution)/shard_map/ppermute | solution.py:378
  616.7 185.9 %collective-permute-start.23 = (f32[512,512]{1,0:T(8,128)}, f32[512,512]{1,0:T(8,128)}, u32[]{:S(2)}, u32[]{:S(2)}) collective-permute-start(f32[512,512]{1,0:T(8,128)} %get-tuple-element.120), channel_id=1, source_target_pairs={{0,3},{1,2},{2,1},{3,0},{4,7},{5,6},{6,5},{7,4},{8,11},{9,10},{10,... | collective-permute-start | bytes 3145736 | tf_op jit(solution)/shard_map/ppermute | solution.py:378
  668.1 82.5 %collective-permute-start.36 = (f32[512,512]{1,0:T(8,128)}, f32[512,512]{1,0:T(8,128)}, u32[]{:S(2)}, u32[]{:S(2)}) collective-permute-start(f32[512,512]{1,0:T(8,128)} %select_select_fusion.4), channel_id=1, source_target_pairs={{8,0},{16,8},{24,16},{9,1},{17,9},{25,17},{10,2},{18,10},{26,18},{... | collective-permute-start | bytes 3145736 | tf_op jit(solution)/shard_map/ppermute | solution.py:410
  684.8 66.2 %collective-permute-start.35 = (f32[512,512]{1,0:T(8,128)}, f32[512,512]{1,0:T(8,128)}, u32[]{:S(2)}, u32[]{:S(2)}) collective-permute-start(f32[512,512]{1,0:T(8,128)} %select_select_fusion.5), channel_id=1, source_target_pairs={{0,8},{8,16},{16,24},{1,9},{9,17},{17,25},{2,10},{10,18},{18,26},{... | collective-permute-start | bytes 3145736 | tf_op jit(solution)/shard_map/ppermute | solution.py:409
  748.6 113.4 %collective-permute-start.24 = (f32[512,512]{1,0:T(8,128)S(1)}, f32[512,512]{1,0:T(8,128)S(1)}, u32[]{:S(2)}, u32[]{:S(2)}) collective-permute-start(f32[512,512]{1,0:T(8,128)S(1)} %copy-done.28), channel_id=1, source_target_pairs={{0,4},{1,5},{2,6},{3,7},{4,0},{5,1},{6,2},{7,3},{8,12},{9,13},{10,... | collective-permute-start | bytes 3145736 | tf_op jit(solution)/shard_map/ppermute | solution.py:378
  748.6 136.0 %collective-permute-start.25 = (f32[512,512]{1,0:T(8,128)}, f32[512,512]{1,0:T(8,128)}, u32[]{:S(2)}, u32[]{:S(2)}) collective-permute-start(f32[512,512]{1,0:T(8,128)} %get-tuple-element.118), channel_id=1, source_target_pairs={{0,5},{1,4},{2,7},{3,6},{4,1},{5,0},{6,3},{7,2},{8,13},{9,12},{10,... | collective-permute-start | bytes 3145736 | tf_op jit(solution)/shard_map/ppermute | solution.py:378
  750.5 157.5 %collective-permute-start.26 = (f32[512,512]{1,0:T(8,128)}, f32[512,512]{1,0:T(8,128)}, u32[]{:S(2)}, u32[]{:S(2)}) collective-permute-start(f32[512,512]{1,0:T(8,128)} %get-tuple-element.117), channel_id=1, source_target_pairs={{0,6},{1,7},{2,4},{3,5},{4,2},{5,3},{6,0},{7,1},{8,14},{9,15},{10,... | collective-permute-start | bytes 3145736 | tf_op jit(solution)/shard_map/ppermute | solution.py:378
  750.9 177.6 %collective-permute-start.27 = (f32[512,512]{1,0:T(8,128)}, f32[512,512]{1,0:T(8,128)}, u32[]{:S(2)}, u32[]{:S(2)}) collective-permute-start(f32[512,512]{1,0:T(8,128)} %get-tuple-element.116), channel_id=1, source_target_pairs={{0,7},{1,6},{2,5},{3,4},{4,3},{5,2},{6,1},{7,0},{8,15},{9,14},{10,... | collective-permute-start | bytes 3145736 | tf_op jit(solution)/shard_map/ppermute | solution.py:378
  802.7 139.1 %collective-permute-start.14 = (f32[512,512]{1,0:T(8,128)}, f32[512,512]{1,0:T(8,128)S(1)}, u32[]{:S(2)}, u32[]{:S(2)}) collective-permute-start(f32[512,512]{1,0:T(8,128)} %get-tuple-element.130), channel_id=1, source_target_pairs={{0,1},{1,0},{2,3},{3,2},{4,5},{5,4},{6,7},{7,6},{8,9},{9,8},{10,11... | collective-permute-start | bytes 3145736 | tf_op jit(solution)/shard_map/ppermute | solution.py:378
  862.0 75.5 %copy-start.9 = (f32[512,512]{1,0:T(8,128)}, f32[512,512]{1,0:T(8,128)S(1)}, u32[]{:S(2)}) copy-start(f32[512,512]{1,0:T(8,128)S(1)} %collective-permute-done.24.refs_7_) | copy-start | bytes 3145732
  862.0 82.9 %collective-permute-start.15 = (f32[512,512]{1,0:T(8,128)}, f32[512,512]{1,0:T(8,128)S(1)}, u32[]{:S(2)}, u32[]{:S(2)}) collective-permute-start(f32[512,512]{1,0:T(8,128)} %get-tuple-element.129), channel_id=1, source_target_pairs={{0,2},{1,3},{2,0},{3,1},{4,6},{5,7},{6,4},{7,5},{8,10},{9,11},{10,... | collective-permute-start | bytes 3145736 | tf_op jit(solution)/shard_map/ppermute | solution.py:378
  931.6 28.4 %collective-permute-start.40 = (f32[512,512]{1,0:T(8,128)S(1)}, f32[512,512]{1,0:T(8,128)}, u32[]{:S(2)}, u32[]{:S(2)}) collective-permute-start(f32[512,512]{1,0:T(8,128)S(1)} %select_select_fusion.2), channel_id=1, source_target_pairs={{8,0},{16,8},{24,16},{9,1},{17,9},{25,17},{10,2},{18,10},{26,18},{... | collective-permute-start | bytes 3145736 | tf_op jit(solution)/shard_map/ppermute | solution.py:410
  940.4 45.2 %collective-permute-start.39 = (f32[512,512]{1,0:T(8,128)S(1)}, f32[512,512]{1,0:T(8,128)}, u32[]{:S(2)}, u32[]{:S(2)}) collective-permute-start(f32[512,512]{1,0:T(8,128)S(1)} %select_select_fusion.3), channel_id=1, source_target_pairs={{0,8},{8,16},{16,24},{1,9},{9,17},{17,25},{2,10},{10,18},{18,26},{... | collective-permute-start | bytes 3145736 | tf_op jit(solution)/shard_map/ppermute | solution.py:409
  941.7 89.2 %collective-permute-start.16 = (f32[512,512]{1,0:T(8,128)}, f32[512,512]{1,0:T(8,128)S(1)}, u32[]{:S(2)}, u32[]{:S(2)}) collective-permute-start(f32[512,512]{1,0:T(8,128)} %get-tuple-element.128), channel_id=1, source_target_pairs={{0,3},{1,2},{2,1},{3,0},{4,7},{5,6},{6,5},{7,4},{8,11},{9,10},{10,... | collective-permute-start | bytes 3145736 | tf_op jit(solution)/shard_map/ppermute | solution.py:378
  941.8 191.8 %copy-start.6 = (f32[512,512]{1,0:T(8,128)}, f32[512,512]{1,0:T(8,128)S(1)}, u32[]{:S(2)}) copy-start(f32[512,512]{1,0:T(8,128)S(1)} %collective-permute-done.14.refs_4_) | copy-start | bytes 3145732
  941.8 116.9 %collective-permute-start.17 = (f32[512,512]{1,0:T(8,128)}, f32[512,512]{1,0:T(8,128)}, u32[]{:S(2)}, u32[]{:S(2)}) collective-permute-start(f32[512,512]{1,0:T(8,128)} %get-tuple-element.127), channel_id=1, source_target_pairs={{0,4},{1,5},{2,6},{3,7},{4,0},{5,1},{6,2},{7,3},{8,12},{9,13},{10,... | collective-permute-start | bytes 3145736 | tf_op jit(solution)/shard_map/ppermute | solution.py:378
  944.9 188.7 %copy-start.7 = (f32[512,512]{1,0:T(8,128)}, f32[512,512]{1,0:T(8,128)S(1)}, u32[]{:S(2)}) copy-start(f32[512,512]{1,0:T(8,128)S(1)} %collective-permute-done.15.refs_5_) | copy-start | bytes 3145732
  944.9 136.3 %collective-permute-start.18 = (f32[512,512]{1,0:T(8,128)}, f32[512,512]{1,0:T(8,128)}, u32[]{:S(2)}, u32[]{:S(2)}) collective-permute-start(f32[512,512]{1,0:T(8,128)} %get-tuple-element.126), channel_id=1, source_target_pairs={{0,5},{1,4},{2,7},{3,6},{4,1},{5,0},{6,3},{7,2},{8,13},{9,12},{10,... | collective-permute-start | bytes 3145736 | tf_op jit(solution)/shard_map/ppermute | solution.py:378
  960.0 144.8 %collective-permute-start.19 = (f32[512,512]{1,0:T(8,128)}, f32[512,512]{1,0:T(8,128)}, u32[]{:S(2)}, u32[]{:S(2)}) collective-permute-start(f32[512,512]{1,0:T(8,128)} %get-tuple-element.125), channel_id=1, source_target_pairs={{0,6},{1,7},{2,4},{3,5},{4,2},{5,3},{6,0},{7,1},{8,14},{9,15},{10,... | collective-permute-start | bytes 3145736 | tf_op jit(solution)/shard_map/ppermute | solution.py:378
  985.7 139.7 %collective-permute-start.20 = (f32[512,512]{1,0:T(8,128)}, f32[512,512]{1,0:T(8,128)}, u32[]{:S(2)}, u32[]{:S(2)}) collective-permute-start(f32[512,512]{1,0:T(8,128)} %get-tuple-element.124), channel_id=1, source_target_pairs={{0,7},{1,6},{2,5},{3,4},{4,3},{5,2},{6,1},{7,0},{8,15},{9,14},{10,... | collective-permute-start | bytes 3145736 | tf_op jit(solution)/shard_map/ppermute | solution.py:378
  1031.0 102.6 %copy-start.8 = (f32[512,512]{1,0:T(8,128)}, f32[512,512]{1,0:T(8,128)S(1)}, u32[]{:S(2)}) copy-start(f32[512,512]{1,0:T(8,128)S(1)} %collective-permute-done.16.refs_6_) | copy-start | bytes 3145732
  1128.1 84.5 %collective-permute-start.42 = (f32[512,512]{1,0:T(8,128)S(1)}, f32[512,512]{1,0:T(8,128)}, u32[]{:S(2)}, u32[]{:S(2)}) collective-permute-start(f32[512,512]{1,0:T(8,128)S(1)} %select_select_fusion), channel_id=1, source_target_pairs={{8,0},{16,8},{24,16},{9,1},{17,9},{25,17},{10,2},{18,10},{26,18},{... | collective-permute-start | bytes 3145736 | tf_op jit(solution)/shard_map/ppermute | solution.py:410
  1136.2 80.1 %collective-permute-start.41 = (f32[512,512]{1,0:T(8,128)S(1)}, f32[512,512]{1,0:T(8,128)S(1)}, u32[]{:S(2)}, u32[]{:S(2)}) collective-permute-start(f32[512,512]{1,0:T(8,128)S(1)} %select_select_fusion.1), channel_id=1, source_target_pairs={{0,8},{8,16},{16,24},{1,9},{9,17},{17,25},{2,10},{10,18},{18,26},{... | collective-permute-start | bytes 3145736 | tf_op jit(solution)/shard_map/ppermute | solution.py:409
  1144.0 46.1 %collective-permute-start.10 = (f32[512,256]{1,0:T(8,128)S(1)}, f32[512,256]{1,0:T(8,128)S(1)}, u32[]{:S(2)}, u32[]{:S(2)}) collective-permute-start(f32[512,256]{1,0:T(8,128)S(1)} %get-tuple-element.135), channel_id=1, source_target_pairs={{0,4},{1,5},{2,6},{3,7},{4,0},{5,1},{6,2},{7,3},{8,12},{9,13},{10,... | collective-permute-start | bytes 1572872 | tf_op jit(solution)/shard_map/ppermute | solution.py:378
  1144.1 68.5 %collective-permute-start.11 = (f32[512,256]{1,0:T(8,128)S(1)}, f32[512,256]{1,0:T(8,128)S(1)}, u32[]{:S(2)}, u32[]{:S(2)}) collective-permute-start(f32[512,256]{1,0:T(8,128)S(1)} %get-tuple-element.134), channel_id=1, source_target_pairs={{0,5},{1,4},{2,7},{3,6},{4,1},{5,0},{6,3},{7,2},{8,13},{9,12},{10,... | collective-permute-start | bytes 1572872 | tf_op jit(solution)/shard_map/ppermute | solution.py:378
  1146.6 115.0 %collective-permute-start.12 = (f32[512,256]{1,0:T(8,128)}, f32[512,256]{1,0:T(8,128)S(1)}, u32[]{:S(2)}, u32[]{:S(2)}) collective-permute-start(f32[512,256]{1,0:T(8,128)} %get-tuple-element.133), channel_id=1, source_target_pairs={{0,6},{1,7},{2,4},{3,5},{4,2},{5,3},{6,0},{7,1},{8,14},{9,15},{10,... | collective-permute-start | bytes 1572872 | tf_op jit(solution)/shard_map/ppermute | solution.py:378
  1190.1 78.8 %copy-start.14 = (f32[512,256]{1,0:T(8,128)}, f32[512,256]{1,0:T(8,128)S(1)}, u32[]{:S(2)}) copy-start(f32[512,256]{1,0:T(8,128)S(1)} %collective-permute-done.10.refs_7_) | copy-start | bytes 1572868
  1190.1 71.6 %collective-permute-start.13 = (f32[512,256]{1,0:T(8,128)}, f32[512,256]{1,0:T(8,128)S(1)}, u32[]{:S(2)}, u32[]{:S(2)}) collective-permute-start(f32[512,256]{1,0:T(8,128)} %get-tuple-element.132), channel_id=1, source_target_pairs={{0,7},{1,6},{2,5},{3,4},{4,3},{5,2},{6,1},{7,0},{8,15},{9,14},{10,... | collective-permute-start | bytes 1572872 | tf_op jit(solution)/shard_map/ppermute | solution.py:378
  1212.5 56.4 %copy-start.15 = (f32[512,256]{1,0:T(8,128)}, f32[512,256]{1,0:T(8,128)S(1)}, u32[]{:S(2)}) copy-start(f32[512,256]{1,0:T(8,128)S(1)} %collective-permute-done.11.refs_8_) | copy-start | bytes 1572868
  1212.5 50.3 %collective-permute-start.7 = (f32[512,256]{1,0:T(8,128)}, f32[512,256]{1,0:T(8,128)S(1)}, u32[]{:S(2)}, u32[]{:S(2)}) collective-permute-start(f32[512,256]{1,0:T(8,128)} %get-tuple-element.138), channel_id=1, source_target_pairs={{0,1},{1,0},{2,3},{3,2},{4,5},{5,4},{6,7},{7,6},{8,9},{9,8},{10,11... | collective-permute-start | bytes 1572872 | tf_op jit(solution)/shard_map/ppermute | solution.py:378
  1212.6 50.3 %collective-permute-start.8 = (f32[512,256]{1,0:T(8,128)}, f32[512,256]{1,0:T(8,128)}, u32[]{:S(2)}, u32[]{:S(2)}) collective-permute-start(f32[512,256]{1,0:T(8,128)} %get-tuple-element.137), channel_id=1, source_target_pairs={{0,2},{1,3},{2,0},{3,1},{4,6},{5,7},{6,4},{7,5},{8,10},{9,11},{10,... | collective-permute-start | bytes 1572872 | tf_op jit(solution)/shard_map/ppermute | solution.py:378
  1216.3 46.5 %collective-permute-start.9 = (f32[512,256]{1,0:T(8,128)}, f32[512,256]{1,0:T(8,128)}, u32[]{:S(2)}, u32[]{:S(2)}) collective-permute-start(f32[512,256]{1,0:T(8,128)} %get-tuple-element.136), channel_id=1, source_target_pairs={{0,3},{1,2},{2,1},{3,0},{4,7},{5,6},{6,5},{7,4},{8,11},{9,10},{10,... | collective-permute-start | bytes 1572872 | tf_op jit(solution)/shard_map/ppermute | solution.py:378
  1261.6 10.5 collective-permute-start
  1261.7 15.1 %collective-permute-start.1 = (f32[512,256]{1,0:T(8,128)}, f32[512,256]{1,0:T(8,128)S(1)}, u32[]{:S(2)}, u32[]{:S(2)}) collective-permute-start(f32[512,256]{1,0:T(8,128)} %get-tuple-element.145), channel_id=1, source_target_pairs={{0,2},{1,3},{2,0},{3,1},{4,6},{5,7},{6,4},{7,5},{8,10},{9,11},{10,... | collective-permute-start | bytes 1572872 | tf_op jit(solution)/shard_map/ppermute | solution.py:378
  1264.3 15.7 %collective-permute-start.44 = (f32[512,256]{1,0:T(8,128)S(1)}, f32[512,256]{1,0:T(8,128)S(1)}, u32[]{:S(2)}, u32[]{:S(2)}) collective-permute-start(f32[512,256]{1,0:T(8,128)S(1)} %select_select_fusion.8), channel_id=1, source_target_pairs={{8,0},{16,8},{24,16},{9,1},{17,9},{25,17},{10,2},{18,10},{26,18},{... | collective-permute-start | bytes 1572872 | tf_op jit(solution)/shard_map/ppermute | solution.py:410
  1270.3 23.7 %collective-permute-start.43 = (f32[512,256]{1,0:T(8,128)S(1)}, f32[512,256]{1,0:T(8,128)S(1)}, u32[]{:S(2)}, u32[]{:S(2)}) collective-permute-start(f32[512,256]{1,0:T(8,128)S(1)} %select_select_fusion.9), channel_id=1, source_target_pairs={{0,8},{8,16},{16,24},{1,9},{9,17},{17,25},{2,10},{10,18},{18,26},{... | collective-permute-start | bytes 1572872 | tf_op jit(solution)/shard_map/ppermute | solution.py:409
  1271.6 50.8 %collective-permute-start.2 = (f32[512,256]{1,0:T(8,128)}, f32[512,256]{1,0:T(8,128)S(1)}, u32[]{:S(2)}, u32[]{:S(2)}) collective-permute-start(f32[512,256]{1,0:T(8,128)} %get-tuple-element.144), channel_id=1, source_target_pairs={{0,3},{1,2},{2,1},{3,0},{4,7},{5,6},{6,5},{7,4},{8,11},{9,10},{10,... | collective-permute-start | bytes 1572872 | tf_op jit(solution)/shard_map/ppermute | solution.py:378
  1272.1 94.1 %copy-start.12 = (f32[512,256]{1,0:T(8,128)}, f32[512,256]{1,0:T(8,128)S(1)}, u32[]{:S(2)}) copy-start(f32[512,256]{1,0:T(8,128)S(1)} %collective-permute-done.refs_4_) | copy-start | bytes 1572868
  1272.1 50.3 %collective-permute-start.3 = (f32[512,256]{1,0:T(8,128)}, f32[512,256]{1,0:T(8,128)S(1)}, u32[]{:S(2)}, u32[]{:S(2)}) collective-permute-start(f32[512,256]{1,0:T(8,128)} %get-tuple-element.143), channel_id=1, source_target_pairs={{0,4},{1,5},{2,6},{3,7},{4,0},{5,1},{6,2},{7,3},{8,12},{9,13},{10,... | collective-permute-start | bytes 1572872 | tf_op jit(solution)/shard_map/ppermute | solution.py:378
  1276.8 89.5 %copy-start.13 = (f32[512,256]{1,0:T(8,128)}, f32[512,256]{1,0:T(8,128)S(1)}, u32[]{:S(2)}) copy-start(f32[512,256]{1,0:T(8,128)S(1)} %collective-permute-done.1.refs_5_) | copy-start | bytes 1572868
  1276.8 62.7 %collective-permute-start.4 = (f32[512,256]{1,0:T(8,128)}, f32[512,256]{1,0:T(8,128)S(1)}, u32[]{:S(2)}, u32[]{:S(2)}) collective-permute-start(f32[512,256]{1,0:T(8,128)} %get-tuple-element.142), channel_id=1, source_target_pairs={{0,5},{1,4},{2,7},{3,6},{4,1},{5,0},{6,3},{7,2},{8,13},{9,12},{10,... | collective-permute-start | bytes 1572872 | tf_op jit(solution)/shard_map/ppermute | solution.py:378
  1280.0 74.7 %collective-permute-start.5 = (f32[512,256]{1,0:T(8,128)}, f32[512,256]{1,0:T(8,128)S(1)}, u32[]{:S(2)}, u32[]{:S(2)}) collective-permute-start(f32[512,256]{1,0:T(8,128)} %get-tuple-element.141), channel_id=1, source_target_pairs={{0,6},{1,7},{2,4},{3,5},{4,2},{5,3},{6,0},{7,1},{8,14},{9,15},{10,... | collective-permute-start | bytes 1572872 | tf_op jit(solution)/shard_map/ppermute | solution.py:378
  1294.8 71.2 %collective-permute-start.6 = (f32[512,256]{1,0:T(8,128)}, f32[512,256]{1,0:T(8,128)S(1)}, u32[]{:S(2)}, u32[]{:S(2)}) collective-permute-start(f32[512,256]{1,0:T(8,128)} %get-tuple-element.140), channel_id=1, source_target_pairs={{0,7},{1,6},{2,5},{3,4},{4,3},{5,2},{6,1},{7,0},{8,15},{9,14},{10,... | collective-permute-start | bytes 1572872 | tf_op jit(solution)/shard_map/ppermute | solution.py:378
  1322.4 43.9 %copy-start.24 = (f32[512,256]{1,0:T(8,128)S(1)}, f32[512,256]{1,0:T(8,128)}, u32[]{:S(2)}) copy-start(f32[512,256]{1,0:T(8,128)} %get-tuple-element.105) | copy-start | bytes 1572868
  1322.4 44.2 %copy-start.19 = (f32[512,256]{1,0:T(8,128)}, f32[512,256]{1,0:T(8,128)S(1)}, u32[]{:S(2)}) copy-start(f32[512,256]{1,0:T(8,128)S(1)} %collective-permute-done.2.refs_6_) | copy-start | bytes 1572868
  1322.4 44.2 %copy-start.20 = (f32[512,256]{1,0:T(8,128)}, f32[512,256]{1,0:T(8,128)S(1)}, u32[]{:S(2)}) copy-start(f32[512,256]{1,0:T(8,128)S(1)} %collective-permute-done.3.refs_7_) | copy-start | bytes 1572868
  1366.8 16.2 %collective-permute-start.46 = (f32[512,256]{1,0:T(8,128)S(1)}, f32[512,256]{1,0:T(8,128)S(1)}, u32[]{:S(2)}, u32[]{:S(2)}) collective-permute-start(f32[512,256]{1,0:T(8,128)S(1)} %select_select_fusion.6), channel_id=1, source_target_pairs={{8,0},{16,8},{24,16},{9,1},{17,9},{25,17},{10,2},{18,10},{26,18},{... | collective-permute-start | bytes 1572872 | tf_op jit(solution)/shard_map/ppermute | solution.py:410
  1371.6 25.8 %collective-permute-start.45 = (f32[512,256]{1,0:T(8,128)S(1)}, f32[512,256]{1,0:T(8,128)S(1)}, u32[]{:S(2)}, u32[]{:S(2)}) collective-permute-start(f32[512,256]{1,0:T(8,128)S(1)} %select_select_fusion.7), channel_id=1, source_target_pairs={{0,8},{8,16},{16,24},{1,9},{9,17},{17,25},{2,10},{10,18},{18,26},{... | collective-permute-start | bytes 1572872 | tf_op jit(solution)/shard_map/ppermute | solution.py:409
  (24 other events, 225.9 us)
Sparse Core Ops, SparseCore 0:
  363.9 67.3 all-gather.1
  480.3 82.9 all-reduce.9

commit v2 on v1

--- a/solution.py
+++ b/solution.py
@@ -38,100 +38,123 @@
     return along_y + ((c[3] * xp1 + c[4] * xm1) + (c[5] * xp2 + c[6] * xm2))
 
 
-def row_coefficients(coefs):
-    moved = [jnp.roll(c, 2, axis=1) if i in (3, 5) else c for i, c in enumerate(coefs)]
-    return jnp.stack([jnp.repeat(c, SUB, axis=0) for c in moved])
-
-
-def row_step_kernel(me_ref, coef_ref, p_ref, o_ref, *, nx, per_dest, lead, groups):
+def difference_matrix(nx):
+    gap = lax.broadcasted_iota(jnp.int32, (nx, nx), 0) - lax.broadcasted_iota(jnp.int32, (nx, nx), 1)
+    sign = jnp.sign(gap).astype(jnp.float32)
+    near, next_near = jnp.abs(gap) == 1, jnp.abs(gap) == 2
+    slope = jnp.where(near, 8.0 * sign, jnp.where(next_near, -sign, 0.0))
+    around = jnp.where(near, 1.0, jnp.where(gap == 0, KEEP_TENTHS, 0.0))
+    once = jnp.concatenate([slope, around], axis=1)
+    return jnp.concatenate([once, once], axis=0).astype(jnp.bfloat16)
+
+
+KEEP_TENTHS = 6.0
+
+
+def row_step_kernel(
+    me_ref, coef_ref, d_ref, p_ref, o_ref, lhs_ref, ds_ref, s_ref, *, nx, per_dest, lead
+):
     me = me_ref[0]
-    rows = p_ref.shape[0]
+    tall = p_ref.shape[0]
     members = o_ref.shape[0]
     depth = o_ref.shape[2] // nx
-    deep = min(4, depth)
-    zero = jnp.zeros((SUB, nx), jnp.float32)
-
-    def block(step, _):
-        r0 = pl.multiple_of(step * (SUB * groups), SUB * groups)
+    zero = jnp.zeros((tall, nx), jnp.float32)
+
+    def at(k):
+        return slice((k + 2) * tall, (k + 3) * tall)
+
+    def put(k, value):
+        high = value.astype(jnp.bfloat16)
+        lhs_ref[at(k), 0:nx] = high
+        lhs_ref[at(k), nx : 2 * nx] = (value - high.astype(jnp.float32)).astype(jnp.bfloat16)
+
+    def product(k0, k1):
+        rows = slice((k0 + 2) * tall, (k1 + 2) * tall)
+        ds_ref[rows, :] = jnp.dot(
+            lhs_ref[rows, :], d_ref[...], preferred_element_type=jnp.float32
+        )
+
+    def part(dest, low, high):
+        y0 = dest * per_dest + lead
+
+        def outside(k):
+            return (low and k < 0) or (high and k >= depth)
 
         def cols(y):
             start = y * nx
             return pl.ds(start if isinstance(start, int) else pl.multiple_of(start, nx), nx)
 
-        def coefs(y):
-            start = y * SUB
-            start = start if isinstance(start, int) else pl.multiple_of(start, SUB)
-            return [coef_ref[i, pl.ds(start, SUB), :] for i in range(7)]
-
-        def around(c, m2, m1, mid, p1, p2):
-            before = pltpu.roll(mid, 1, 1)
-            along_y = c[0] * p1 + c[1] * m1 + c[2] * (p2 - m2)
-            ahead = pltpu.roll(c[5] * mid + c[3] * before, nx - 2, 1)
-            return along_y + (ahead + (c[4] * before + c[6] * pltpu.roll(before, 1, 1)))
-
-        def part(dest, inner, low, high):
-            y0 = dest * per_dest + lead + inner
-            q = {}
-            for k in range(-4, deep + 4):
-                outside = (low and k < 0) or (high and k >= deep)
-                for g in range(groups):
-                    spot = pl.ds(pl.multiple_of(r0 + SUB * g, SUB), SUB)
-                    q[k, g] = zero if outside else p_ref[spot, cols(y0 + k)]
-            s = {}
-            for k in range(-2, deep + 2):
-                outside = (low and k < 0) or (high and k >= deep)
-                c = None if outside else coefs(y0 + k)
-                for g in range(groups):
-                    s[k, g] = zero if outside else KEEP * q[k, g] + around(
-                        c, *[q[k + j, g] for j in range(-2, 3)]
-                    )
-            slot = jnp.bitwise_xor(jnp.int32(dest), me)
-            for k in range(deep):
-                c = coefs(y0 + k)
-                for g in range(groups):
-                    value = KEEP * s[k, g] + around(c, *[s[k + j, g] for j in range(-2, 3)])
-                    spot = pl.ds(pl.multiple_of(r0 + SUB * g, SUB), SUB)
-                    o_ref[slot, spot, cols(inner + k)] = 0.5 * (q[k, g] + value)
-
-        for inner in range(0, depth, deep):
-            low = lead + inner == 0
-            high = lead + inner + deep == per_dest
-            if low:
-                part(0, inner, True, high and members == 1)
-
-            def one(dest, _):
-                part(dest, inner, False, False)
-                return 0
-
-            lax.fori_loop(int(low), members - int(high), one, 0)
-            if high and not (low and members == 1):
-                part(members - 1, inner, False, True)
+        def q(k):
+            return zero if outside(k) else p_ref[:, cols(y0 + k)]
+
+        def tendency(k, m2, m1, p1, p2):
+            c = [coef_ref[i, pl.ds(y0 + k, 1), :] for i in range(4)]
+            along_y = (c[0] * p1 + c[1] * m1) + c[2] * (p2 - m2)
+            return along_y + (diffusion * ds_ref[at(k), nx : 2 * nx] - c[3] * ds_ref[at(k), 0:nx])
+
+        inside = [k for k in range(-2, depth + 2) if not outside(k)]
+        for k in inside:
+            put(k, q(k))
+        product(inside[0], inside[-1] + 1)
+        for k in range(-2, depth + 2):
+            if outside(k):
+                s_ref[at(k), :] = zero
+                continue
+            value = tendency(k, q(k - 2), q(k - 1), q(k + 1), q(k + 2))
+            s_ref[at(k), :] = value
+            if 0 <= k < depth:
+                put(k, value)
+        product(0, depth)
+        slot = jnp.bitwise_xor(jnp.int32(dest), me)
+        for k in range(depth):
+            value = tendency(
+                k, s_ref[at(k - 2), :], s_ref[at(k - 1), :], s_ref[at(k + 1), :], s_ref[at(k + 2), :]
+            )
+            o_ref[slot, :, k * nx : (k + 1) * nx] = 0.5 * (q(k) + value)
+
+    low, high = lead == 0, lead + depth == per_dest
+    if low:
+        part(0, True, high and members == 1)
+
+    def one(dest, _):
+        part(dest, False, False)
         return 0
 
-    lax.fori_loop(0, rows // (SUB * groups), block, 0)
-
-
-def row_step(cov, table, me, nx, members, lead, depth):
+    lax.fori_loop(int(low), members - int(high), one, 0)
+    if high and not (low and members == 1):
+        part(members - 1, False, True)
+
+
+def row_step(cov, coefs, me, nx, members, lead, depth):
     rows, cells = cov.shape
     per_dest = cells // members // nx
     tall = min(64, rows)
-    groups = 2 if tall % (2 * SUB) == 0 else 1
+    table = jnp.stack(coefs)
+    matrix = difference_matrix(nx)
+    once = pl.Buffered(1)
+    stack = (depth + 4) * tall
     return pl.pallas_call(
-        functools.partial(row_step_kernel, nx=nx, per_dest=per_dest, lead=lead, groups=groups),
+        functools.partial(row_step_kernel, nx=nx, per_dest=per_dest, lead=lead),
         out_shape=jax.ShapeDtypeStruct((members, rows, depth * nx), jnp.float32),
         grid_spec=pltpu.PrefetchScalarGridSpec(
             num_scalar_prefetch=1,
             grid=(rows // tall,),
             in_specs=[
-                pl.BlockSpec(table.shape, lambda i, m: (0, 0, 0), pipeline_mode=pl.Buffered(1)),
+                pl.BlockSpec(table.shape, lambda i, m: (0, 0, 0), pipeline_mode=once),
+                pl.BlockSpec(matrix.shape, lambda i, m: (0, 0), pipeline_mode=once),
                 pl.BlockSpec((tall, cells), lambda i, m: (i, 0)),
             ],
             out_specs=pl.BlockSpec((members, tall, depth * nx), lambda i, m: (0, i, 0)),
+            scratch_shapes=[
+                pltpu.VMEM((stack, 2 * nx), jnp.bfloat16),
+                pltpu.VMEM((stack, 2 * nx), jnp.float32),
+                pltpu.VMEM((stack, nx), jnp.float32),
+            ],
         ),
         compiler_params=pltpu.CompilerParams(vmem_limit_bytes=56 << 20),
         cost_estimate=work(members * rows * depth * nx, 60),
         name="row_step",
-    )(me, table, cov)
+    )(me, table, matrix, cov)
 
 
 def work(elements, flops):
@@ -347,12 +370,12 @@
     coefs = stencil_coefficients(courant_x_field, courant_y_field)
 
     per_dest = zonal // nx
-    table = row_coefficients(coefs)
     shares, slots = plan(per_dest)
     leads = [sum(shares[:i]) for i in range(len(shares))]
     blocks = []
+    row_coefs = coefs[:3] + [courant_x_field / 12.0]
     for lead, depth in zip(leads, shares):
-        blocks.append(row_step(cov_prior, table, me_arg, nx, members, lead, depth))
+        blocks.append(row_step(cov_prior, row_coefs, me_arg, nx, members, lead, depth))
 
     column_coefs = jnp.stack(
         [

time: 1440 us -> 1200 us (0.83)
  Pallas kernels: 526 us -> 284 us
    pallas_call x2, Pallas kernels: 320 us -> 78.3 us  [row_step(): pl.pallas_call(functools.partial(row_step_kernel, nx=nx, per_dest=per_des...]
  transfers between devices with their start and end apart: 49 -> 49, of which waited for: 28 -> 28; matrix products, arithmetic and copies ran while one was open for 10% -> 12% of each run, Pallas kernels for 12% -> 15%
where the time goes in v2:
time: 1200 us; the launch traced here: 1190 us
  waiting for transfers between devices  552 us (46%)
  Pallas kernels  284 us (24%)
  starting transfers between devices  149 us (12%)
  other arithmetic  87.9 us (7%)
  local copies, waits for them, and re-layouts  58.3 us (5%)
  matrix products  39.8 us (3%)
  between operations  15 us (1%)
    ppermute x35, waiting for transfers between devices, local(): got.append(lax.ppermute(blocks[index][s, :, cut], 'row', pairs))  423 us
    pallas_call x6, Pallas kernels, column_step(): pl.pallas_call(functools.partial(column_step_kernel, sources=sources, hal...  206 us
    ppermute x35, starting transfers between devices, local(): got.append(lax.ppermute(blocks[index][s, :, cut], 'row', pairs))  103 us
    pallas_call x2, Pallas kernels, row_step(): pl.pallas_call(functools.partial(row_step_kernel, nx=nx, per_dest=per_des...  78.3 us
    ppermute x5, waiting for transfers between devices, local(): below = lax.ppermute(jnp.concatenate(last, axis=0), 'grp', forward)  52.8 us
    all_gather x1, waiting for transfers between devices, local(): picked = lax.all_gather(picked, 'row', axis=0, tiled=True)  36.8 us
    ppermute x5, starting transfers between devices, local(): above = lax.ppermute(jnp.concatenate(head, axis=0), 'grp', backward)  33.8 us
    dot_general x16, matrix products, pick_columns(): total = total + jnp.dot(array[s], chosen, precision=lax.Precision.HIGH)  29.1 us
  transfers between devices with their start and end apart: 49, of which 28 were waited for; matrix products, arithmetic and copies ran while one was open for 12% of the time, Pallas kernels for 15%

profile of v2, /device:TPU:22, one launch (start us, length us, event | category | flops | bytes accessed | tf_op | source)
XLA Modules:
  0.0 1187.1 jit_solution(14834997330189003145)
XLA Ops:
  9.8 30.4 %row_step.3.refs_3_ = f32[8,512,512]{2,1,0:T(8,128)} custom-call(s32[1]{0:T(128)} %bitcast.me_ref, f32[4,128,128]{2,1,0:T(8,128)} %pad_maximum_fusion.4.coef_ref, bf16[256,256]{1,0:T(8,128)(2,1)} %pad_maximum_fusion.5.d_ref, f32[512,16384]{1,0:T(8,128)} %p_ref.3), custom_call_target="tpu_custom_call" | custom-call | flops 125829120 | bytes 67108864 | tf_op jit(solution)/shard_map/row_step/pallas_call | solution.py:136
  40.2 47.9 %row_step.2.refs_3_ = f32[8,512,1536]{2,1,0:T(8,128)} custom-call(s32[1]{0:T(128)} %bitcast.me_ref, f32[4,128,128]{2,1,0:T(8,128)} %pad_maximum_fusion.4.coef_ref, bf16[256,256]{1,0:T(8,128)(2,1)} %pad_maximum_fusion.5.d_ref, f32[512,16384]{1,0:T(8,128)} %p_ref.3), custom_call_target="tpu_custom_call" | custom-call | flops 377487360 | bytes 201326592 | tf_op jit(solution)/shard_map/row_step/pallas_call | solution.py:136
  97.1 3.1 fusion.3
  103.2 3.1 fusion.5
  118.0 6.1 slice_bitcast_fusion.23
  125.6 3.2 broadcast_dynamic-update-slice_fusion.6
  129.0 3.2 broadcast_dynamic-update-slice_fusion.5
  132.2 3.2 broadcast_dynamic-update-slice_fusion.4
  135.4 3.2 broadcast_dynamic-update-slice_fusion.3
  138.6 3.2 broadcast_dynamic-update-slice_fusion.2
  141.8 3.3 broadcast_dynamic-update-slice_fusion.1
  145.1 3.2 broadcast_dynamic-update-slice_fusion.refs_0_
  148.3 36.8 %all-gather.2.cloned.1.call-done = f32[4096,256]{1,0:T(8,128)} async-done(((f32[512,256]{1,0:T(8,128)}), f32[4096,256]{1,0:T(8,128)}) %all-gather.2.cloned.1.call-update) | async-done | bytes 4194320 | tf_op jit(solution)/shard_map/all_gather | solution.py:406
  187.7 4.6 collective-permute-start.38
  192.3 10.8 collective-permute-done.37
  203.5 4.9 pad_maximum_fusion.1.refs_1_
  208.4 18.5 %column_step.6 = f32[4096,256]{1,0:T(8,128)} custom-call(s32[1]{0:T(128)} %bitcast.me_ref, f32[7,5120,128]{2,1,0:T(8,128)} %broadcast_dynamic-update-slice_fusion.refs_0_, f32[5120,256]{1,0:T(8,128)} %pad_maximum_fusion.1.refs_1_), custom_call_target="tpu_custom_call" | custom-call | flops 104857600 | bytes 33554432 | tf_op jit(solution)/shard_map/column_step/pallas_call | solution.py:305
  226.9 3.2 gather_fusion
  238.6 12.2 %slice_bitcast_fusion.25 = (f32[512,512]{1,0:T(8,128)}, f32[512,512]{1,0:T(8,128)}, f32[512,512]{1,0:T(8,128)}, f32[512,512]{1,0:T(8,128)}, f32[512,512]{1,0:T(8...) fusion(f32[8,512,1536]{2,1,0:T(8,128)} %row_step.2.refs_3_), kind=kLoop, calls=%fused_computation.79 | loop fusion | bytes 33554432 | tf_op jit(solution)/shard_map/squeeze | solution.py:401
  250.8 26.5 %collective-permute-done.30.refs_6_ = f32[512,512]{1,0:T(8,128)S(1)} collective-permute-done((f32[512,512]{1,0:T(8,128)}, f32[512,512]{1,0:T(8,128)S(1)}, u32[]{:S(2)}, u32[]{:S(2)}) %collective-permute-start.30) | collective-permute-done | bytes 1048608 | tf_op jit(solution)/shard_map/ppermute | solution.py:401
  277.3 3.5 collective-permute-done.31.refs_7_
  280.8 70.7 %collective-permute-start.22 = (f32[512,512]{1,0:T(8,128)}, f32[512,512]{1,0:T(8,128)}, u32[]{:S(2)}, u32[]{:S(2)}) collective-permute-start(f32[512,512]{1,0:T(8,128)} %get-tuple-element.121), channel_id=1, source_target_pairs={{0,2},{1,3},{2,0},{3,1},{4,6},{5,7},{6,4},{7,5},{8,10},{9,11},{10,... | collective-permute-start | bytes 3145736 | tf_op jit(solution)/shard_map/ppermute | solution.py:401
  351.5 19.0 %collective-permute-done.32.refs_8_ = f32[512,512]{1,0:T(8,128)} collective-permute-done((f32[512,512]{1,0:T(8,128)}, f32[512,512]{1,0:T(8,128)}, u32[]{:S(2)}, u32[]{:S(2)}) %collective-permute-start.32) | collective-permute-done | bytes 1048608 | tf_op jit(solution)/shard_map/ppermute | solution.py:401
  370.5 3.2 collective-permute-start.23
  373.8 21.3 %collective-permute-done.33.refs_9_ = f32[512,512]{1,0:T(8,128)} collective-permute-done((f32[512,512]{1,0:T(8,128)}, f32[512,512]{1,0:T(8,128)}, u32[]{:S(2)}, u32[]{:S(2)}) %collective-permute-start.33) | collective-permute-done | bytes 1048608 | tf_op jit(solution)/shard_map/ppermute | solution.py:401
  395.0 22.9 %collective-permute-done.34.refs_10_ = f32[512,512]{1,0:T(8,128)} collective-permute-done((f32[512,512]{1,0:T(8,128)}, f32[512,512]{1,0:T(8,128)}, u32[]{:S(2)}, u32[]{:S(2)}) %collective-permute-start.34) | collective-permute-done | bytes 1048608 | tf_op jit(solution)/shard_map/ppermute | solution.py:401
  418.0 3.9 select_select_fusion.5
  423.2 3.9 select_select_fusion.4
  427.1 13.5 %collective-permute-start.36 = (f32[512,512]{1,0:T(8,128)}, f32[512,512]{1,0:T(8,128)}, u32[]{:S(2)}, u32[]{:S(2)}) collective-permute-start(f32[512,512]{1,0:T(8,128)} %select_select_fusion.4), channel_id=1, source_target_pairs={{8,0},{16,8},{24,16},{9,1},{17,9},{25,17},{10,2},{18,10},{26,18},{... | collective-permute-start | bytes 3145736 | tf_op jit(solution)/shard_map/ppermute | solution.py:433
  443.0 11.7 cholesky.44
  456.1 9.8 custom-call.12
  475.1 11.7 cholesky.55
  488.2 9.8 custom-call.13
  513.1 44.2 %column_step.7.refs_13_ = f32[4096,2048]{1,0:T(8,128)} custom-call(s32[1]{0:T(128)} %bitcast.me_ref, f32[7,5120,128]{2,1,0:T(8,128)} %broadcast_dynamic-update-slice_fusion.refs_0_, f32[512,512]{1,0:T(8,128)} %collective-permute-done.35.refs_1_, f32[512,512]{1,0:T(8,128)} %collective-permute-done.36.refs_2_, f32[8,512,512]{2,1,0:T(8,128)} %row_step.3.refs_3_, ...), custom_call_target="tpu_custom_call" | custom-call | flops 209715200 | bytes 67108864 | tf_op jit(solution)/shard_map/column_step/pallas_call | solution.py:305
  557.3 59.3 %collective-permute-done.24.refs_7_ = f32[512,512]{1,0:T(8,128)S(1)} collective-permute-done((f32[512,512]{1,0:T(8,128)S(1)}, f32[512,512]{1,0:T(8,128)S(1)}, u32[]{:S(2)}, u32[]{:S(2)}) %collective-permute-start.24) | collective-permute-done | bytes 1048608 | tf_op jit(solution)/shard_map/ppermute | solution.py:401
  619.0 20.3 %collective-permute-done.25.refs_8_ = f32[512,512]{1,0:T(8,128)} collective-permute-done((f32[512,512]{1,0:T(8,128)}, f32[512,512]{1,0:T(8,128)}, u32[]{:S(2)}, u32[]{:S(2)}) %collective-permute-start.25) | collective-permute-done | bytes 1048608 | tf_op jit(solution)/shard_map/ppermute | solution.py:401
  639.3 23.4 %collective-permute-done.26.refs_9_ = f32[512,512]{1,0:T(8,128)} collective-permute-done((f32[512,512]{1,0:T(8,128)}, f32[512,512]{1,0:T(8,128)}, u32[]{:S(2)}, u32[]{:S(2)}) %collective-permute-start.26) | collective-permute-done | bytes 1048608 | tf_op jit(solution)/shard_map/ppermute | solution.py:401
  662.6 20.5 %collective-permute-done.27.refs_10_ = f32[512,512]{1,0:T(8,128)} collective-permute-done((f32[512,512]{1,0:T(8,128)}, f32[512,512]{1,0:T(8,128)}, u32[]{:S(2)}, u32[]{:S(2)}) %collective-permute-start.27) | collective-permute-done | bytes 1048608 | tf_op jit(solution)/shard_map/ppermute | solution.py:401
  686.2 5.3 collective-permute-start.40
  698.9 15.1 %collective-permute-done.40.refs_2_ = f32[512,512]{1,0:T(8,128)} collective-permute-done((f32[512,512]{1,0:T(8,128)S(1)}, f32[512,512]{1,0:T(8,128)}, u32[]{:S(2)}, u32[]{:S(2)}) %collective-permute-start.40) | collective-permute-done | bytes 1048608 | tf_op jit(solution)/shard_map/ppermute | solution.py:433
  715.4 24.3 %collective-permute-done.39.refs_1_ = f32[512,512]{1,0:T(8,128)} collective-permute-done((f32[512,512]{1,0:T(8,128)S(1)}, f32[512,512]{1,0:T(8,128)}, u32[]{:S(2)}, u32[]{:S(2)}) %collective-permute-start.39) | collective-permute-done | bytes 1048608 | tf_op jit(solution)/shard_map/ppermute | solution.py:432
  740.8 44.3 %column_step.8.refs_13_ = f32[4096,2048]{1,0:T(8,128)} custom-call(s32[1]{0:T(128)} %bitcast.me_ref, f32[7,5120,128]{2,1,0:T(8,128)} %broadcast_dynamic-update-slice_fusion.refs_0_, f32[512,512]{1,0:T(8,128)} %collective-permute-done.39.refs_1_, f32[512,512]{1,0:T(8,128)} %collective-permute-done.40.refs_2_, ...), custom_call_target="tpu_custom_call", output_to_operand_aliasing={{}: (14, {})} | custom-call | flops 209715200 | bytes 67108864 | tf_op jit(solution)/shard_map/column_step/pallas_call | solution.py:305
  785.1 27.6 %collective-permute-done.17.refs_7_ = f32[512,512]{1,0:T(8,128)} collective-permute-done((f32[512,512]{1,0:T(8,128)}, f32[512,512]{1,0:T(8,128)}, u32[]{:S(2)}, u32[]{:S(2)}) %collective-permute-start.17) | collective-permute-done | bytes 1048608 | tf_op jit(solution)/shard_map/ppermute | solution.py:401
  812.7 22.5 %collective-permute-done.18.refs_8_ = f32[512,512]{1,0:T(8,128)} collective-permute-done((f32[512,512]{1,0:T(8,128)}, f32[512,512]{1,0:T(8,128)}, u32[]{:S(2)}, u32[]{:S(2)}) %collective-permute-start.18) | collective-permute-done | bytes 1048608 | tf_op jit(solution)/shard_map/ppermute | solution.py:401
  835.2 23.6 %collective-permute-done.19.refs_9_ = f32[512,512]{1,0:T(8,128)} collective-permute-done((f32[512,512]{1,0:T(8,128)}, f32[512,512]{1,0:T(8,128)}, u32[]{:S(2)}, u32[]{:S(2)}) %collective-permute-start.19) | collective-permute-done | bytes 1048608 | tf_op jit(solution)/shard_map/ppermute | solution.py:401
  858.8 20.6 %collective-permute-done.20.refs_10_ = f32[512,512]{1,0:T(8,128)} collective-permute-done((f32[512,512]{1,0:T(8,128)}, f32[512,512]{1,0:T(8,128)}, u32[]{:S(2)}, u32[]{:S(2)}) %collective-permute-start.20) | collective-permute-done | bytes 1048608 | tf_op jit(solution)/shard_map/ppermute | solution.py:401
  882.1 5.5 collective-permute-start.42
  891.5 6.5 slice_bitcast_fusion.42
  902.4 41.8 %collective-permute-done.10.refs_7_ = f32[512,256]{1,0:T(8,128)S(1)} collective-permute-done((f32[512,256]{1,0:T(8,128)S(1)}, f32[512,256]{1,0:T(8,128)S(1)}, u32[]{:S(2)}, u32[]{:S(2)}) %collective-permute-start.10) | collective-permute-done | bytes 524320 | tf_op jit(solution)/shard_map/ppermute | solution.py:401
  944.5 22.1 %collective-permute-done.11.refs_8_ = f32[512,256]{1,0:T(8,128)S(1)} collective-permute-done((f32[512,256]{1,0:T(8,128)S(1)}, f32[512,256]{1,0:T(8,128)S(1)}, u32[]{:S(2)}, u32[]{:S(2)}) %collective-permute-start.11) | collective-permute-done | bytes 524320 | tf_op jit(solution)/shard_map/ppermute | solution.py:401
  966.6 3.8 collective-permute-start.8
  971.4 44.2 %column_step.9.refs_13_ = f32[4096,2048]{1,0:T(8,128)} custom-call(s32[1]{0:T(128)} %bitcast.me_ref, f32[7,5120,128]{2,1,0:T(8,128)} %broadcast_dynamic-update-slice_fusion.refs_0_, f32[512,512]{1,0:T(8,128)} %copy-done.27, f32[512,512]{1,0:T(8,128)} %collective-permute-done.42.refs_2_, ...), custom_call_target="tpu_custom_call", output_to_operand_aliasing={{}: (14, {})} | custom-call | flops 209715200 | bytes 67108864 | tf_op jit(solution)/shard_map/column_step/pallas_call | solution.py:305
  1018.4 4.6 collective-permute-start.44
  1026.4 4.4 collective-permute-done.1.refs_5_
  1030.8 3.2 collective-permute-done.44.refs_2_
  1034.1 14.0 %collective-permute-done.43.refs_1_ = f32[512,256]{1,0:T(8,128)S(1)} collective-permute-done((f32[512,256]{1,0:T(8,128)S(1)}, f32[512,256]{1,0:T(8,128)S(1)}, u32[]{:S(2)}, u32[]{:S(2)}) %collective-permute-start.43) | collective-permute-done | bytes 524320 | tf_op jit(solution)/shard_map/ppermute | solution.py:432
  1048.9 27.4 %column_step.10.refs_13_ = f32[4096,2048]{1,0:T(8,128)} custom-call(s32[1]{0:T(128)} %bitcast.me_ref, f32[7,5120,128]{2,1,0:T(8,128)} %broadcast_dynamic-update-slice_fusion.refs_0_, f32[512,256]{1,0:T(8,128)} %copy-done.30, f32[512,256]{1,0:T(8,128)} %copy-done.29, f32[8,512,1536]{2,1,0:T(8,128)} %row_step.2.refs_3_, ...), custom_call_target="tpu_custom_call", output_to_operand_aliasing={{}: (14, {})} | custom-call | flops 104857600 | bytes 33554432 | tf_op jit(solution)/shard_map/column_step/pallas_call | solution.py:305
  1076.3 17.2 %collective-permute-done.4.refs_8_ = f32[512,256]{1,0:T(8,128)S(1)} collective-permute-done((f32[512,256]{1,0:T(8,128)}, f32[512,256]{1,0:T(8,128)S(1)}, u32[]{:S(2)}, u32[]{:S(2)}) %collective-permute-start.4) | collective-permute-done | bytes 524320 | tf_op jit(solution)/shard_map/ppermute | solution.py:401
  1093.5 15.3 %collective-permute-done.5.refs_9_ = f32[512,256]{1,0:T(8,128)S(1)} collective-permute-done((f32[512,256]{1,0:T(8,128)}, f32[512,256]{1,0:T(8,128)S(1)}, u32[]{:S(2)}, u32[]{:S(2)}) %collective-permute-start.5) | collective-permute-done | bytes 524320 | tf_op jit(solution)/shard_map/ppermute | solution.py:401
  1108.8 11.2 collective-permute-done.6.refs_10_
  1120.8 4.9 collective-permute-start.46
  1127.0 10.1 collective-permute-done.46.refs_2_
  1137.1 14.4 %collective-permute-done.45.refs_1_ = f32[512,256]{1,0:T(8,128)S(1)} collective-permute-done((f32[512,256]{1,0:T(8,128)S(1)}, f32[512,256]{1,0:T(8,128)S(1)}, u32[]{:S(2)}, u32[]{:S(2)}) %collective-permute-start.45) | collective-permute-done | bytes 524320 | tf_op jit(solution)/shard_map/ppermute | solution.py:432
  1152.4 27.4 %column_step.11 = f32[4096,2048]{1,0:T(8,128)} custom-call(s32[1]{0:T(128)} %bitcast.me_ref, f32[7,5120,128]{2,1,0:T(8,128)} %broadcast_dynamic-update-slice_fusion.refs_0_, f32[512,256]{1,0:T(8,128)} %copy-done.32, f32[512,256]{1,0:T(8,128)} %copy-done.31, f32[8,512,1536]{2,1,0:T(8,128)} %row_step.2.refs_3_, ...), custom_call_target="tpu_custom_call", output_to_operand_aliasing={{}: (14, {})} | custom-call | flops 104857600 | bytes 33554432 | tf_op jit(solution)/shard_map/column_step/pallas_call | solution.py:305
  (236 shorter events, 107.4 us)
Async XLA Ops:
  6.5 178.6 %all-gather.2.cloned.1.call-start = ((), (), s32[]{:S(2)}) async-start(), calls=%async_computation | async-start | bytes 4718592 | tf_op jit(solution)/shard_map/all_gather | solution.py:406
  40.2 48.0 %copy-start.34 = (s32[2,128]{1,0:T(2,128)S(1)}, s32[2,128]{1,0:T(2,128)}, u32[]{:S(2)}) copy-start(s32[2,128]{1,0:T(2,128)} %param.15) | copy-start | bytes 3076
  117.6 323.1 %all-reduce.10.cloned.1.call-start = ((), (), s32[]{:S(2)}) async-start(), calls=%async_computation.1 | async-start | bytes 4718592 | tf_op jit(solution)/shard_map/psum | solution.py:421
  124.1 111.7 %collective-permute-start.28 = (f32[512,512]{1,0:T(8,128)}, f32[512,512]{1,0:T(8,128)S(1)}, u32[]{:S(2)}, u32[]{:S(2)}) collective-permute-start(f32[512,512]{1,0:T(8,128)} %get-tuple-element.148), channel_id=1, source_target_pairs={{0,1},{1,0},{2,3},{3,2},{4,5},{5,4},{6,7},{7,6},{8,9},{9,8},{10,11... | collective-permute-start | bytes 3145736 | tf_op jit(solution)/shard_map/ppermute | solution.py:401
  124.1 113.2 %collective-permute-start.29 = (f32[512,512]{1,0:T(8,128)}, f32[512,512]{1,0:T(8,128)S(1)}, u32[]{:S(2)}, u32[]{:S(2)}) collective-permute-start(f32[512,512]{1,0:T(8,128)} %get-tuple-element.154), channel_id=1, source_target_pairs={{0,2},{1,3},{2,0},{3,1},{4,6},{5,7},{6,4},{7,5},{8,10},{9,11},{10,... | collective-permute-start | bytes 3145736 | tf_op jit(solution)/shard_map/ppermute | solution.py:401
  186.4 16.7 %collective-permute-start.37 = (f32[512,256]{1,0:T(8,128)S(1)}, f32[512,256]{1,0:T(8,128)S(1)}, u32[]{:S(2)}, u32[]{:S(2)}) collective-permute-start(f32[512,256]{1,0:T(8,128)S(1)} %get-tuple-element.157), channel_id=1, source_target_pairs={{0,8},{8,16},{16,24},{1,9},{9,17},{17,25},{2,10},{10,18},{18,26},{... | collective-permute-start | bytes 1572872 | tf_op jit(solution)/shard_map/ppermute | solution.py:407
  187.7 15.8 %collective-permute-start.38 = (f32[512,256]{1,0:T(8,128)S(1)}, f32[512,256]{1,0:T(8,128)S(1)}, u32[]{:S(2)}, u32[]{:S(2)}) collective-permute-start(f32[512,256]{1,0:T(8,128)S(1)} %get-tuple-element.158), channel_id=1, source_target_pairs={{8,0},{16,8},{24,16},{9,1},{17,9},{25,17},{10,2},{18,10},{26,18},{... | collective-permute-start | bytes 1572872 | tf_op jit(solution)/shard_map/ppermute | solution.py:408
  234.0 43.3 %collective-permute-start.30 = (f32[512,512]{1,0:T(8,128)}, f32[512,512]{1,0:T(8,128)S(1)}, u32[]{:S(2)}, u32[]{:S(2)}) collective-permute-start(f32[512,512]{1,0:T(8,128)} %get-tuple-element.153), channel_id=1, source_target_pairs={{0,3},{1,2},{2,1},{3,0},{4,7},{5,6},{6,5},{7,4},{8,11},{9,10},{10,... | collective-permute-start | bytes 3145736 | tf_op jit(solution)/shard_map/ppermute | solution.py:401
  234.1 46.8 %collective-permute-start.31 = (f32[512,512]{1,0:T(8,128)}, f32[512,512]{1,0:T(8,128)}, u32[]{:S(2)}, u32[]{:S(2)}) collective-permute-start(f32[512,512]{1,0:T(8,128)} %get-tuple-element.152), channel_id=1, source_target_pairs={{0,4},{1,5},{2,6},{3,7},{4,0},{5,1},{6,2},{7,3},{8,12},{9,13},{10,... | collective-permute-start | bytes 3145736 | tf_op jit(solution)/shard_map/ppermute | solution.py:401
  234.7 135.9 %collective-permute-start.32 = (f32[512,512]{1,0:T(8,128)}, f32[512,512]{1,0:T(8,128)}, u32[]{:S(2)}, u32[]{:S(2)}) collective-permute-start(f32[512,512]{1,0:T(8,128)} %get-tuple-element.151), channel_id=1, source_target_pairs={{0,5},{1,4},{2,7},{3,6},{4,1},{5,0},{6,3},{7,2},{8,13},{9,12},{10,... | collective-permute-start | bytes 3145736 | tf_op jit(solution)/shard_map/ppermute | solution.py:401
  235.7 187.5 %copy-start.3 = (f32[512,512]{1,0:T(8,128)}, f32[512,512]{1,0:T(8,128)S(1)}, u32[]{:S(2)}) copy-start(f32[512,512]{1,0:T(8,128)S(1)} %collective-permute-done.28.refs_4_) | copy-start | bytes 3145732
  235.7 159.3 %collective-permute-start.33 = (f32[512,512]{1,0:T(8,128)}, f32[512,512]{1,0:T(8,128)}, u32[]{:S(2)}, u32[]{:S(2)}) collective-permute-start(f32[512,512]{1,0:T(8,128)} %get-tuple-element.150), channel_id=1, source_target_pairs={{0,6},{1,7},{2,4},{3,5},{4,2},{5,3},{6,0},{7,1},{8,14},{9,15},{10,... | collective-permute-start | bytes 3145736 | tf_op jit(solution)/shard_map/ppermute | solution.py:401
  237.3 185.9 %copy-start.4 = (f32[512,512]{1,0:T(8,128)}, f32[512,512]{1,0:T(8,128)S(1)}, u32[]{:S(2)}) copy-start(f32[512,512]{1,0:T(8,128)S(1)} %collective-permute-done.29.refs_5_) | copy-start | bytes 3145732
  237.3 180.7 %collective-permute-start.34 = (f32[512,512]{1,0:T(8,128)}, f32[512,512]{1,0:T(8,128)}, u32[]{:S(2)}, u32[]{:S(2)}) collective-permute-start(f32[512,512]{1,0:T(8,128)} %get-tuple-element.149), channel_id=1, source_target_pairs={{0,7},{1,6},{2,5},{3,4},{4,3},{5,2},{6,1},{7,0},{8,15},{9,14},{10,... | collective-permute-start | bytes 3145736 | tf_op jit(solution)/shard_map/ppermute | solution.py:401
  277.3 145.9 %copy-start.5 = (f32[512,512]{1,0:T(8,128)}, f32[512,512]{1,0:T(8,128)S(1)}, u32[]{:S(2)}) copy-start(f32[512,512]{1,0:T(8,128)S(1)} %collective-permute-done.30.refs_6_) | copy-start | bytes 3145732
  277.3 225.5 %collective-permute-start.21 = (f32[512,512]{1,0:T(8,128)}, f32[512,512]{1,0:T(8,128)}, u32[]{:S(2)}, u32[]{:S(2)}) collective-permute-start(f32[512,512]{1,0:T(8,128)} %get-tuple-element.122), channel_id=1, source_target_pairs={{0,1},{1,0},{2,3},{3,2},{4,5},{5,4},{6,7},{7,6},{8,9},{9,8},{10,11... | collective-permute-start | bytes 3145736 | tf_op jit(solution)/shard_map/ppermute | solution.py:401
  280.8 222.4 %collective-permute-start.22 = (f32[512,512]{1,0:T(8,128)}, f32[512,512]{1,0:T(8,128)}, u32[]{:S(2)}, u32[]{:S(2)}) collective-permute-start(f32[512,512]{1,0:T(8,128)} %get-tuple-element.121), channel_id=1, source_target_pairs={{0,2},{1,3},{2,0},{3,1},{4,6},{5,7},{6,4},{7,5},{8,10},{9,11},{10,... | collective-permute-start | bytes 3145736 | tf_op jit(solution)/shard_map/ppermute | solution.py:401
  370.5 186.7 %collective-permute-start.23 = (f32[512,512]{1,0:T(8,128)}, f32[512,512]{1,0:T(8,128)}, u32[]{:S(2)}, u32[]{:S(2)}) collective-permute-start(f32[512,512]{1,0:T(8,128)} %get-tuple-element.120), channel_id=1, source_target_pairs={{0,3},{1,2},{2,1},{3,0},{4,7},{5,6},{6,5},{7,4},{8,11},{9,10},{10,... | collective-permute-start | bytes 3145736 | tf_op jit(solution)/shard_map/ppermute | solution.py:401
  421.9 83.2 %collective-permute-start.35 = (f32[512,512]{1,0:T(8,128)}, f32[512,512]{1,0:T(8,128)}, u32[]{:S(2)}, u32[]{:S(2)}) collective-permute-start(f32[512,512]{1,0:T(8,128)} %select_select_fusion.5), channel_id=1, source_target_pairs={{0,8},{8,16},{16,24},{1,9},{9,17},{17,25},{2,10},{10,18},{18,26},{... | collective-permute-start | bytes 3145736 | tf_op jit(solution)/shard_map/ppermute | solution.py:432
  427.1 78.5 %collective-permute-start.36 = (f32[512,512]{1,0:T(8,128)}, f32[512,512]{1,0:T(8,128)}, u32[]{:S(2)}, u32[]{:S(2)}) collective-permute-start(f32[512,512]{1,0:T(8,128)} %select_select_fusion.4), channel_id=1, source_target_pairs={{8,0},{16,8},{24,16},{9,1},{17,9},{25,17},{10,2},{18,10},{26,18},{... | collective-permute-start | bytes 3145736 | tf_op jit(solution)/shard_map/ppermute | solution.py:433
  503.2 113.4 %collective-permute-start.24 = (f32[512,512]{1,0:T(8,128)S(1)}, f32[512,512]{1,0:T(8,128)S(1)}, u32[]{:S(2)}, u32[]{:S(2)}) collective-permute-start(f32[512,512]{1,0:T(8,128)S(1)} %copy-done.28), channel_id=1, source_target_pairs={{0,4},{1,5},{2,6},{3,7},{4,0},{5,1},{6,2},{7,3},{8,12},{9,13},{10,... | collective-permute-start | bytes 3145736 | tf_op jit(solution)/shard_map/ppermute | solution.py:401
  503.2 136.0 %collective-permute-start.25 = (f32[512,512]{1,0:T(8,128)}, f32[512,512]{1,0:T(8,128)}, u32[]{:S(2)}, u32[]{:S(2)}) collective-permute-start(f32[512,512]{1,0:T(8,128)} %get-tuple-element.118), channel_id=1, source_target_pairs={{0,5},{1,4},{2,7},{3,6},{4,1},{5,0},{6,3},{7,2},{8,13},{9,12},{10,... | collective-permute-start | bytes 3145736 | tf_op jit(solution)/shard_map/ppermute | solution.py:401
  505.1 157.5 %collective-permute-start.26 = (f32[512,512]{1,0:T(8,128)}, f32[512,512]{1,0:T(8,128)}, u32[]{:S(2)}, u32[]{:S(2)}) collective-permute-start(f32[512,512]{1,0:T(8,128)} %get-tuple-element.117), channel_id=1, source_target_pairs={{0,6},{1,7},{2,4},{3,5},{4,2},{5,3},{6,0},{7,1},{8,14},{9,15},{10,... | collective-permute-start | bytes 3145736 | tf_op jit(solution)/shard_map/ppermute | solution.py:401
  505.6 177.6 %collective-permute-start.27 = (f32[512,512]{1,0:T(8,128)}, f32[512,512]{1,0:T(8,128)}, u32[]{:S(2)}, u32[]{:S(2)}) collective-permute-start(f32[512,512]{1,0:T(8,128)} %get-tuple-element.116), channel_id=1, source_target_pairs={{0,7},{1,6},{2,5},{3,4},{4,3},{5,2},{6,1},{7,0},{8,15},{9,14},{10,... | collective-permute-start | bytes 3145736 | tf_op jit(solution)/shard_map/ppermute | solution.py:401
  557.3 138.5 %collective-permute-start.14 = (f32[512,512]{1,0:T(8,128)}, f32[512,512]{1,0:T(8,128)S(1)}, u32[]{:S(2)}, u32[]{:S(2)}) collective-permute-start(f32[512,512]{1,0:T(8,128)} %get-tuple-element.130), channel_id=1, source_target_pairs={{0,1},{1,0},{2,3},{3,2},{4,5},{5,4},{6,7},{7,6},{8,9},{9,8},{10,11... | collective-permute-start | bytes 3145736 | tf_op jit(solution)/shard_map/ppermute | solution.py:401
  616.6 74.9 %copy-start.9 = (f32[512,512]{1,0:T(8,128)}, f32[512,512]{1,0:T(8,128)S(1)}, u32[]{:S(2)}) copy-start(f32[512,512]{1,0:T(8,128)S(1)} %collective-permute-done.24.refs_7_) | copy-start | bytes 3145732
  616.6 82.2 %collective-permute-start.15 = (f32[512,512]{1,0:T(8,128)}, f32[512,512]{1,0:T(8,128)S(1)}, u32[]{:S(2)}, u32[]{:S(2)}) collective-permute-start(f32[512,512]{1,0:T(8,128)} %get-tuple-element.129), channel_id=1, source_target_pairs={{0,2},{1,3},{2,0},{3,1},{4,6},{5,7},{6,4},{7,5},{8,10},{9,11},{10,... | collective-permute-start | bytes 3145736 | tf_op jit(solution)/shard_map/ppermute | solution.py:401
  686.2 27.8 %collective-permute-start.40 = (f32[512,512]{1,0:T(8,128)S(1)}, f32[512,512]{1,0:T(8,128)}, u32[]{:S(2)}, u32[]{:S(2)}) collective-permute-start(f32[512,512]{1,0:T(8,128)S(1)} %select_select_fusion.2), channel_id=1, source_target_pairs={{8,0},{16,8},{24,16},{9,1},{17,9},{25,17},{10,2},{18,10},{26,18},{... | collective-permute-start | bytes 3145736 | tf_op jit(solution)/shard_map/ppermute | solution.py:433
  694.4 45.3 %collective-permute-start.39 = (f32[512,512]{1,0:T(8,128)S(1)}, f32[512,512]{1,0:T(8,128)}, u32[]{:S(2)}, u32[]{:S(2)}) collective-permute-start(f32[512,512]{1,0:T(8,128)S(1)} %select_select_fusion.3), channel_id=1, source_target_pairs={{0,8},{8,16},{16,24},{1,9},{9,17},{17,25},{2,10},{10,18},{18,26},{... | collective-permute-start | bytes 3145736 | tf_op jit(solution)/shard_map/ppermute | solution.py:432
  695.7 89.4 %collective-permute-start.16 = (f32[512,512]{1,0:T(8,128)}, f32[512,512]{1,0:T(8,128)S(1)}, u32[]{:S(2)}, u32[]{:S(2)}) collective-permute-start(f32[512,512]{1,0:T(8,128)} %get-tuple-element.128), channel_id=1, source_target_pairs={{0,3},{1,2},{2,1},{3,0},{4,7},{5,6},{6,5},{7,4},{8,11},{9,10},{10,... | collective-permute-start | bytes 3145736 | tf_op jit(solution)/shard_map/ppermute | solution.py:401
  695.8 191.8 %copy-start.6 = (f32[512,512]{1,0:T(8,128)}, f32[512,512]{1,0:T(8,128)S(1)}, u32[]{:S(2)}) copy-start(f32[512,512]{1,0:T(8,128)S(1)} %collective-permute-done.14.refs_4_) | copy-start | bytes 3145732
  695.8 116.9 %collective-permute-start.17 = (f32[512,512]{1,0:T(8,128)}, f32[512,512]{1,0:T(8,128)}, u32[]{:S(2)}, u32[]{:S(2)}) collective-permute-start(f32[512,512]{1,0:T(8,128)} %get-tuple-element.127), channel_id=1, source_target_pairs={{0,4},{1,5},{2,6},{3,7},{4,0},{5,1},{6,2},{7,3},{8,12},{9,13},{10,... | collective-permute-start | bytes 3145736 | tf_op jit(solution)/shard_map/ppermute | solution.py:401
  698.9 188.7 %copy-start.7 = (f32[512,512]{1,0:T(8,128)}, f32[512,512]{1,0:T(8,128)S(1)}, u32[]{:S(2)}) copy-start(f32[512,512]{1,0:T(8,128)S(1)} %collective-permute-done.15.refs_5_) | copy-start | bytes 3145732
  698.9 136.3 %collective-permute-start.18 = (f32[512,512]{1,0:T(8,128)}, f32[512,512]{1,0:T(8,128)}, u32[]{:S(2)}, u32[]{:S(2)}) collective-permute-start(f32[512,512]{1,0:T(8,128)} %get-tuple-element.126), channel_id=1, source_target_pairs={{0,5},{1,4},{2,7},{3,6},{4,1},{5,0},{6,3},{7,2},{8,13},{9,12},{10,... | collective-permute-start | bytes 3145736 | tf_op jit(solution)/shard_map/ppermute | solution.py:401
  714.0 144.8 %collective-permute-start.19 = (f32[512,512]{1,0:T(8,128)}, f32[512,512]{1,0:T(8,128)}, u32[]{:S(2)}, u32[]{:S(2)}) collective-permute-start(f32[512,512]{1,0:T(8,128)} %get-tuple-element.125), channel_id=1, source_target_pairs={{0,6},{1,7},{2,4},{3,5},{4,2},{5,3},{6,0},{7,1},{8,14},{9,15},{10,... | collective-permute-start | bytes 3145736 | tf_op jit(solution)/shard_map/ppermute | solution.py:401
  739.7 139.7 %collective-permute-start.20 = (f32[512,512]{1,0:T(8,128)}, f32[512,512]{1,0:T(8,128)}, u32[]{:S(2)}, u32[]{:S(2)}) collective-permute-start(f32[512,512]{1,0:T(8,128)} %get-tuple-element.124), channel_id=1, source_target_pairs={{0,7},{1,6},{2,5},{3,4},{4,3},{5,2},{6,1},{7,0},{8,15},{9,14},{10,... | collective-permute-start | bytes 3145736 | tf_op jit(solution)/shard_map/ppermute | solution.py:401
  785.1 102.5 %copy-start.8 = (f32[512,512]{1,0:T(8,128)}, f32[512,512]{1,0:T(8,128)S(1)}, u32[]{:S(2)}) copy-start(f32[512,512]{1,0:T(8,128)S(1)} %collective-permute-done.16.refs_6_) | copy-start | bytes 3145732
  882.1 84.5 %collective-permute-start.42 = (f32[512,512]{1,0:T(8,128)S(1)}, f32[512,512]{1,0:T(8,128)}, u32[]{:S(2)}, u32[]{:S(2)}) collective-permute-start(f32[512,512]{1,0:T(8,128)S(1)} %select_select_fusion), channel_id=1, source_target_pairs={{8,0},{16,8},{24,16},{9,1},{17,9},{25,17},{10,2},{18,10},{26,18},{... | collective-permute-start | bytes 3145736 | tf_op jit(solution)/shard_map/ppermute | solution.py:433
  890.2 80.2 %collective-permute-start.41 = (f32[512,512]{1,0:T(8,128)S(1)}, f32[512,512]{1,0:T(8,128)S(1)}, u32[]{:S(2)}, u32[]{:S(2)}) collective-permute-start(f32[512,512]{1,0:T(8,128)S(1)} %select_select_fusion.1), channel_id=1, source_target_pairs={{0,8},{8,16},{16,24},{1,9},{9,17},{17,25},{2,10},{10,18},{18,26},{... | collective-permute-start | bytes 3145736 | tf_op jit(solution)/shard_map/ppermute | solution.py:432
  898.0 46.1 %collective-permute-start.10 = (f32[512,256]{1,0:T(8,128)S(1)}, f32[512,256]{1,0:T(8,128)S(1)}, u32[]{:S(2)}, u32[]{:S(2)}) collective-permute-start(f32[512,256]{1,0:T(8,128)S(1)} %get-tuple-element.135), channel_id=1, source_target_pairs={{0,4},{1,5},{2,6},{3,7},{4,0},{5,1},{6,2},{7,3},{8,12},{9,13},{10,... | collective-permute-start | bytes 1572872 | tf_op jit(solution)/shard_map/ppermute | solution.py:401
  898.1 68.5 %collective-permute-start.11 = (f32[512,256]{1,0:T(8,128)S(1)}, f32[512,256]{1,0:T(8,128)S(1)}, u32[]{:S(2)}, u32[]{:S(2)}) collective-permute-start(f32[512,256]{1,0:T(8,128)S(1)} %get-tuple-element.134), channel_id=1, source_target_pairs={{0,5},{1,4},{2,7},{3,6},{4,1},{5,0},{6,3},{7,2},{8,13},{9,12},{10,... | collective-permute-start | bytes 1572872 | tf_op jit(solution)/shard_map/ppermute | solution.py:401
  900.6 115.0 %collective-permute-start.12 = (f32[512,256]{1,0:T(8,128)}, f32[512,256]{1,0:T(8,128)S(1)}, u32[]{:S(2)}, u32[]{:S(2)}) collective-permute-start(f32[512,256]{1,0:T(8,128)} %get-tuple-element.133), channel_id=1, source_target_pairs={{0,6},{1,7},{2,4},{3,5},{4,2},{5,3},{6,0},{7,1},{8,14},{9,15},{10,... | collective-permute-start | bytes 1572872 | tf_op jit(solution)/shard_map/ppermute | solution.py:401
  944.1 78.8 %copy-start.14 = (f32[512,256]{1,0:T(8,128)}, f32[512,256]{1,0:T(8,128)S(1)}, u32[]{:S(2)}) copy-start(f32[512,256]{1,0:T(8,128)S(1)} %collective-permute-done.10.refs_7_) | copy-start | bytes 1572868
  944.1 71.6 %collective-permute-start.13 = (f32[512,256]{1,0:T(8,128)}, f32[512,256]{1,0:T(8,128)S(1)}, u32[]{:S(2)}, u32[]{:S(2)}) collective-permute-start(f32[512,256]{1,0:T(8,128)} %get-tuple-element.132), channel_id=1, source_target_pairs={{0,7},{1,6},{2,5},{3,4},{4,3},{5,2},{6,1},{7,0},{8,15},{9,14},{10,... | collective-permute-start | bytes 1572872 | tf_op jit(solution)/shard_map/ppermute | solution.py:401
  966.6 56.4 %copy-start.15 = (f32[512,256]{1,0:T(8,128)}, f32[512,256]{1,0:T(8,128)S(1)}, u32[]{:S(2)}) copy-start(f32[512,256]{1,0:T(8,128)S(1)} %collective-permute-done.11.refs_8_) | copy-start | bytes 1572868
  966.6 50.3 %collective-permute-start.7 = (f32[512,256]{1,0:T(8,128)}, f32[512,256]{1,0:T(8,128)S(1)}, u32[]{:S(2)}, u32[]{:S(2)}) collective-permute-start(f32[512,256]{1,0:T(8,128)} %get-tuple-element.138), channel_id=1, source_target_pairs={{0,1},{1,0},{2,3},{3,2},{4,5},{5,4},{6,7},{7,6},{8,9},{9,8},{10,11... | collective-permute-start | bytes 1572872 | tf_op jit(solution)/shard_map/ppermute | solution.py:401
  966.6 50.3 %collective-permute-start.8 = (f32[512,256]{1,0:T(8,128)}, f32[512,256]{1,0:T(8,128)}, u32[]{:S(2)}, u32[]{:S(2)}) collective-permute-start(f32[512,256]{1,0:T(8,128)} %get-tuple-element.137), channel_id=1, source_target_pairs={{0,2},{1,3},{2,0},{3,1},{4,6},{5,7},{6,4},{7,5},{8,10},{9,11},{10,... | collective-permute-start | bytes 1572872 | tf_op jit(solution)/shard_map/ppermute | solution.py:401
  970.4 46.5 %collective-permute-start.9 = (f32[512,256]{1,0:T(8,128)}, f32[512,256]{1,0:T(8,128)}, u32[]{:S(2)}, u32[]{:S(2)}) collective-permute-start(f32[512,256]{1,0:T(8,128)} %get-tuple-element.136), channel_id=1, source_target_pairs={{0,3},{1,2},{2,1},{3,0},{4,7},{5,6},{6,5},{7,4},{8,11},{9,10},{10,... | collective-permute-start | bytes 1572872 | tf_op jit(solution)/shard_map/ppermute | solution.py:401
  1015.6 10.5 collective-permute-start
  1015.7 15.1 %collective-permute-start.1 = (f32[512,256]{1,0:T(8,128)}, f32[512,256]{1,0:T(8,128)S(1)}, u32[]{:S(2)}, u32[]{:S(2)}) collective-permute-start(f32[512,256]{1,0:T(8,128)} %get-tuple-element.145), channel_id=1, source_target_pairs={{0,2},{1,3},{2,0},{3,1},{4,6},{5,7},{6,4},{7,5},{8,10},{9,11},{10,... | collective-permute-start | bytes 1572872 | tf_op jit(solution)/shard_map/ppermute | solution.py:401
  1018.4 15.7 %collective-permute-start.44 = (f32[512,256]{1,0:T(8,128)S(1)}, f32[512,256]{1,0:T(8,128)S(1)}, u32[]{:S(2)}, u32[]{:S(2)}) collective-permute-start(f32[512,256]{1,0:T(8,128)S(1)} %select_select_fusion.8), channel_id=1, source_target_pairs={{8,0},{16,8},{24,16},{9,1},{17,9},{25,17},{10,2},{18,10},{26,18},{... | collective-permute-start | bytes 1572872 | tf_op jit(solution)/shard_map/ppermute | solution.py:433
  1024.3 23.8 %collective-permute-start.43 = (f32[512,256]{1,0:T(8,128)S(1)}, f32[512,256]{1,0:T(8,128)S(1)}, u32[]{:S(2)}, u32[]{:S(2)}) collective-permute-start(f32[512,256]{1,0:T(8,128)S(1)} %select_select_fusion.9), channel_id=1, source_target_pairs={{0,8},{8,16},{16,24},{1,9},{9,17},{17,25},{2,10},{10,18},{18,26},{... | collective-permute-start | bytes 1572872 | tf_op jit(solution)/shard_map/ppermute | solution.py:432
  1025.6 50.7 %collective-permute-start.2 = (f32[512,256]{1,0:T(8,128)}, f32[512,256]{1,0:T(8,128)S(1)}, u32[]{:S(2)}, u32[]{:S(2)}) collective-permute-start(f32[512,256]{1,0:T(8,128)} %get-tuple-element.144), channel_id=1, source_target_pairs={{0,3},{1,2},{2,1},{3,0},{4,7},{5,6},{6,5},{7,4},{8,11},{9,10},{10,... | collective-permute-start | bytes 1572872 | tf_op jit(solution)/shard_map/ppermute | solution.py:401
  1026.1 94.1 %copy-start.12 = (f32[512,256]{1,0:T(8,128)}, f32[512,256]{1,0:T(8,128)S(1)}, u32[]{:S(2)}) copy-start(f32[512,256]{1,0:T(8,128)S(1)} %collective-permute-done.refs_4_) | copy-start | bytes 1572868
  1026.1 50.2 %collective-permute-start.3 = (f32[512,256]{1,0:T(8,128)}, f32[512,256]{1,0:T(8,128)S(1)}, u32[]{:S(2)}, u32[]{:S(2)}) collective-permute-start(f32[512,256]{1,0:T(8,128)} %get-tuple-element.143), channel_id=1, source_target_pairs={{0,4},{1,5},{2,6},{3,7},{4,0},{5,1},{6,2},{7,3},{8,12},{9,13},{10,... | collective-permute-start | bytes 1572872 | tf_op jit(solution)/shard_map/ppermute | solution.py:401
  1030.8 89.5 %copy-start.13 = (f32[512,256]{1,0:T(8,128)}, f32[512,256]{1,0:T(8,128)S(1)}, u32[]{:S(2)}) copy-start(f32[512,256]{1,0:T(8,128)S(1)} %collective-permute-done.1.refs_5_) | copy-start | bytes 1572868
  1030.8 62.7 %collective-permute-start.4 = (f32[512,256]{1,0:T(8,128)}, f32[512,256]{1,0:T(8,128)S(1)}, u32[]{:S(2)}, u32[]{:S(2)}) collective-permute-start(f32[512,256]{1,0:T(8,128)} %get-tuple-element.142), channel_id=1, source_target_pairs={{0,5},{1,4},{2,7},{3,6},{4,1},{5,0},{6,3},{7,2},{8,13},{9,12},{10,... | collective-permute-start | bytes 1572872 | tf_op jit(solution)/shard_map/ppermute | solution.py:401
  1034.0 74.7 %collective-permute-start.5 = (f32[512,256]{1,0:T(8,128)}, f32[512,256]{1,0:T(8,128)S(1)}, u32[]{:S(2)}, u32[]{:S(2)}) collective-permute-start(f32[512,256]{1,0:T(8,128)} %get-tuple-element.141), channel_id=1, source_target_pairs={{0,6},{1,7},{2,4},{3,5},{4,2},{5,3},{6,0},{7,1},{8,14},{9,15},{10,... | collective-permute-start | bytes 1572872 | tf_op jit(solution)/shard_map/ppermute | solution.py:401
  1048.9 71.1 %collective-permute-start.6 = (f32[512,256]{1,0:T(8,128)}, f32[512,256]{1,0:T(8,128)S(1)}, u32[]{:S(2)}, u32[]{:S(2)}) collective-permute-start(f32[512,256]{1,0:T(8,128)} %get-tuple-element.140), channel_id=1, source_target_pairs={{0,7},{1,6},{2,5},{3,4},{4,3},{5,2},{6,1},{7,0},{8,15},{9,14},{10,... | collective-permute-start | bytes 1572872 | tf_op jit(solution)/shard_map/ppermute | solution.py:401
  1076.3 44.0 %copy-start.24 = (f32[512,256]{1,0:T(8,128)S(1)}, f32[512,256]{1,0:T(8,128)}, u32[]{:S(2)}) copy-start(f32[512,256]{1,0:T(8,128)} %get-tuple-element.105) | copy-start | bytes 1572868
  1076.3 44.3 %copy-start.19 = (f32[512,256]{1,0:T(8,128)}, f32[512,256]{1,0:T(8,128)S(1)}, u32[]{:S(2)}) copy-start(f32[512,256]{1,0:T(8,128)S(1)} %collective-permute-done.2.refs_6_) | copy-start | bytes 1572868
  1076.3 44.3 %copy-start.20 = (f32[512,256]{1,0:T(8,128)}, f32[512,256]{1,0:T(8,128)S(1)}, u32[]{:S(2)}) copy-start(f32[512,256]{1,0:T(8,128)S(1)} %collective-permute-done.3.refs_7_) | copy-start | bytes 1572868
  1120.8 16.3 %collective-permute-start.46 = (f32[512,256]{1,0:T(8,128)S(1)}, f32[512,256]{1,0:T(8,128)S(1)}, u32[]{:S(2)}, u32[]{:S(2)}) collective-permute-start(f32[512,256]{1,0:T(8,128)S(1)} %select_select_fusion.6), channel_id=1, source_target_pairs={{8,0},{16,8},{24,16},{9,1},{17,9},{25,17},{10,2},{18,10},{26,18},{... | collective-permute-start | bytes 1572872 | tf_op jit(solution)/shard_map/ppermute | solution.py:433
  1125.7 25.8 %collective-permute-start.45 = (f32[512,256]{1,0:T(8,128)S(1)}, f32[512,256]{1,0:T(8,128)S(1)}, u32[]{:S(2)}, u32[]{:S(2)}) collective-permute-start(f32[512,256]{1,0:T(8,128)S(1)} %select_select_fusion.7), channel_id=1, source_target_pairs={{0,8},{8,16},{16,24},{1,9},{9,17},{17,25},{2,10},{10,18},{18,26},{... | collective-permute-start | bytes 1572872 | tf_op jit(solution)/shard_map/ppermute | solution.py:432
  (24 other events, 229.7 us)
Sparse Core Ops, SparseCore 0:
  117.7 67.3 all-gather.1
  234.1 82.9 all-reduce.9

commit v3 on v2

--- a/solution.py
+++ b/solution.py
@@ -15,27 +15,7 @@
 EXACT = lax.Precision.HIGHEST
 
 
-def stencil_coefficients(u, v):
-    nx = u.shape[1]
-    x = lax.broadcasted_iota(jnp.int32, u.shape, 1)
-    u12, v12 = u / 12.0, v / 12.0
-    return [
-        diffusion - 8.0 * v12,
-        diffusion + 8.0 * v12,
-        v12,
-        jnp.where(x < nx - 1, diffusion - 8.0 * u12, 0.0),
-        jnp.where(x >= 1, diffusion + 8.0 * u12, 0.0),
-        jnp.where(x < nx - 2, u12, 0.0),
-        jnp.where(x >= 2, -u12, 0.0),
-    ]
-
-
 KEEP = 1.0 - 4.0 * diffusion
-
-
-def neighbours(c, ym2, ym1, yp1, yp2, xp1, xm1, xp2, xm2):
-    along_y = c[0] * yp1 + c[1] * ym1 + c[2] * (yp2 - ym2)
-    return along_y + ((c[3] * xp1 + c[4] * xm1) + (c[5] * xp2 + c[6] * xm2))
 
 
 def difference_matrix(nx):
@@ -190,26 +170,24 @@
     o_ref, q_ref, s_ref = refs
     me = me_ref[0]
     tiles = o_ref.shape[1] // LANES
-    border = jnp.zeros((FRONT, LANES), jnp.float32)
-    span = (grid_rows + 4 * REACH) * nx
+    stride = nx + SUB
+    border = jnp.zeros((SUB, LANES), jnp.float32)
     for t in range(tiles):
         for ref in (q_ref, s_ref):
-            ref[t, 0:FRONT, :] = border
-            ref[t, FRONT + span : FRONT + span + SUB, :] = border
+            for y in range(grid_rows + 4 * REACH + 1):
+                ref[t, y * stride : y * stride + SUB, :] = border
 
     for ref, (kind, at) in zip(own, sources):
         tall = ref.shape[0]
-        if kind == "partner":
-            start = FRONT + halo + jnp.bitwise_xor(me, at) * tall
-        else:
-            start = FRONT + at
-        start = pl.multiple_of(start, SUB)
+        start = halo + jnp.bitwise_xor(me, at) * tall if kind == "partner" else at
         piece = min(64, tall)
 
         def copy(i, _):
             r = pl.multiple_of(i * piece, piece)
+            cell = start + r
+            to = pl.multiple_of(FRONT + cell + (cell // nx) * SUB, SUB)
             for t in range(tiles):
-                q_ref[t, pl.ds(start + r, piece), :] = ref[
+                q_ref[t, pl.ds(to, piece), :] = ref[
                     pl.ds(r, piece), t * LANES : (t + 1) * LANES
                 ]
             return 0
@@ -221,24 +199,21 @@
             base = FRONT + xg * SUB
 
             def at(y, shift=0):
-                rows = y * nx + base
-                if shift == 0:
-                    rows = pl.multiple_of(rows, SUB)
-                else:
-                    rows = rows + shift
+                rows = y * stride + base
+                rows = pl.multiple_of(rows, SUB) if shift == 0 else rows + shift
                 return [src[t, pl.ds(rows, SUB), :] for t in range(tiles)]
 
             def step(y, win):
                 far = at(y + 2)
                 xp1, xm1, xp2, xm2 = at(y, 1), at(y, -1), at(y, 2), at(y, -2)
                 spot = pl.multiple_of(y * nx + xg * SUB, SUB)
-                c = [coef_ref[i, pl.ds(spot, SUB), :] for i in range(7)]
+                u, v = coef_ref[0, pl.ds(spot, SUB), :], coef_ref[1, pl.ds(spot, SUB), :]
+                u8, v8 = 8.0 * u, 8.0 * v
+                c = (diffusion - v8, diffusion + v8, v, diffusion - u8, diffusion + u8, u)
                 for t in range(tiles):
-                    value = neighbours(
-                        c, win[0][t], win[1][t], win[3][t], far[t],
-                        xp1[t], xm1[t], xp2[t], xm2[t],
-                    )
-                    emit(t, spot, KEEP * win[2][t] + value)
+                    along_y = c[0] * win[3][t] + c[1] * win[1][t] + c[2] * (far[t] - win[0][t])
+                    along_x = c[3] * xp1[t] + c[4] * xm1[t] + c[5] * (xp2[t] - xm2[t])
+                    emit(t, y, xg, KEEP * win[2][t] + (along_y + along_x))
                 return win[1:] + [far]
 
             def several(i, win):
@@ -252,15 +227,33 @@
 
         lax.fori_loop(0, nx // SUB, strip, 0)
 
-    def emit_first(t, spot, value):
-        s_ref[t, pl.ds(spot + FRONT, SUB), :] = value
-
-    def emit_last(t, spot, value):
-        row = pl.multiple_of(spot - 2 * REACH * nx, SUB)
-        mid = q_ref[t, pl.ds(pl.multiple_of(spot + FRONT, SUB), SUB), :]
+    def cell_at(y, xg):
+        return pl.ds(pl.multiple_of(y * stride + FRONT + xg * SUB, SUB), SUB)
+
+    def emit_first(t, y, xg, value):
+        s_ref[t, cell_at(y, xg), :] = value
+
+    def emit_last(t, y, xg, value):
+        row = pl.multiple_of((y - 2 * REACH) * nx + xg * SUB, SUB)
+        mid = q_ref[t, cell_at(y, xg), :]
         o_ref[pl.ds(row, SUB), t * LANES : (t + 1) * LANES] = 0.5 * (mid + value)
 
     sweep(q_ref, REACH, grid_rows + 2 * REACH, emit_first)
+
+    def clear(y0):
+        nothing = jnp.zeros((nx, LANES), jnp.float32)
+        for t in range(tiles):
+            for y in (y0, y0 + 1):
+                s_ref[t, y * stride + FRONT : y * stride + FRONT + nx, :] = nothing
+
+    @pl.when(me_ref[1] == 1)
+    def _():
+        clear(REACH)
+
+    @pl.when(me_ref[2] == 1)
+    def _():
+        clear(grid_rows + 2 * REACH)
+
     sweep(s_ref, 2 * REACH, grid_rows, emit_last)
 
     if update:
@@ -300,7 +293,7 @@
         specs.append(pl.BlockSpec(memory_space=pl.ANY))
         args.append(into)
         aliases = {len(args): 0}
-    span = (grid_rows + 4 * REACH) * nx + FRONT + SUB
+    span = (grid_rows + 4 * REACH) * (nx + SUB) + SUB
     scratch = pltpu.VMEM((tile // LANES, span, LANES), jnp.float32)
     return pl.pallas_call(
         functools.partial(
@@ -366,14 +359,15 @@
     grid_rows = local_rows // nx
     halo = 2 * REACH * nx
     me, group = lax.axis_index("row"), lax.axis_index("grp")
-    me_arg = me.reshape(1).astype(jnp.int32)
-    coefs = stencil_coefficients(courant_x_field, courant_y_field)
+    ends = (group == 0).astype(jnp.int32), (group == clusters - 1).astype(jnp.int32)
+    me_arg = jnp.stack([me.astype(jnp.int32), *ends])
 
     per_dest = zonal // nx
     shares, slots = plan(per_dest)
     leads = [sum(shares[:i]) for i in range(len(shares))]
     blocks = []
-    row_coefs = coefs[:3] + [courant_x_field / 12.0]
+    v12 = courant_y_field / 12.0
+    row_coefs = [diffusion - 8.0 * v12, diffusion + 8.0 * v12, v12, courant_x_field / 12.0]
     for lead, depth in zip(leads, shares):
         blocks.append(row_step(cov_prior, row_coefs, me_arg, nx, members, lead, depth))
 
@@ -381,12 +375,12 @@
         [
             jnp.broadcast_to(
                 lax.dynamic_slice_in_dim(
-                    jnp.pad(c, ((2 * REACH, 2 * REACH), (0, 0))),
+                    jnp.pad(c / 12.0, ((2 * REACH, 2 * REACH), (0, 0))),
                     group * grid_rows, grid_rows + 4 * REACH, 0,
                 ).reshape(-1)[:, None],
                 (local_rows + 2 * halo, LANES),
             )
-            for c in coefs
+            for c in (courant_x_field, courant_y_field)
         ]
     )
 
@@ -422,15 +416,26 @@
     gains = gains_of(columns, mine.T, inner, obs_var)
 
     edge = halo // rows
-    result = None
-    for k, (index, start, take) in enumerate(slots):
-        got = received[k]
-        if result is not None:
-            got, result = lax.optimization_barrier((got, result))
+
+    def edges(got):
         last = [lax.select_n(jnp.bitwise_xor(me, members - edge + i), *got) for i in range(edge)]
         head = [lax.select_n(jnp.bitwise_xor(me, i), *got) for i in range(edge)]
-        below = lax.ppermute(jnp.concatenate(last, axis=0), "grp", forward)
-        above = lax.ppermute(jnp.concatenate(head, axis=0), "grp", backward)
+        return jnp.concatenate(last, axis=0), jnp.concatenate(head, axis=0)
+
+    def around(last, head):
+        return lax.ppermute(last, "grp", forward), lax.ppermute(head, "grp", backward)
+
+    result = None
+    later = around(*edges(received[0]))
+    for k, (index, start, take) in enumerate(slots):
+        got, (below, above) = received[k], later
+        if k + 1 < len(slots):
+            if result is None:
+                received[k + 1], gains = lax.optimization_barrier((received[k + 1], gains))
+            else:
+                received[k + 1], result = lax.optimization_barrier((received[k + 1], result))
+            below, pair = lax.optimization_barrier((below, edges(received[k + 1])))
+            later = around(*pair)
         parts = [below, above, blocks[index]] + got[1:]
         sources = [("fixed", 0), ("fixed", halo + local_rows), ("partner", 0)]
         sources += [("partner", s) for s in range(1, members)]

time: 1200 us -> 1120 us (0.933)
  the two profiles are of different devices: /device:TPU:22 before, /device:TPU:9 now
where the time goes in v3:
time: 1120 us; the launch traced here: 1110 us
  waiting for transfers between devices  528 us (47%)
  Pallas kernels  268 us (24%)
  starting transfers between devices  112 us (10%)
  other arithmetic  110 us (10%)
  local copies, waits for them, and re-layouts  39.2 us (4%)
  matrix products  38.8 us (3%)
  between operations  14.9 us (1%)
    ppermute x35, waiting for transfers between devices, local(): got.append(lax.ppermute(blocks[index][s, :, cut], 'row', pairs))  436 us
    pallas_call x6, Pallas kernels, column_step(): pl.pallas_call(functools.partial(column_step_kernel, sources=sources, hal...  188 us
    ppermute x35, starting transfers between devices, local(): got.append(lax.ppermute(blocks[index][s, :, cut], 'row', pairs))  80.3 us
    pallas_call x2, Pallas kernels, row_step(): pl.pallas_call(functools.partial(row_step_kernel, nx=nx, per_dest=per_des...  79.8 us
    all_gather x1, waiting for transfers between devices, local(): picked = lax.all_gather(picked, 'row', axis=0, tiled=True)  60.7 us
    dot_general x16, matrix products, pick_columns(): total = total + jnp.dot(array[s], chosen, precision=lax.Precision.HIGH)  29.1 us
    squeeze x3, local copies, waits for them, and re-layouts, local(): got.append(lax.ppermute(blocks[index][s, :, cut], 'row', pairs))  25.4 us
    another operation x6, other arithmetic, solve(): factor = jnp.linalg.cholesky(system)  24.8 us
  transfers between devices with their start and end apart: 49, of which 20 were waited for; matrix products, arithmetic and copies ran while one was open for 14% of the time, Pallas kernels for 15%

profile of v3, /device:TPU:9, one launch (start us, length us, event | category | flops | bytes accessed | tf_op | source)
XLA Modules:
  0.0 1110.4 jit_solution(10020485588423477861)
XLA Ops:
  10.4 31.1 %row_step.2.refs_3_ = f32[8,512,512]{2,1,0:T(8,128)} custom-call(s32[3]{0:T(128)} %pad_add_fusion.me_ref, f32[4,128,128]{2,1,0:T(8,128)} %pad_maximum_fusion.5.coef_ref, bf16[256,256]{1,0:T(8,128)(2,1)} %pad_maximum_fusion.6.d_ref, f32[512,16384]{1,0:T(8,128)} %p_ref.3), custom_call_target="tpu_custom_call" | custom-call | flops 125829120 | bytes 67108864 | tf_op jit(solution)/shard_map/row_step/pallas_call | solution.py:116
  41.5 48.7 %row_step.3.refs_3_ = f32[8,512,1536]{2,1,0:T(8,128)} custom-call(s32[3]{0:T(128)} %pad_add_fusion.me_ref, f32[4,128,128]{2,1,0:T(8,128)} %pad_maximum_fusion.5.coef_ref, bf16[256,256]{1,0:T(8,128)(2,1)} %pad_maximum_fusion.6.d_ref, f32[512,16384]{1,0:T(8,128)} %p_ref.3), custom_call_target="tpu_custom_call" | custom-call | flops 377487360 | bytes 201326592 | tf_op jit(solution)/shard_map/row_step/pallas_call | solution.py:116
  93.2 3.0 fusion.8
  99.2 3.1 fusion.3
  102.3 3.0 fusion.4
  105.3 3.1 fusion.5
  120.0 6.1 slice_bitcast_fusion.39
  126.9 60.7 %all-gather.2.cloned.1.call-done = f32[4096,256]{1,0:T(8,128)} async-done(((f32[512,256]{1,0:T(8,128)}), f32[4096,256]{1,0:T(8,128)}) %all-gather.2.cloned.1.call-update) | async-done | bytes 4194320 | tf_op jit(solution)/shard_map/all_gather | solution.py:400
  188.9 3.1 collective-permute-start.15
  194.8 3.0 pad_maximum_fusion.1.refs_0_
  197.8 5.2 collective-permute-done.15
  202.9 13.2 %collective-permute-done.16 = f32[512,256]{1,0:T(8,128)S(1)} collective-permute-done((f32[512,256]{1,0:T(8,128)S(1)}, f32[512,256]{1,0:T(8,128)S(1)}, u32[]{:S(2)}, u32[]{:S(2)}) %collective-permute-start.16) | collective-permute-done | bytes 524320 | tf_op jit(solution)/shard_map/ppermute | solution.py:402
  218.8 15.5 %column_step.6 = f32[4096,256]{1,0:T(8,128)} custom-call(s32[3]{0:T(128)} %pad_add_fusion.me_ref, f32[2,5120,128]{2,1,0:T(8,128)} %pad_maximum_fusion.1.refs_0_, f32[5120,256]{1,0:T(8,128)} %pad_maximum_fusion.2.refs_1_), custom_call_target="tpu_custom_call" | custom-call | flops 104857600 | bytes 33554432 | tf_op jit(solution)/shard_map/column_step/pallas_call | solution.py:298
  234.3 3.2 gather_fusion
  238.3 3.0 dynamic-slice_select_fusion
  241.5 3.5 collective-permute-start.3
  247.0 12.5 %slice_bitcast_fusion.16 = (f32[512,512]{1,0:T(8,128)}, f32[512,512]{1,0:T(8,128)}, f32[512,512]{1,0:T(8,128)}, f32[512,512]{1,0:T(8,128)}, f32[512,512]{1,0:T(8...) fusion(f32[8,512,1536]{2,1,0:T(8,128)} %row_step.3.refs_3_), kind=kLoop, calls=%fused_computation.64 | loop fusion | bytes 33554432 | tf_op jit(solution)/shard_map/squeeze | solution.py:395
  259.6 26.0 %collective-permute-done.2.refs_6_ = f32[512,512]{1,0:T(8,128)S(1)} collective-permute-done((f32[512,512]{1,0:T(8,128)}, f32[512,512]{1,0:T(8,128)S(1)}, u32[]{:S(2)}, u32[]{:S(2)}) %collective-permute-start.2) | collective-permute-done | bytes 1048608 | tf_op jit(solution)/shard_map/ppermute | solution.py:395
  287.9 70.3 %collective-permute-done.3.refs_7_ = f32[512,512]{1,0:T(8,128)} collective-permute-done((f32[512,512]{1,0:T(8,128)}, f32[512,512]{1,0:T(8,128)}, u32[]{:S(2)}, u32[]{:S(2)}) %collective-permute-start.3) | collective-permute-done | bytes 1048608 | tf_op jit(solution)/shard_map/ppermute | solution.py:395
  361.0 42.1 %collective-permute-done.4.refs_8_ = f32[512,512]{1,0:T(8,128)} collective-permute-done((f32[512,512]{1,0:T(8,128)}, f32[512,512]{1,0:T(8,128)}, u32[]{:S(2)}, u32[]{:S(2)}) %collective-permute-start.4) | collective-permute-done | bytes 1048608 | tf_op jit(solution)/shard_map/ppermute | solution.py:395
  403.1 3.4 collective-permute-start.12
  406.5 87.1 %collective-permute-done.5.refs_9_ = f32[512,512]{1,0:T(8,128)} collective-permute-done((f32[512,512]{1,0:T(8,128)}, f32[512,512]{1,0:T(8,128)}, u32[]{:S(2)}, u32[]{:S(2)}) %collective-permute-start.5) | collective-permute-done | bytes 1048608 | tf_op jit(solution)/shard_map/ppermute | solution.py:395
  494.9 21.1 %collective-permute-done.6.refs_10_ = f32[512,512]{1,0:T(8,128)} collective-permute-done((f32[512,512]{1,0:T(8,128)}, f32[512,512]{1,0:T(8,128)}, u32[]{:S(2)}, u32[]{:S(2)}) %collective-permute-start.6) | collective-permute-done | bytes 1048608 | tf_op jit(solution)/shard_map/ppermute | solution.py:395
  518.0 3.9 select_select_fusion.5
  521.9 3.9 select_select_fusion.2
  528.0 11.7 %cholesky.44 = f32[128,128]{1,0:T(8,128)S(1)} custom-call(f32[128,128]{1,0:T(8,128)S(1)} %copy.13), custom_call_target="Cholesky" | custom-call | tf_op jit(solution)/shard_map/jit(cholesky)/cholesky | solution.py:325
  541.0 9.8 custom-call.12
  554.9 3.3 convolution_negate_fusion
  558.7 11.7 %cholesky.55 = f32[128,128]{1,0:T(8,128)S(1)} custom-call(f32[128,128]{1,0:T(8,128)S(1)} %copy.19), custom_call_target="Cholesky" | custom-call | tf_op jit(solution)/shard_map/jit(cholesky)/cholesky | solution.py:325
  570.5 3.8 fusion.12
  574.3 4.9 reduce-precision_convert_fusion
  580.5 9.8 custom-call.13
  590.4 7.0 pad_maximum_fusion.refs_11_
  602.8 3.1 collective-permute-done.14.refs_10_
  606.0 3.5 collective-permute-start.7
  611.0 10.7 collective-permute-done.9.refs_5_
  623.7 4.7 collective-permute-start.22
  628.5 3.9 select_select_fusion.3
  632.3 53.1 %collective-permute-done.19.refs_5_ = f32[512,512]{1,0:T(8,128)S(1)} collective-permute-done((f32[512,512]{1,0:T(8,128)S(1)}, f32[512,512]{1,0:T(8,128)S(1)}, u32[]{:S(2)}, u32[]{:S(2)}) %collective-permute-start.19) | collective-permute-done | bytes 1048608 | tf_op jit(solution)/shard_map/ppermute | solution.py:395
  686.7 21.2 %collective-permute-done.20.refs_6_ = f32[512,512]{1,0:T(8,128)S(1)} collective-permute-done((f32[512,512]{1,0:T(8,128)S(1)}, f32[512,512]{1,0:T(8,128)S(1)}, u32[]{:S(2)}, u32[]{:S(2)}) %collective-permute-start.20) | collective-permute-done | bytes 1048608 | tf_op jit(solution)/shard_map/ppermute | solution.py:395
  711.5 3.9 select_select_fusion.4
  716.3 5.0 collective-permute-start.17
  721.4 6.8 slice_bitcast_fusion.42
  728.2 30.2 %collective-permute-start.27 = (f32[512,256]{1,0:T(8,128)}, f32[512,256]{1,0:T(8,128)S(1)}, u32[]{:S(2)}, u32[]{:S(2)}) collective-permute-start(f32[512,256]{1,0:T(8,128)} %get-tuple-element.156), channel_id=1, source_target_pairs={{0,1},{1,0},{2,3},{3,2},{4,5},{5,4},{6,7},{7,6},{8,9},{9,8},{10,11... | collective-permute-start | bytes 1572872 | tf_op jit(solution)/shard_map/ppermute | solution.py:395
  759.4 4.6 collective-permute-start.28
  764.0 41.3 %column_step.7.refs_13_ = f32[4096,2048]{1,0:T(8,128)} custom-call(s32[3]{0:T(128)} %pad_add_fusion.me_ref, f32[2,5120,128]{2,1,0:T(8,128)} %pad_maximum_fusion.1.refs_0_, f32[512,512]{1,0:T(8,128)} %copy-done.27, f32[512,512]{1,0:T(8,128)} %copy-done.29, f32[8,512,512]{2,1,0:T(8,128)} %row_step.2.refs_3_, f32[512,512]{1,0:T(8,128)} %copy-done.1, ...), custom_call_target="tpu_custom_call" | custom-call | flops 209715200 | bytes 67108864 | tf_op jit(solution)/shard_map/column_step/pallas_call | solution.py:298
  807.2 3.6 select_select_fusion
  813.9 3.3 select_select_fusion.1
  817.2 8.6 collective-permute-done.29.refs_6_
  825.8 4.1 collective-permute-start.26
  831.1 30.4 %collective-permute-done.31.refs_8_ = f32[512,256]{1,0:T(8,128)} collective-permute-done((f32[512,256]{1,0:T(8,128)S(1)}, f32[512,256]{1,0:T(8,128)}, u32[]{:S(2)}, u32[]{:S(2)}) %collective-permute-start.31) | collective-permute-done | bytes 524320 | tf_op jit(solution)/shard_map/ppermute | solution.py:395
  861.5 4.6 collective-permute-start.33
  866.1 20.8 %collective-permute-done.32.refs_9_ = f32[512,256]{1,0:T(8,128)} collective-permute-done((f32[512,256]{1,0:T(8,128)S(1)}, f32[512,256]{1,0:T(8,128)}, u32[]{:S(2)}, u32[]{:S(2)}) %collective-permute-start.32) | collective-permute-done | bytes 524320 | tf_op jit(solution)/shard_map/ppermute | solution.py:395
  890.5 41.4 %column_step.8.refs_13_ = f32[4096,2048]{1,0:T(8,128)} custom-call(s32[3]{0:T(128)} %pad_add_fusion.me_ref, f32[2,5120,128]{2,1,0:T(8,128)} %pad_maximum_fusion.1.refs_0_, f32[512,512]{1,0:T(8,128)} %collective-permute-done.17.refs_1_, f32[512,512]{1,0:T(8,128)} %copy-done.28, f32[8,512,1536]{2,1,0:T(8,128)} %row_step.3.refs_3_, ...), custom_call_target="tpu_custom_call", output_to_operand_aliasing={{}: (14, {})} | custom-call | flops 209715200 | bytes 67108864 | tf_op jit(solution)/shard_map/column_step/pallas_call | solution.py:298
  942.9 41.5 %column_step.9.refs_13_ = f32[4096,2048]{1,0:T(8,128)} custom-call(s32[3]{0:T(128)} %pad_add_fusion.me_ref, f32[2,5120,128]{2,1,0:T(8,128)} %pad_maximum_fusion.1.refs_0_, f32[512,512]{1,0:T(8,128)} %collective-permute-done.26.refs_1_, f32[512,512]{1,0:T(8,128)} %collective-permute-done.43.refs_2_, ...), custom_call_target="tpu_custom_call", output_to_operand_aliasing={{}: (14, {})} | custom-call | flops 209715200 | bytes 67108864 | tf_op jit(solution)/shard_map/column_step/pallas_call | solution.py:298
  984.4 17.1 %collective-permute-done.40.refs_8_ = f32[512,256]{1,0:T(8,128)S(1)} collective-permute-done((f32[512,256]{1,0:T(8,128)}, f32[512,256]{1,0:T(8,128)S(1)}, u32[]{:S(2)}, u32[]{:S(2)}) %collective-permute-start.40) | collective-permute-done | bytes 524320 | tf_op jit(solution)/shard_map/ppermute | solution.py:395
  1001.5 12.7 %collective-permute-done.41.refs_9_ = f32[512,256]{1,0:T(8,128)} collective-permute-done((f32[512,256]{1,0:T(8,128)}, f32[512,256]{1,0:T(8,128)}, u32[]{:S(2)}, u32[]{:S(2)}) %collective-permute-start.41) | collective-permute-done | bytes 524320 | tf_op jit(solution)/shard_map/ppermute | solution.py:395
  1014.2 11.7 %collective-permute-done.42.refs_10_ = f32[512,256]{1,0:T(8,128)} collective-permute-done((f32[512,256]{1,0:T(8,128)}, f32[512,256]{1,0:T(8,128)}, u32[]{:S(2)}, u32[]{:S(2)}) %collective-permute-start.42) | collective-permute-done | bytes 524320 | tf_op jit(solution)/shard_map/ppermute | solution.py:395
  1025.9 3.1 collective-permute-start.35
  1034.6 6.0 collective-permute-done.35.refs_1_
  1040.6 4.1 collective-permute-start.44
  1046.0 6.8 collective-permute-done.46.refs_2_
  1052.9 24.3 %column_step.10.refs_13_ = f32[4096,2048]{1,0:T(8,128)} custom-call(s32[3]{0:T(128)} %pad_add_fusion.me_ref, f32[2,5120,128]{2,1,0:T(8,128)} %pad_maximum_fusion.1.refs_0_, f32[512,256]{1,0:T(8,128)} %copy-done.38, f32[512,256]{1,0:T(8,128)} %collective-permute-done.46.refs_2_, f32[8,512,1536]{2,1,0:T(8,128)} %row_step.3.refs_3_, ...), custom_call_target="tpu_custom_call", output_to_operand_aliasing={{}: (14, {})} | custom-call | flops 104857600 | bytes 33554432 | tf_op jit(solution)/shard_map/column_step/pallas_call | solution.py:298
  1078.8 24.3 %column_step.11 = f32[4096,2048]{1,0:T(8,128)} custom-call(s32[3]{0:T(128)} %pad_add_fusion.me_ref, f32[2,5120,128]{2,1,0:T(8,128)} %pad_maximum_fusion.1.refs_0_, f32[512,256]{1,0:T(8,128)} %copy-done.39, f32[512,256]{1,0:T(8,128)} %copy-done.40, f32[8,512,1536]{2,1,0:T(8,128)} %row_step.3.refs_3_, ...), custom_call_target="tpu_custom_call", output_to_operand_aliasing={{}: (14, {})} | custom-call | flops 104857600 | bytes 33554432 | tf_op jit(solution)/shard_map/column_step/pallas_call | solution.py:298
  (245 shorter events, 94.4 us)
Async XLA Ops:
  6.5 181.0 %all-gather.2.cloned.1.call-start = ((), (), s32[]{:S(2)}) async-start(), calls=%async_computation | async-start | bytes 4718592 | tf_op jit(solution)/shard_map/all_gather | solution.py:400
  41.5 48.8 %copy-start.44 = (s32[2,128]{1,0:T(2,128)S(1)}, s32[2,128]{1,0:T(2,128)}, u32[]{:S(2)}) copy-start(s32[2,128]{1,0:T(2,128)} %param.15) | copy-start | bytes 3076
  119.7 406.2 %all-reduce.5.cloned.1.call-start = ((), (), s32[]{:S(2)}) async-start(), calls=%async_computation.1 | async-start | bytes 4718592 | tf_op jit(solution)/shard_map/psum | solution.py:415
  126.1 119.1 %collective-permute-start = (f32[512,512]{1,0:T(8,128)}, f32[512,512]{1,0:T(8,128)S(1)}, u32[]{:S(2)}, u32[]{:S(2)}) collective-permute-start(f32[512,512]{1,0:T(8,128)} %get-tuple-element.174), channel_id=1, source_target_pairs={{0,1},{1,0},{2,3},{3,2},{4,5},{5,4},{6,7},{7,6},{8,9},{9,8},{10,11... | collective-permute-start | bytes 3145736 | tf_op jit(solution)/shard_map/ppermute | solution.py:395
  126.8 119.7 %collective-permute-start.1 = (f32[512,512]{1,0:T(8,128)}, f32[512,512]{1,0:T(8,128)S(1)}, u32[]{:S(2)}, u32[]{:S(2)}) collective-permute-start(f32[512,512]{1,0:T(8,128)} %get-tuple-element.180), channel_id=1, source_target_pairs={{0,2},{1,3},{2,0},{3,1},{4,6},{5,7},{6,4},{7,5},{8,10},{9,11},{10,... | collective-permute-start | bytes 3145736 | tf_op jit(solution)/shard_map/ppermute | solution.py:395
  188.9 14.1 %collective-permute-start.15 = (f32[512,256]{1,0:T(8,128)S(1)}, f32[512,256]{1,0:T(8,128)S(1)}, u32[]{:S(2)}, u32[]{:S(2)}) collective-permute-start(f32[512,256]{1,0:T(8,128)S(1)} %get-tuple-element.183), channel_id=1, source_target_pairs={{0,8},{8,16},{16,24},{1,9},{9,17},{17,25},{2,10},{10,18},{18,26},{... | collective-permute-start | bytes 1572872 | tf_op jit(solution)/shard_map/ppermute | solution.py:401
  192.0 24.1 %collective-permute-start.16 = (f32[512,256]{1,0:T(8,128)S(1)}, f32[512,256]{1,0:T(8,128)S(1)}, u32[]{:S(2)}, u32[]{:S(2)}) collective-permute-start(f32[512,256]{1,0:T(8,128)S(1)} %get-tuple-element.184), channel_id=1, source_target_pairs={{8,0},{16,8},{24,16},{9,1},{17,9},{25,17},{10,2},{18,10},{26,18},{... | collective-permute-start | bytes 1572872 | tf_op jit(solution)/shard_map/ppermute | solution.py:402
  241.4 44.1 %collective-permute-start.2 = (f32[512,512]{1,0:T(8,128)}, f32[512,512]{1,0:T(8,128)S(1)}, u32[]{:S(2)}, u32[]{:S(2)}) collective-permute-start(f32[512,512]{1,0:T(8,128)} %get-tuple-element.179), channel_id=1, source_target_pairs={{0,3},{1,2},{2,1},{3,0},{4,7},{5,6},{6,5},{7,4},{8,11},{9,10},{10,... | collective-permute-start | bytes 3145736 | tf_op jit(solution)/shard_map/ppermute | solution.py:395
  241.5 116.7 %collective-permute-start.3 = (f32[512,512]{1,0:T(8,128)}, f32[512,512]{1,0:T(8,128)}, u32[]{:S(2)}, u32[]{:S(2)}) collective-permute-start(f32[512,512]{1,0:T(8,128)} %get-tuple-element.178), channel_id=1, source_target_pairs={{0,4},{1,5},{2,6},{3,7},{4,0},{5,1},{6,2},{7,3},{8,12},{9,13},{10,... | collective-permute-start | bytes 3145736 | tf_op jit(solution)/shard_map/ppermute | solution.py:395
  245.0 158.2 %collective-permute-start.4 = (f32[512,512]{1,0:T(8,128)}, f32[512,512]{1,0:T(8,128)}, u32[]{:S(2)}, u32[]{:S(2)}) collective-permute-start(f32[512,512]{1,0:T(8,128)} %get-tuple-element.177), channel_id=1, source_target_pairs={{0,5},{1,4},{2,7},{3,6},{4,1},{5,0},{6,3},{7,2},{8,13},{9,12},{10,... | collective-permute-start | bytes 3145736 | tf_op jit(solution)/shard_map/ppermute | solution.py:395
  245.2 276.7 %copy-start.1 = (f32[512,512]{1,0:T(8,128)}, f32[512,512]{1,0:T(8,128)S(1)}, u32[]{:S(2)}) copy-start(f32[512,512]{1,0:T(8,128)S(1)} %collective-permute-done.refs_4_) | copy-start | bytes 3145732
  245.2 248.4 %collective-permute-start.5 = (f32[512,512]{1,0:T(8,128)}, f32[512,512]{1,0:T(8,128)}, u32[]{:S(2)}, u32[]{:S(2)}) collective-permute-start(f32[512,512]{1,0:T(8,128)} %get-tuple-element.176), channel_id=1, source_target_pairs={{0,6},{1,7},{2,4},{3,5},{4,2},{5,3},{6,0},{7,1},{8,14},{9,15},{10,... | collective-permute-start | bytes 3145736 | tf_op jit(solution)/shard_map/ppermute | solution.py:395
  246.5 275.4 %copy-start.2 = (f32[512,512]{1,0:T(8,128)}, f32[512,512]{1,0:T(8,128)S(1)}, u32[]{:S(2)}) copy-start(f32[512,512]{1,0:T(8,128)S(1)} %collective-permute-done.1.refs_5_) | copy-start | bytes 3145732
  246.5 269.5 %collective-permute-start.6 = (f32[512,512]{1,0:T(8,128)}, f32[512,512]{1,0:T(8,128)}, u32[]{:S(2)}, u32[]{:S(2)}) collective-permute-start(f32[512,512]{1,0:T(8,128)} %get-tuple-element.175), channel_id=1, source_target_pairs={{0,7},{1,6},{2,5},{3,4},{4,3},{5,2},{6,1},{7,0},{8,15},{9,14},{10,... | collective-permute-start | bytes 3145736 | tf_op jit(solution)/shard_map/ppermute | solution.py:395
  285.5 236.3 %copy-start.3 = (f32[512,512]{1,0:T(8,128)}, f32[512,512]{1,0:T(8,128)S(1)}, u32[]{:S(2)}) copy-start(f32[512,512]{1,0:T(8,128)S(1)} %collective-permute-done.2.refs_6_) | copy-start | bytes 3145732
  285.5 304.8 %collective-permute-start.10 = (f32[512,512]{1,0:T(8,128)}, f32[512,512]{1,0:T(8,128)}, u32[]{:S(2)}, u32[]{:S(2)}) collective-permute-start(f32[512,512]{1,0:T(8,128)} %get-tuple-element.170), channel_id=1, source_target_pairs={{0,3},{1,2},{2,1},{3,0},{4,7},{5,6},{6,5},{7,4},{8,11},{9,10},{10,... | collective-permute-start | bytes 3145736 | tf_op jit(solution)/shard_map/ppermute | solution.py:395
  358.2 239.2 %collective-permute-start.11 = (f32[512,512]{1,0:T(8,128)}, f32[512,512]{1,0:T(8,128)}, u32[]{:S(2)}, u32[]{:S(2)}) collective-permute-start(f32[512,512]{1,0:T(8,128)} %get-tuple-element.169), channel_id=1, source_target_pairs={{0,4},{1,5},{2,6},{3,7},{4,0},{5,1},{6,2},{7,3},{8,12},{9,13},{10,... | collective-permute-start | bytes 3145736 | tf_op jit(solution)/shard_map/ppermute | solution.py:395
  403.1 196.2 %collective-permute-start.12 = (f32[512,512]{1,0:T(8,128)}, f32[512,512]{1,0:T(8,128)}, u32[]{:S(2)}, u32[]{:S(2)}) collective-permute-start(f32[512,512]{1,0:T(8,128)} %get-tuple-element.168), channel_id=1, source_target_pairs={{0,5},{1,4},{2,7},{3,6},{4,1},{5,0},{6,3},{7,2},{8,13},{9,12},{10,... | collective-permute-start | bytes 3145736 | tf_op jit(solution)/shard_map/ppermute | solution.py:395
  493.6 107.4 %collective-permute-start.13 = (f32[512,512]{1,0:T(8,128)}, f32[512,512]{1,0:T(8,128)}, u32[]{:S(2)}, u32[]{:S(2)}) collective-permute-start(f32[512,512]{1,0:T(8,128)} %get-tuple-element.167), channel_id=1, source_target_pairs={{0,6},{1,7},{2,4},{3,5},{4,2},{5,3},{6,0},{7,1},{8,14},{9,15},{10,... | collective-permute-start | bytes 3145736 | tf_op jit(solution)/shard_map/ppermute | solution.py:395
  516.0 89.9 %collective-permute-start.14 = (f32[512,512]{1,0:T(8,128)}, f32[512,512]{1,0:T(8,128)}, u32[]{:S(2)}, u32[]{:S(2)}) collective-permute-start(f32[512,512]{1,0:T(8,128)} %get-tuple-element.166), channel_id=1, source_target_pairs={{0,7},{1,6},{2,5},{3,4},{4,3},{5,2},{6,1},{7,0},{8,15},{9,14},{10,... | collective-permute-start | bytes 3145736 | tf_op jit(solution)/shard_map/ppermute | solution.py:395
  590.3 15.6 %collective-permute-start.8 = (f32[512,512]{1,0:T(8,128)}, f32[512,512]{1,0:T(8,128)S(1)}, u32[]{:S(2)}, u32[]{:S(2)}) collective-permute-start(f32[512,512]{1,0:T(8,128)} %get-tuple-element.172), channel_id=1, source_target_pairs={{0,1},{1,0},{2,3},{3,2},{4,5},{5,4},{6,7},{7,6},{8,9},{9,8},{10,11... | collective-permute-start | bytes 3145736 | tf_op jit(solution)/shard_map/ppermute | solution.py:395
  597.4 24.3 %collective-permute-start.9 = (f32[512,512]{1,0:T(8,128)S(1)}, f32[512,512]{1,0:T(8,128)S(1)}, u32[]{:S(2)}, u32[]{:S(2)}) collective-permute-start(f32[512,512]{1,0:T(8,128)S(1)} %copy-done.35), channel_id=1, source_target_pairs={{0,2},{1,3},{2,0},{3,1},{4,6},{5,7},{6,4},{7,5},{8,10},{9,11},{10,... | collective-permute-start | bytes 3145736 | tf_op jit(solution)/shard_map/ppermute | solution.py:395
  599.4 24.4 %collective-permute-start.18 = (f32[512,512]{1,0:T(8,128)S(1)}, f32[512,512]{1,0:T(8,128)S(1)}, u32[]{:S(2)}, u32[]{:S(2)}) collective-permute-start(f32[512,512]{1,0:T(8,128)S(1)} %copy-done.34), channel_id=1, source_target_pairs={{0,1},{1,0},{2,3},{3,2},{4,5},{5,4},{6,7},{7,6},{8,9},{9,8},{10,11... | collective-permute-start | bytes 3145736 | tf_op jit(solution)/shard_map/ppermute | solution.py:395
  601.0 84.4 %collective-permute-start.19 = (f32[512,512]{1,0:T(8,128)S(1)}, f32[512,512]{1,0:T(8,128)S(1)}, u32[]{:S(2)}, u32[]{:S(2)}) collective-permute-start(f32[512,512]{1,0:T(8,128)S(1)} %copy-done.33), channel_id=1, source_target_pairs={{0,2},{1,3},{2,0},{3,1},{4,6},{5,7},{6,4},{7,5},{8,10},{9,11},{10,... | collective-permute-start | bytes 3145736 | tf_op jit(solution)/shard_map/ppermute | solution.py:395
  605.9 101.9 %collective-permute-start.20 = (f32[512,512]{1,0:T(8,128)S(1)}, f32[512,512]{1,0:T(8,128)S(1)}, u32[]{:S(2)}, u32[]{:S(2)}) collective-permute-start(f32[512,512]{1,0:T(8,128)S(1)} %copy-done.32), channel_id=1, source_target_pairs={{0,3},{1,2},{2,1},{3,0},{4,7},{5,6},{6,5},{7,4},{8,11},{9,10},{10,... | collective-permute-start | bytes 3145736 | tf_op jit(solution)/shard_map/ppermute | solution.py:395
  606.0 105.5 %copy-start.8 = (f32[512,512]{1,0:T(8,128)}, f32[512,512]{1,0:T(8,128)S(1)}, u32[]{:S(2)}) copy-start(f32[512,512]{1,0:T(8,128)S(1)} %collective-permute-done.8.refs_4_) | copy-start | bytes 3145732
  606.0 104.2 %collective-permute-start.7 = (f32[512,512]{1,0:T(8,128)S(1)}, f32[512,512]{1,0:T(8,128)S(1)}, u32[]{:S(2)}, u32[]{:S(2)}) collective-permute-start(f32[512,512]{1,0:T(8,128)S(1)} %copy-done.37), channel_id=1, source_target_pairs={{0,8},{8,16},{16,24},{1,9},{9,17},{17,25},{2,10},{10,18},{18,26},{... | collective-permute-start | bytes 3145736 | tf_op jit(solution)/shard_map/ppermute | solution.py:426
  621.7 89.7 %copy-start.9 = (f32[512,512]{1,0:T(8,128)}, f32[512,512]{1,0:T(8,128)S(1)}, u32[]{:S(2)}) copy-start(f32[512,512]{1,0:T(8,128)S(1)} %collective-permute-done.9.refs_5_) | copy-start | bytes 3145732
  621.7 93.6 %collective-permute-start.21 = (f32[512,512]{1,0:T(8,128)S(1)}, f32[512,512]{1,0:T(8,128)S(1)}, u32[]{:S(2)}, u32[]{:S(2)}) collective-permute-start(f32[512,512]{1,0:T(8,128)S(1)} %copy-done.31), channel_id=1, source_target_pairs={{0,4},{1,5},{2,6},{3,7},{4,0},{5,1},{6,2},{7,3},{8,12},{9,13},{10,... | collective-permute-start | bytes 3145736 | tf_op jit(solution)/shard_map/ppermute | solution.py:395
  623.7 190.2 %copy-start.4 = (f32[512,512]{1,0:T(8,128)}, f32[512,512]{1,0:T(8,128)S(1)}, u32[]{:S(2)}) copy-start(f32[512,512]{1,0:T(8,128)S(1)} %collective-permute-done.18.refs_4_) | copy-start | bytes 3145732
  623.7 86.4 %copy-start.36 = (f32[512,512]{1,0:T(8,128)S(1)}, f32[512,512]{1,0:T(8,128)}, u32[]{:S(2)}) copy-start(f32[512,512]{1,0:T(8,128)} %select_select_fusion.2) | copy-start | bytes 3145732
  623.7 104.5 %collective-permute-start.22 = (f32[512,512]{1,0:T(8,128)S(1)}, f32[512,512]{1,0:T(8,128)S(1)}, u32[]{:S(2)}, u32[]{:S(2)}) collective-permute-start(f32[512,512]{1,0:T(8,128)S(1)} %copy-done.30), channel_id=1, source_target_pairs={{0,5},{1,4},{2,7},{3,6},{4,1},{5,0},{6,3},{7,2},{8,13},{9,12},{10,... | collective-permute-start | bytes 3145736 | tf_op jit(solution)/shard_map/ppermute | solution.py:395
  685.4 128.5 %copy-start.5 = (f32[512,512]{1,0:T(8,128)}, f32[512,512]{1,0:T(8,128)S(1)}, u32[]{:S(2)}) copy-start(f32[512,512]{1,0:T(8,128)S(1)} %collective-permute-done.19.refs_5_) | copy-start | bytes 3145732
  685.4 119.9 %collective-permute-start.23 = (f32[512,512]{1,0:T(8,128)}, f32[512,512]{1,0:T(8,128)}, u32[]{:S(2)}, u32[]{:S(2)}) collective-permute-start(f32[512,512]{1,0:T(8,128)} %get-tuple-element.159), channel_id=1, source_target_pairs={{0,6},{1,7},{2,4},{3,5},{4,2},{5,3},{6,0},{7,1},{8,14},{9,15},{10,... | collective-permute-start | bytes 3145736 | tf_op jit(solution)/shard_map/ppermute | solution.py:395
  707.9 97.5 %collective-permute-start.24 = (f32[512,512]{1,0:T(8,128)}, f32[512,512]{1,0:T(8,128)}, u32[]{:S(2)}, u32[]{:S(2)}) collective-permute-start(f32[512,512]{1,0:T(8,128)} %get-tuple-element.158), channel_id=1, source_target_pairs={{0,7},{1,6},{2,5},{3,4},{4,3},{5,2},{6,1},{7,0},{8,15},{9,14},{10,... | collective-permute-start | bytes 3145736 | tf_op jit(solution)/shard_map/ppermute | solution.py:395
  710.1 48.2 %collective-permute-start.25 = (f32[512,512]{1,0:T(8,128)S(1)}, f32[512,512]{1,0:T(8,128)S(1)}, u32[]{:S(2)}, u32[]{:S(2)}) collective-permute-start(f32[512,512]{1,0:T(8,128)S(1)} %copy-done.36), channel_id=1, source_target_pairs={{8,0},{16,8},{24,16},{9,1},{17,9},{25,17},{10,2},{18,10},{26,18},{... | collective-permute-start | bytes 3145736 | tf_op jit(solution)/shard_map/ppermute | solution.py:426
  716.3 97.3 %collective-permute-start.17 = (f32[512,512]{1,0:T(8,128)}, f32[512,512]{1,0:T(8,128)}, u32[]{:S(2)}, u32[]{:S(2)}) collective-permute-start(f32[512,512]{1,0:T(8,128)} %select_select_fusion.4), channel_id=1, source_target_pairs={{0,8},{8,16},{16,24},{1,9},{9,17},{17,25},{2,10},{10,18},{18,26},{... | collective-permute-start | bytes 3145736 | tf_op jit(solution)/shard_map/ppermute | solution.py:426
  728.2 77.4 %collective-permute-start.27 = (f32[512,256]{1,0:T(8,128)}, f32[512,256]{1,0:T(8,128)S(1)}, u32[]{:S(2)}, u32[]{:S(2)}) collective-permute-start(f32[512,256]{1,0:T(8,128)} %get-tuple-element.156), channel_id=1, source_target_pairs={{0,1},{1,0},{2,3},{3,2},{4,5},{5,4},{6,7},{7,6},{8,9},{9,8},{10,11... | collective-permute-start | bytes 1572872 | tf_op jit(solution)/shard_map/ppermute | solution.py:395
  759.4 51.3 %collective-permute-start.28 = (f32[512,256]{1,0:T(8,128)}, f32[512,256]{1,0:T(8,128)}, u32[]{:S(2)}, u32[]{:S(2)}) collective-permute-start(f32[512,256]{1,0:T(8,128)} %get-tuple-element.155), channel_id=1, source_target_pairs={{0,2},{1,3},{2,0},{3,1},{4,6},{5,7},{6,4},{7,5},{8,10},{9,11},{10,... | collective-permute-start | bytes 1572872 | tf_op jit(solution)/shard_map/ppermute | solution.py:395
  805.3 20.4 %collective-permute-start.29 = (f32[512,256]{1,0:T(8,128)}, f32[512,256]{1,0:T(8,128)}, u32[]{:S(2)}, u32[]{:S(2)}) collective-permute-start(f32[512,256]{1,0:T(8,128)} %get-tuple-element.154), channel_id=1, source_target_pairs={{0,3},{1,2},{2,1},{3,0},{4,7},{5,6},{6,5},{7,4},{8,11},{9,10},{10,... | collective-permute-start | bytes 1572872 | tf_op jit(solution)/shard_map/ppermute | solution.py:395
  805.4 24.4 %collective-permute-start.30 = (f32[512,256]{1,0:T(8,128)}, f32[512,256]{1,0:T(8,128)}, u32[]{:S(2)}, u32[]{:S(2)}) collective-permute-start(f32[512,256]{1,0:T(8,128)} %get-tuple-element.153), channel_id=1, source_target_pairs={{0,4},{1,5},{2,6},{3,7},{4,0},{5,1},{6,2},{7,3},{8,12},{9,13},{10,... | collective-permute-start | bytes 1572872 | tf_op jit(solution)/shard_map/ppermute | solution.py:395
  805.6 134.9 %copy-start.17 = (f32[512,256]{1,0:T(8,128)}, f32[512,256]{1,0:T(8,128)S(1)}, u32[]{:S(2)}) copy-start(f32[512,256]{1,0:T(8,128)S(1)} %collective-permute-done.27.refs_4_) | copy-start | bytes 1572868
  805.6 83.9 %collective-permute-start.34 = (f32[512,512]{1,0:T(8,128)}, f32[512,512]{1,0:T(8,128)S(1)}, u32[]{:S(2)}, u32[]{:S(2)}) collective-permute-start(f32[512,512]{1,0:T(8,128)} %select_select_fusion.3), channel_id=1, source_target_pairs={{8,0},{16,8},{24,16},{9,1},{17,9},{25,17},{10,2},{18,10},{26,18},{... | collective-permute-start | bytes 3145736 | tf_op jit(solution)/shard_map/ppermute | solution.py:426
  810.7 50.7 %collective-permute-start.31 = (f32[512,256]{1,0:T(8,128)S(1)}, f32[512,256]{1,0:T(8,128)}, u32[]{:S(2)}, u32[]{:S(2)}) collective-permute-start(f32[512,256]{1,0:T(8,128)S(1)} %copy-done.42), channel_id=1, source_target_pairs={{0,5},{1,4},{2,7},{3,6},{4,1},{5,0},{6,3},{7,2},{8,13},{9,12},{10,... | collective-permute-start | bytes 1572872 | tf_op jit(solution)/shard_map/ppermute | solution.py:395
  813.7 73.2 %collective-permute-start.32 = (f32[512,256]{1,0:T(8,128)S(1)}, f32[512,256]{1,0:T(8,128)}, u32[]{:S(2)}, u32[]{:S(2)}) collective-permute-start(f32[512,256]{1,0:T(8,128)S(1)} %copy-done.41), channel_id=1, source_target_pairs={{0,6},{1,7},{2,4},{3,5},{4,2},{5,3},{6,0},{7,1},{8,14},{9,15},{10,... | collective-permute-start | bytes 1572872 | tf_op jit(solution)/shard_map/ppermute | solution.py:395
  825.8 110.6 %collective-permute-start.26 = (f32[512,512]{1,0:T(8,128)}, f32[512,512]{1,0:T(8,128)}, u32[]{:S(2)}, u32[]{:S(2)}) collective-permute-start(f32[512,512]{1,0:T(8,128)} %select_select_fusion.1), channel_id=1, source_target_pairs={{0,8},{8,16},{16,24},{1,9},{9,17},{17,25},{2,10},{10,18},{18,26},{... | collective-permute-start | bytes 3145736 | tf_op jit(solution)/shard_map/ppermute | solution.py:426
  829.8 106.6 %collective-permute-start.43 = (f32[512,512]{1,0:T(8,128)}, f32[512,512]{1,0:T(8,128)}, u32[]{:S(2)}, u32[]{:S(2)}) collective-permute-start(f32[512,512]{1,0:T(8,128)} %select_select_fusion), channel_id=1, source_target_pairs={{8,0},{16,8},{24,16},{9,1},{17,9},{25,17},{10,2},{18,10},{26,18},{... | collective-permute-start | bytes 3145736 | tf_op jit(solution)/shard_map/ppermute | solution.py:426
  861.5 70.4 %collective-permute-start.33 = (f32[512,256]{1,0:T(8,128)}, f32[512,256]{1,0:T(8,128)S(1)}, u32[]{:S(2)}, u32[]{:S(2)}) collective-permute-start(f32[512,256]{1,0:T(8,128)} %get-tuple-element.150), channel_id=1, source_target_pairs={{0,7},{1,6},{2,5},{3,4},{4,3},{5,2},{6,1},{7,0},{8,15},{9,14},{10,... | collective-permute-start | bytes 1572872 | tf_op jit(solution)/shard_map/ppermute | solution.py:395
  886.9 46.7 %collective-permute-start.36 = (f32[512,256]{1,0:T(8,128)}, f32[512,256]{1,0:T(8,128)S(1)}, u32[]{:S(2)}, u32[]{:S(2)}) collective-permute-start(f32[512,256]{1,0:T(8,128)} %get-tuple-element.148), channel_id=1, source_target_pairs={{0,1},{1,0},{2,3},{3,2},{4,5},{5,4},{6,7},{7,6},{8,9},{9,8},{10,11... | collective-permute-start | bytes 1572872 | tf_op jit(solution)/shard_map/ppermute | solution.py:395
  890.5 43.1 %collective-permute-start.37 = (f32[512,256]{1,0:T(8,128)}, f32[512,256]{1,0:T(8,128)S(1)}, u32[]{:S(2)}, u32[]{:S(2)}) collective-permute-start(f32[512,256]{1,0:T(8,128)} %get-tuple-element.147), channel_id=1, source_target_pairs={{0,2},{1,3},{2,0},{3,1},{4,6},{5,7},{6,4},{7,5},{8,10},{9,11},{10,... | collective-permute-start | bytes 1572872 | tf_op jit(solution)/shard_map/ppermute | solution.py:395
  931.9 52.5 %collective-permute-start.38 = (f32[512,256]{1,0:T(8,128)}, f32[512,256]{1,0:T(8,128)S(1)}, u32[]{:S(2)}, u32[]{:S(2)}) collective-permute-start(f32[512,256]{1,0:T(8,128)} %get-tuple-element.146), channel_id=1, source_target_pairs={{0,3},{1,2},{2,1},{3,0},{4,7},{5,6},{6,5},{7,4},{8,11},{9,10},{10,... | collective-permute-start | bytes 1572872 | tf_op jit(solution)/shard_map/ppermute | solution.py:395
  933.6 98.8 %copy-start.18 = (f32[512,256]{1,0:T(8,128)}, f32[512,256]{1,0:T(8,128)S(1)}, u32[]{:S(2)}) copy-start(f32[512,256]{1,0:T(8,128)S(1)} %collective-permute-done.36.refs_4_) | copy-start | bytes 1572868
  933.6 50.8 %collective-permute-start.39 = (f32[512,256]{1,0:T(8,128)}, f32[512,256]{1,0:T(8,128)S(1)}, u32[]{:S(2)}, u32[]{:S(2)}) collective-permute-start(f32[512,256]{1,0:T(8,128)} %get-tuple-element.145), channel_id=1, source_target_pairs={{0,4},{1,5},{2,6},{3,7},{4,0},{5,1},{6,2},{7,3},{8,12},{9,13},{10,... | collective-permute-start | bytes 1572872 | tf_op jit(solution)/shard_map/ppermute | solution.py:395
  933.6 98.8 %copy-start.19 = (f32[512,256]{1,0:T(8,128)}, f32[512,256]{1,0:T(8,128)S(1)}, u32[]{:S(2)}) copy-start(f32[512,256]{1,0:T(8,128)S(1)} %collective-permute-done.37.refs_5_) | copy-start | bytes 1572868
  933.6 67.9 %collective-permute-start.40 = (f32[512,256]{1,0:T(8,128)}, f32[512,256]{1,0:T(8,128)S(1)}, u32[]{:S(2)}, u32[]{:S(2)}) collective-permute-start(f32[512,256]{1,0:T(8,128)} %get-tuple-element.144), channel_id=1, source_target_pairs={{0,5},{1,4},{2,7},{3,6},{4,1},{5,0},{6,3},{7,2},{8,13},{9,12},{10,... | collective-permute-start | bytes 1572872 | tf_op jit(solution)/shard_map/ppermute | solution.py:395
  936.4 77.8 %collective-permute-start.41 = (f32[512,256]{1,0:T(8,128)}, f32[512,256]{1,0:T(8,128)}, u32[]{:S(2)}, u32[]{:S(2)}) collective-permute-start(f32[512,256]{1,0:T(8,128)} %get-tuple-element.143), channel_id=1, source_target_pairs={{0,6},{1,7},{2,4},{3,5},{4,2},{5,3},{6,0},{7,1},{8,14},{9,15},{10,... | collective-permute-start | bytes 1572872 | tf_op jit(solution)/shard_map/ppermute | solution.py:395
  936.4 89.5 %collective-permute-start.42 = (f32[512,256]{1,0:T(8,128)}, f32[512,256]{1,0:T(8,128)}, u32[]{:S(2)}, u32[]{:S(2)}) collective-permute-start(f32[512,256]{1,0:T(8,128)} %get-tuple-element.142), channel_id=1, source_target_pairs={{0,7},{1,6},{2,5},{3,4},{4,3},{5,2},{6,1},{7,0},{8,15},{9,14},{10,... | collective-permute-start | bytes 1572872 | tf_op jit(solution)/shard_map/ppermute | solution.py:395
  942.9 87.4 %copy-start.24 = (f32[512,256]{1,0:T(8,128)S(1)}, f32[512,256]{1,0:T(8,128)}, u32[]{:S(2)}) copy-start(f32[512,256]{1,0:T(8,128)} %get-tuple-element.127) | copy-start | bytes 1572868
  984.4 50.2 %copy-start.21 = (f32[512,256]{1,0:T(8,128)}, f32[512,256]{1,0:T(8,128)S(1)}, u32[]{:S(2)}) copy-start(f32[512,256]{1,0:T(8,128)S(1)} %collective-permute-done.38.refs_6_) | copy-start | bytes 1572868
  984.4 50.1 %copy-start.22 = (f32[512,256]{1,0:T(8,128)}, f32[512,256]{1,0:T(8,128)S(1)}, u32[]{:S(2)}) copy-start(f32[512,256]{1,0:T(8,128)S(1)} %collective-permute-done.39.refs_7_) | copy-start | bytes 1572868
  1025.9 14.7 %collective-permute-start.35 = (f32[512,256]{1,0:T(8,128)}, f32[512,256]{1,0:T(8,128)S(1)}, u32[]{:S(2)}, u32[]{:S(2)}) collective-permute-start(f32[512,256]{1,0:T(8,128)} %select_select_fusion.9), channel_id=1, source_target_pairs={{0,8},{8,16},{16,24},{1,9},{9,17},{17,25},{2,10},{10,18},{18,26},{... | collective-permute-start | bytes 1572872 | tf_op jit(solution)/shard_map/ppermute | solution.py:426
  1029.0 23.9 %collective-permute-start.46 = (f32[512,256]{1,0:T(8,128)}, f32[512,256]{1,0:T(8,128)}, u32[]{:S(2)}, u32[]{:S(2)}) collective-permute-start(f32[512,256]{1,0:T(8,128)} %select_select_fusion.8), channel_id=1, source_target_pairs={{8,0},{16,8},{24,16},{9,1},{17,9},{25,17},{10,2},{18,10},{26,18},{... | collective-permute-start | bytes 1572872 | tf_op jit(solution)/shard_map/ppermute | solution.py:426
  1040.6 36.6 %collective-permute-start.44 = (f32[512,256]{1,0:T(8,128)}, f32[512,256]{1,0:T(8,128)S(1)}, u32[]{:S(2)}, u32[]{:S(2)}) collective-permute-start(f32[512,256]{1,0:T(8,128)} %select_select_fusion.7), channel_id=1, source_target_pairs={{0,8},{8,16},{16,24},{1,9},{9,17},{17,25},{2,10},{10,18},{18,26},{... | collective-permute-start | bytes 1572872 | tf_op jit(solution)/shard_map/ppermute | solution.py:426
  1044.7 32.5 %collective-permute-start.45 = (f32[512,256]{1,0:T(8,128)}, f32[512,256]{1,0:T(8,128)S(1)}, u32[]{:S(2)}, u32[]{:S(2)}) collective-permute-start(f32[512,256]{1,0:T(8,128)} %select_select_fusion.6), channel_id=1, source_target_pairs={{8,0},{16,8},{24,16},{9,1},{17,9},{25,17},{10,2},{18,10},{26,18},{... | collective-permute-start | bytes 1572872 | tf_op jit(solution)/shard_map/ppermute | solution.py:426
  (33 other events, 377.0 us)
Sparse Core Ops, SparseCore 0:
  119.8 67.7 all-gather.1
  241.5 73.3 all-reduce.4
